TPU v7x, 512 devices: a whole 4x8x8 slice. The times are simulated.
512 devices in a mesh: seq: 64 (over y, z), trk: 8 (over x, core).
Axes of the slice: x: 4, y: 8, z: 8, core: 2. Of those that a mesh axis runs over, the one named last changes fastest.
Arguments:
- embeddings: bfloat16 [4, 8192, 1920], P(None, 'seq', 'trk'), may hold values from -16 to 16
- head: bfloat16 [1920, 4096], P(None, 'trk'), may hold values from -0.125 to 0.125
- exon_starts: int32 [4, 128, 8], replicated, may hold values from 0 to 8184, as said below
- exon_lengths: int32 [4, 128, 8], replicated, may hold values from 1 to 8, as said below
- gene_owner: int32 [4, 128], replicated, may hold values from 0 to 63, as said below
- gene_targets: float32 [4, 256, 4096], P(None, 'seq', 'trk'), may hold values from 2 to 400, as said below
Outputs:
- gene_pred: float32 [4, 256, 4096], P(None, 'seq', 'trk')
- loss: float32 [4, 4096], P(None, 'trk')
- grad_head: float32 [1920, 4096], P('seq', 'trk')
Inputs may be any that keep to these rules, and one draw needn't show every extreme that they name: `exon_starts`: each gene has 8 exon blocks; blocks may intersect. Some block of each window starts at 0 and some at 8184. `exon_lengths`: some block of each window has length 8. `gene_owner`: in each window no owner holds more than 4 genes, and some owner holds exactly 4. `gene_targets`: entries of empty slots are read by nothing.
All inputs are finite; a program needn't handle non-finite values.
Results may differ from a plain program's by a relative error of at most 0.0041.
Values may be sent and summed in bfloat16 or wider, within the bound.
No kernel may reach another device: no remote copies, remote signals or barrier semaphores. Data moves between devices by JAX's collectives and lax.ppermute only.
A program may use at most 64 MiB of HBM per device.

v0:
```python
import jax
import jax.numpy as jnp
from jax import lax
from jax.sharding import PartitionSpec as P


def slot_table(gene_owner, capacity):
    genes = gene_owner.shape[1]
    same = gene_owner[:, :, None] == gene_owner[:, None, :]
    earlier = jnp.arange(genes)[None, :] < jnp.arange(genes)[:, None]
    ahead = jnp.sum((same & earlier[None]).astype(jnp.int32), axis=2)
    return gene_owner * capacity + ahead


def coverage(starts, lengths, positions):
    where_bin = positions[None, None, None, :]
    inside = (where_bin >= starts[..., None]) & (where_bin < (starts + lengths)[..., None])
    return jnp.sum(inside.astype(jnp.float32), axis=2)


def fold_sources(received):
    return jnp.sum(received, axis=1)


def per_device(embeddings, head, exon_starts, exon_lengths, gene_owner, gene_targets):
    seq_devices = lax.axis_size("seq")
    seq_place = lax.axis_index("seq")
    windows, bin_dev, _ = embeddings.shape
    genes = gene_owner.shape[1]
    capacity = gene_targets.shape[1]
    slot_total = seq_devices * capacity
    whole = lax.all_gather(embeddings, "trk", axis=2, tiled=True)
    logits = jnp.einsum("wbd,dt->wbt", whole, head, preferred_element_type=jnp.float32)
    pred = jax.nn.softplus(logits).astype(jnp.bfloat16)
    positions = seq_place * bin_dev + jnp.arange(bin_dev, dtype=jnp.int32)
    cover = coverage(exon_starts, exon_lengths, positions)
    slot_of = slot_table(gene_owner, capacity)
    onehot = (slot_of[..., None] == jnp.arange(slot_total, dtype=jnp.int32)).astype(jnp.float32)
    member = jnp.einsum("wgs,wgb->wsb", onehot, cover, precision=lax.Precision.HIGHEST).astype(
        jnp.bfloat16
    )
    valid = jnp.sum(onehot, axis=1)
    valid_here = lax.dynamic_slice_in_dim(valid, seq_place * capacity, capacity, 1)
    targets_here = gene_targets * valid_here[..., None]
    target_part = jnp.sum(targets_here, axis=1)
    partial_value = jnp.einsum("wsb,wbt->wst", member, pred, preferred_element_type=jnp.float32)
    blocks = partial_value.reshape(windows, seq_devices, capacity, partial_value.shape[2])
    gene_here = fold_sources(lax.all_to_all(blocks, "seq", split_axis=1, concat_axis=1, tiled=True))
    safe = jnp.where(valid_here[..., None] > 0, gene_here, 1.0)
    fit_part = jnp.sum(targets_here * jnp.log(safe), axis=1)
    total, target_sum, fit = lax.psum((jnp.sum(gene_here, axis=1), target_part, fit_part), "seq")
    scale_rows = (genes / target_sum)[:, None, :]
    gene_grad = (
        scale_rows
        * (
            valid_here[..., None] * (0.2 + 0.8 * target_sum / total)[:, None, :]
            - targets_here / safe
        )
    ).astype(jnp.bfloat16)
    bin_grad = jnp.einsum(
        "wsb,wst->wbt",
        member,
        lax.all_gather(gene_grad, "seq", axis=1, tiled=True),
        preferred_element_type=jnp.float32,
    )
    logit_grad = (bin_grad * jax.nn.sigmoid(logits)).astype(jnp.bfloat16)
    grad_head = lax.psum_scatter(
        jnp.einsum("wbd,wbt->dt", whole, logit_grad, preferred_element_type=jnp.float32),
        "seq",
        scatter_dimension=0,
        tiled=True,
    )
    log_total = jnp.log(total)
    loss = (-fit + target_sum * log_total + 0.2 * (total - target_sum * log_total)) / target_sum
    return (gene_here, loss, grad_head)


def solution(mesh):
    return jax.shard_map(
        per_device,
        mesh=mesh,
        in_specs=(P(None, "seq", "trk"), P(None, "trk"), P(), P(), P(), P(None, "seq", "trk")),
        out_specs=(P(None, "seq", "trk"), P(None, "trk"), P("seq", "trk")),
        check_vma=False,
    )
```

profile of v0, /device:TPU:2, one launch (start us, length us, event | category | flops | bytes accessed | tf_op | source)
XLA Modules:
  0.0 664.6 jit_solution(17121487797619391338)
XLA Ops:
  7.2 0.0 copy-start
  7.2 0.0 all-gather.3.cloned.1.call-start
  7.2 0.7 all-gather.3.cloned.1.call-update
  7.9 0.8 copy.28
  8.8 0.7 add.46
  9.5 0.1 copy.29
  9.7 1.0 convert_reduce_fusion.2
  10.7 0.7 multiply_add_fusion
  11.4 1.4 convert_reduce_fusion
  12.8 0.4 convolution_convert_fusion
  13.2 30.7 %all-gather.3.cloned.1.call-done = bf16[4,128,1920]{1,2,0:T(8,128)(2,1)} async-done(((bf16[4,128,240]{1,2,0:T(8,128)(2,1)}), bf16[4,128,1920]{1,2,0:T(8,128)(2,1)}) %all-gather.3.cloned.1.call-update) | async-done | bytes 1966096 | tf_op jit(solution)/shard_map/all_gather | solution.py:32
  43.9 0.0 copy-done
  43.9 2.8 fusion.13
  46.8 2.2 fusion.9
  48.9 2.9 reshape.35
  51.8 3.5 copy.30
  55.4 13.6 %all-to-all-start = ((f32[4,64,4,512]{3,2,0,1:T(4,128)}), f32[4,64,4,512]{3,2,0,1:T(4,128)}, u32[]{:S(2)}, u32[]{:S(2)}) async-start(f32[4,64,4,512]{3,2,0,1:T(4,128)} %copy.30), calls=%async_computation | async-start | bytes 4194304 | tf_op jit(solution)/shard_map/all_to_all | solution.py:48
  68.9 0.0 copy-start.2
  68.9 0.0 all-gather.5.cloned.1.call-start
  69.0 0.1 convert_reduce_fusion.1
  69.1 0.1 broadcast_compare_fusion
  69.2 51.5 %all-to-all-done = f32[4,64,4,512]{3,2,0,1:T(4,128)} async-done(((f32[4,64,4,512]{3,2,0,1:T(4,128)}), f32[4,64,4,512]{3,2,0,1:T(4,128)}, u32[]{:S(2)}, u32[]{:S(2)}) %all-to-all-start) | async-done | bytes 2097184 | tf_op jit(solution)/shard_map/all_to_all | solution.py:48
  120.7 2.1 fusion.20
  122.7 0.0 copy-start.1
  122.8 0.0 copy-done.2
  122.8 0.1 multiply_reduce_fusion
  122.9 282.3 %all-reduce.1 = (f32[4,512]{1,0:T(4,128)S(1)}, f32[4,512]{1,0:T(4,128)S(1)}, f32[4,512]{1,0:T(4,128)S(1)}) all-reduce(f32[4,512]{1,0:T(4,128)S(1)} %get-tuple-element.18, f32[4,512]{1,0:T(4,128)S(1)} %get-tuple-element.15, f32[4,512]{1,0:T(4,128)S(1)} %get-tuple-element.17), channel_id=1, replica_groups=mesh['seq'=64,'trk'=8] {'seq'}, use_global_device_ids=true, to_apply=%region_7.8 | all-reduce | flops 6144 | bytes 49152 | tf_op jit(solution)/shard_map/psum | solution.py:51
  405.2 0.6 fusion.16
  405.8 0.1 multiply_convert_fusion
  405.9 0.6 copy.31
  406.5 0.0 all-gather.5.cloned.1.call-update
  406.5 0.0 all-reduce.4.cloned.1.call-start
  406.6 76.9 %all-gather.5.cloned.1.call-done = bf16[4,256,512]{2,0,1:T(4,128)(2,1)} async-done(((bf16[4,4,512]{2,0,1:T(4,128)(2,1)}), bf16[4,256,512]{2,0,1:T(4,128)(2,1)}) %all-gather.5.cloned.1.call-update) | async-done | bytes 1048592 | tf_op jit(solution)/shard_map/all_gather | solution.py:63
  483.5 5.5 convolution_bitcast_fusion
  489.0 0.0 copy-done.1
  489.0 0.0 all-reduce.4.cloned.1.call-update
  489.0 1.3 dynamic-slice
  490.9 165.2 %all-reduce.4.cloned.1.call-done = f32[1920,512]{0,1:T(8,128)} async-done(((f32[1920,512]{0,1:T(8,128)}), f32[1920,512]{0,1:T(8,128)}) %all-reduce.4.cloned.1.call-update) | async-done | bytes 3932176
  656.1 1.2 constant_dynamic-slice_fusion
  657.3 0.8 copy.35
  (2 shorter events, 0.0 us)
Async XLA Ops:
  7.2 36.7 %copy-start = (bf16[1920,512]{1,0:T(8,128)(2,1)S(1)}, bf16[1920,512]{1,0:T(8,128)(2,1)}, u32[]{:S(2)}) copy-start(bf16[1920,512]{1,0:T(8,128)(2,1)} %param.7) | copy-start | bytes 5898244
  7.2 36.7 %all-gather.3.cloned.1.call-start = ((), (), s32[]{:S(2)}) async-start(), calls=%async_computation.1 | async-start | bytes 2211840 | tf_op jit(solution)/shard_map/all_gather | solution.py:32
  55.4 65.3 %all-to-all-start = ((f32[4,64,4,512]{3,2,0,1:T(4,128)}), f32[4,64,4,512]{3,2,0,1:T(4,128)}, u32[]{:S(2)}, u32[]{:S(2)}) async-start(f32[4,64,4,512]{3,2,0,1:T(4,128)} %copy.30), calls=%async_computation | async-start | bytes 4194304 | tf_op jit(solution)/shard_map/all_to_all | solution.py:48
  68.9 53.8 %copy-start.2 = (f32[4,4,512]{2,1,0:T(4,128)S(1)}, f32[4,4,512]{2,1,0:T(4,128)}, u32[]{:S(2)}) copy-start(f32[4,4,512]{2,1,0:T(4,128)} %param.11) | copy-start | bytes 98308
  68.9 414.6 %all-gather.5.cloned.1.call-start = ((), (), s32[]{:S(2)}) async-start(), calls=%async_computation.2 | async-start | bytes 1064960 | tf_op jit(solution)/shard_map/all_gather | solution.py:63
  122.7 366.2 %copy-start.1 = (f32[4,4,512]{2,1,0:T(4,128)}, f32[4,4,512]{2,1,0:T(4,128)S(1)}, u32[]{:S(2)}) copy-start(f32[4,4,512]{2,1,0:T(4,128)S(1)} %get-tuple-element.16) | copy-start | bytes 98308
  406.5 249.6 %all-reduce.4.cloned.1.call-start = ((), (), s32[]{:S(2)}) async-start(), calls=%async_computation.3 | async-start | bytes 7864320
Sparse Core Ops, SparseCore 0:
  10.1 33.7 all-gather.2
  406.7 76.7 all-gather.4
  489.1 166.9 all-reduce.3
where the time goes:
time: 665 us
  waiting for transfers between devices  325 us (49%)
  blocking collectives  282 us (42%)
  between operations  14.5 us (2%)
  starting transfers between devices  13.7 us (2%)
  local copies, waits for them, and re-layouts  11.2 us (2%)
  matrix products  10.9 us (2%)
  other arithmetic  7 us (1%)
    psum x1, blocking collectives, per_device(): lax.psum((jnp.sum(gene_here, axis=1), target_part, fit_part), 'seq')  282 us
    unnamed x4, waiting for transfers between devices  166 us
    all_gather x1, waiting for transfers between devices, per_device(): lax.all_gather(gene_grad, 'seq', axis=1, tiled=True)  76.9 us
    all_to_all x1, waiting for transfers between devices, per_device(): lax.all_to_all(blocks, 'seq', split_axis=1, concat_axis=1, tiled=True)  51.5 us
    all_gather x1, waiting for transfers between devices, per_device(): whole = lax.all_gather(embeddings, 'trk', axis=2, tiled=True)  30.7 us
    all_to_all x1, starting transfers between devices, per_device(): lax.all_to_all(blocks, 'seq', split_axis=1, concat_axis=1, tiled=True)  13.6 us
  transfers between devices with their start and end apart: 4, of which 4 were waited for; matrix products, arithmetic and copies ran while one was open for 1% of the time, Pallas kernels for 0%

commit v1 on v0

v1 whole, which is shorter than its diff:
```python
import jax
import jax.numpy as jnp
from jax import lax
from jax.sharding import Mesh, PartitionSpec as P

SEQ = ("y", "z")
F32 = jnp.float32
BF16 = jnp.bfloat16
MIDDLE = 28.28


def exchange(blocks, axes):
    return lax.all_to_all(blocks, axes, split_axis=0, concat_axis=0, tiled=True)


def gather(block, axes):
    size = lax.axis_size(axes)
    return exchange(jnp.broadcast_to(block[None], (size,) + block.shape), axes)


def halves(values):
    high = lax.reduce_precision(values, 8, 7)
    return high.astype(BF16), (values - high).astype(BF16)


def spread(counts):
    scaled = counts * (1.0 / MIDDLE)
    for _ in range(4):
        scaled = scaled * scaled
    return scaled


def unspread(coded):
    for _ in range(4):
        coded = jnp.sqrt(coded)
    return coded * MIDDLE


def squared(ratio):
    small = ratio < 2.0**63
    scaled = jnp.where(small, ratio, ratio * 2.0**-96)
    return jnp.where(small, scaled * scaled, -(scaled * scaled))


def rooted(coded):
    root = jnp.sqrt(jnp.abs(coded))
    return jnp.where(coded < 0, root * 2.0**96, root)


def slot_table(gene_owner, capacity):
    genes = gene_owner.shape[1]
    same = gene_owner[:, :, None] == gene_owner[:, None, :]
    earlier = jnp.arange(genes)[None, :] < jnp.arange(genes)[:, None]
    ahead = jnp.sum((same & earlier[None]).astype(jnp.int32), axis=2)
    return gene_owner * capacity + ahead


def by_place(table, places):
    windows, genes = table.shape[:2]
    held = genes // places
    split = table.reshape((windows, places, held) + table.shape[2:])
    return jnp.moveaxis(split, 1, 0).reshape((genes * windows,) + table.shape[2:])


def per_device(embeddings, head, exon_starts, exon_lengths, gene_owner, gene_targets):
    places = lax.axis_size(SEQ)
    place = lax.axis_index(SEQ)
    windows, bin_dev, channels_dev = embeddings.shape
    channels, tracks = head.shape
    genes = gene_owner.shape[1]
    capacity = gene_targets.shape[1]
    held = genes // places
    per_place = windows * held
    rows = places * per_place
    xs, cores = lax.axis_size("x"), lax.axis_size("c")

    ours = gather(embeddings.transpose(0, 2, 1), "x")
    whole = gather(ours, "c")

    row = jnp.arange(rows, dtype=jnp.int32)
    row_window = (row // held) % windows
    starts = by_place(exon_starts, places)
    ends = starts + by_place(exon_lengths, places)
    bins = place * bin_dev + jnp.arange(bin_dev, dtype=jnp.int32)
    inside = (bins >= starts[..., None]) & (bins < ends[..., None])
    cover = jnp.sum(inside.astype(F32), axis=1)
    in_window = row_window[:, None] == jnp.arange(windows)
    cover = (cover[:, None, :] * in_window[..., None].astype(F32)).astype(BF16)
    cover = cover.reshape(rows, windows * bin_dev)
    slot_of = slot_table(gene_owner, capacity)
    slot_row = by_place(slot_of, places)
    here = place * capacity + jnp.arange(capacity, dtype=jnp.int32)
    chosen = in_window[..., None] & (slot_row[:, None, None] == here)
    chosen = chosen.reshape(rows, windows * capacity)
    valid_here = jnp.any(chosen, axis=0).astype(F32)[:, None]
    targets_here = gene_targets.reshape(windows * capacity, tracks)
    targets_here = jnp.where(valid_here > 0, targets_here, 1.0)
    coded = spread(targets_here).astype(BF16)
    target_rows = jnp.dot(chosen.astype(BF16), coded, preferred_element_type=F32)
    target_part = jnp.sum((targets_here * valid_here).reshape(windows, capacity, tracks), axis=1)

    logits = jnp.einsum(
        "cxwkb,xckt->wbt",
        whole,
        head.reshape(xs, cores, channels_dev, tracks),
        preferred_element_type=F32,
    ).reshape(windows * bin_dev, tracks)
    pred = jax.nn.softplus(logits).astype(BF16)
    slope = jax.nn.sigmoid(logits)
    partial = jnp.dot(cover, pred, preferred_element_type=F32)
    total_part = jnp.sum(partial.reshape(places, windows, held, tracks), axis=(0, 2))

    piece = windows * tracks // places
    pieces = jnp.concatenate(
        [*halves(total_part.reshape(places, piece)), *halves(target_part.reshape(places, piece))], axis=1
    )
    extra = jnp.pad(pieces[:, None, :], ((0, 0), (0, per_place - 1), (0, 0)))
    sent = jnp.concatenate(
        [
            partial.astype(BF16).reshape(places, per_place, tracks),
            target_rows.astype(BF16).reshape(places, per_place, tracks),
            extra,
        ],
        axis=2,
    )
    got = jnp.sum(exchange(sent, SEQ).astype(F32), axis=0)
    gene_pred = got[:, :tracks]
    gene_tgt = unspread(got[:, tracks : 2 * tracks])
    ratio = squared(gene_tgt / gene_pred).astype(BF16)
    fit_part = jnp.sum((gene_tgt * jnp.log(gene_pred)).reshape(windows, held, tracks), axis=1)
    sums = got[0, 2 * tracks :].reshape(2, 2, piece).sum(axis=1)
    common = jnp.concatenate(halves(sums), axis=1).reshape(4 * piece)
    fit_pieces = jnp.concatenate(halves(fit_part.reshape(places, piece)), axis=1)
    extra = jnp.concatenate(
        [
            jnp.broadcast_to(common, (places, 1, 4 * piece)),
            jnp.pad(fit_pieces, ((0, 0), (0, 2 * piece)))[:, None, :],
            jnp.zeros((places, per_place - 2, 4 * piece), BF16),
        ],
        axis=1,
    )
    sent = jnp.concatenate(
        [jnp.broadcast_to(ratio, (places, per_place, tracks)), extra], axis=2
    )
    got = exchange(sent, SEQ)
    ratios = got[:, :, :tracks].reshape(rows, tracks)
    sums = got[:, 0, tracks:].astype(F32).reshape(places, 2, 2, piece).sum(axis=2)
    total = sums[:, 0].reshape(windows, tracks)
    target_sum = sums[:, 1].reshape(windows, tracks)
    fit_piece = jnp.sum(got[:, 1, tracks : tracks + 2 * piece].astype(F32), axis=0).reshape(2, piece).sum(axis=0)

    scale = genes / target_sum
    level = scale * (0.2 + 0.8 * target_sum / total)
    gene_grad = (
        level[None, :, None, :] - scale[None, :, None, :] * rooted(ratios.astype(F32)).reshape(places, windows, held, tracks)
    ).astype(BF16).reshape(rows, tracks)
    bin_grad = lax.dot_general(cover, gene_grad, (((0,), (0,)), ((), ())), preferred_element_type=F32)
    logit_grad = (bin_grad * slope).astype(BF16).reshape(windows, bin_dev, tracks)
    grad = jnp.einsum("cxwkb,wbt->xckt", whole, logit_grad, preferred_element_type=F32)
    block = channels // places
    grad = grad.astype(BF16).reshape(places, block, tracks)
    spare = jnp.concatenate(halves(fit_piece))
    spare = jnp.pad(spare, (0, tracks - 2 * piece))
    sent = jnp.concatenate(
        [grad, jnp.broadcast_to(spare, (places, 1, tracks)), jnp.zeros((places, 1, tracks), BF16)], axis=1
    )
    got = exchange(sent, SEQ)
    grad_head = jnp.sum(got[:, :block].astype(F32), axis=0)
    fit = got[:, block, : 2 * piece].astype(F32).reshape(places, 2, piece).sum(axis=1).reshape(windows, tracks)
    log_total = jnp.log(total)
    loss = (-fit + target_sum * log_total + 0.2 * (total - target_sum * log_total)) / target_sum
    back = lax.dot_general(chosen.astype(BF16), ratios, (((0,), (0,)), ((), ())), preferred_element_type=F32)
    gene_here = jnp.where(valid_here > 0, targets_here / rooted(jnp.where(valid_here > 0, back, 1.0)), 0.0)
    return (gene_here.reshape(gene_targets.shape), loss, grad_head)


def solution(mesh):
    fine = Mesh(mesh.devices.reshape(8, 8, 4, 2), ("y", "z", "x", "c"))
    return jax.shard_map(
        per_device,
        mesh=fine,
        in_specs=(P(None, SEQ, ("x", "c")), P(None, ("x", "c")), P(), P(), P(), P(None, SEQ, ("x", "c"))),
        out_specs=(P(None, SEQ, ("x", "c")), P(None, ("x", "c")), P(SEQ, ("x", "c"))),
        check_vma=False,
    )
```

time: 665 us -> 200 us (0.30)
  the two profiles are of different devices: /device:TPU:2 before, /device:TPU:24 now
where the time goes in v1:
time: 200 us
  waiting for transfers between devices  110 us (55%)
  starting transfers between devices  34.4 us (17%)
  other arithmetic  20.3 us (10%)
  local copies, waits for them, and re-layouts  20.1 us (10%)
  matrix products  7.92 us (4%)
  blocking collectives  5.31 us (3%)
    all_to_all x4, waiting for transfers between devices, exchange(): return lax.all_to_all(blocks, axes, split_axis=0, concat_axis=0, tiled=True)  110 us
    all_to_all x4, starting transfers between devices, exchange(): return lax.all_to_all(blocks, axes, split_axis=0, concat_axis=0, tiled=True)  34.4 us
    all_to_all x1, blocking collectives, exchange(): return lax.all_to_all(blocks, axes, split_axis=0, concat_axis=0, tiled=True)  5.31 us
  transfers between devices with their start and end apart: 4, of which 4 were waited for; matrix products, arithmetic and copies ran while one was open for 5% of the time, Pallas kernels for 0%

profile of v1, /device:TPU:24, one launch (start us, length us, event | category | flops | bytes accessed | tf_op | source)
XLA Modules:
  0.0 199.5 jit_solution(13781200873346887141)
XLA Ops:
  0.7 2.2 %broadcast_in_dim.76 = bf16[4,4,240,128]{3,2,1,0:T(8,128)(2,1)} broadcast(bf16[4,240,128]{2,1,0:T(8,128)(2,1)} %bitcast.94), dimensions={1,2,3} | broadcast | bytes 1228800 | tf_op jit(solution)/shard_map/broadcast_in_dim | solution.py:18
  2.8 4.3 %all-to-all-start = ((bf16[4,4,240,128]{3,2,1,0:T(8,128)(2,1)}), bf16[4,4,240,128]{3,2,1,0:T(8,128)(2,1)S(1)}, u32[]{:S(2)}, u32[]{:S(2)}) async-start(bf16[4,4,240,128]{3,2,1,0:T(8,128)(2,1)} %broadcast_in_dim.76), calls=%async_computation | async-start | bytes 1966080 | tf_op jit(solution)/shard_map/all_to_all | solution.py:13
  7.2 0.2 convert_reduce_fusion.3
  7.5 0.5 copy.108
  8.5 0.5 copy-done.11
  9.2 0.6 reduce-precision_convert_fusion.1
  9.8 0.5 iota_add_fusion
  10.3 0.9 copy.113
  11.4 0.8 copy.111
  12.4 1.2 fusion.13
  13.6 2.9 %convert_reduce_fusion.2 = f32[512,128]{1,0:T(8,128)S(1)} fusion(s32[512,8]{1,0:T(8,128)S(1)} %add.83, s32[512,8]{1,0:T(8,128)S(1)} %bitcast.85, s32[128]{0:T(128)S(1)} %copy-done.14), kind=kLoop, calls=%fused_computation.7 | loop fusion | flops 2555904 | bytes 295424 | tf_op jit(solution)/shard_map/reduce_sum | solution.py:86
  16.5 0.7 multiply_convert_fusion
  17.3 4.3 %all-to-all-done = bf16[4,4,240,128]{3,2,1,0:T(8,128)(2,1)S(1)} async-done(((bf16[4,4,240,128]{3,2,1,0:T(8,128)(2,1)}), bf16[4,4,240,128]{3,2,1,0:T(8,128)(2,1)S(1)}, u32[]{:S(2)}, u32[]{:S(2)}) %all-to-all-start) | async-done | bytes 983072 | tf_op jit(solution)/shard_map/all_to_all | solution.py:13
  21.5 0.3 broadcast_in_dim.77
  21.8 5.3 %all_to_all.25 = bf16[2,4,4,240,128]{4,3,2,1,0:T(8,128)(2,1)S(1)} all-to-all(bf16[2,4,4,240,128]{4,3,2,1,0:T(8,128)(2,1)S(1)} %broadcast_in_dim.77), channel_id=1, replica_groups=mesh['y'=8,'z'=8,'x'=4,'c'=2] {'c'}, dimensions={0} | all-to-all | bytes 3932160 | tf_op jit(solution)/shard_map/all_to_all | solution.py:13
  27.1 1.3 fusion.6
  28.4 1.0 copy-done.15
  29.4 1.8 fusion.20
  31.2 1.8 reshape.324
  33.1 1.3 convert_bitcast_fusion
  34.4 1.0 reduce_sum.110
  35.4 0.8 reshape.325
  36.2 0.8 maximum_bitcast_fusion
  37.0 2.2 %fusion.14 = bf16[64,8,1152]{2,1,0:T(8,128)(2,1)} fusion(bf16[64,1,128]{2,1,0:T(2,128)(2,1)S(1)} %copy.136, bf16[64,8,512]{2,1,0:T(8,128)(2,1)} %fusion.13, bf16[64,8,512]{2,1,0:T(8,128)(2,1)S(1)} %convert_bitcast_fusion), kind=kLoop, calls=%fused_computation.22 | loop fusion | flops 4718592 | bytes 2244608 | tf_op jit(solution)/shard_map/concatenate | solution.py:118
  39.2 16.4 %all-to-all-start.2 = ((bf16[64,8,1152]{2,1,0:T(8,128)(2,1)}), bf16[64,8,1152]{2,1,0:T(8,128)(2,1)S(1)}, u32[]{:S(2)}, u32[]{:S(2)}) async-start(bf16[64,8,1152]{2,1,0:T(8,128)(2,1)} %fusion.14), calls=%async_computation.2 | async-start | bytes 2359296 | tf_op jit(solution)/shard_map/all_to_all | solution.py:13
  55.6 32.7 %all-to-all-done.2 = bf16[64,8,1152]{2,1,0:T(8,128)(2,1)S(1)} async-done(((bf16[64,8,1152]{2,1,0:T(8,128)(2,1)}), bf16[64,8,1152]{2,1,0:T(8,128)(2,1)S(1)}, u32[]{:S(2)}, u32[]{:S(2)}) %all-to-all-start.2) | async-done | bytes 1179680 | tf_op jit(solution)/shard_map/all_to_all | solution.py:13
  88.4 0.2 convert_reduce_fusion.1
  89.2 1.0 maximum_maximum_fusion.1
  90.2 7.2 %all-to-all-start.3 = ((bf16[64,8,640]{2,1,0:T(8,128)(2,1)}), bf16[64,8,640]{2,1,0:T(8,128)(2,1)S(1)}, u32[]{:S(2)}, u32[]{:S(2)}) async-start(bf16[64,8,640]{2,1,0:T(8,128)(2,1)} %maximum_maximum_fusion.1), calls=%async_computation.3 | async-start | bytes 1310720 | tf_op jit(solution)/shard_map/all_to_all | solution.py:13
  97.5 20.4 %all-to-all-done.3 = bf16[64,8,640]{2,1,0:T(8,128)(2,1)S(1)} async-done(((bf16[64,8,640]{2,1,0:T(8,128)(2,1)}), bf16[64,8,640]{2,1,0:T(8,128)(2,1)S(1)}, u32[]{:S(2)}, u32[]{:S(2)}) %all-to-all-start.3) | async-done | bytes 655392 | tf_op jit(solution)/shard_map/all_to_all | solution.py:13
  118.6 0.2 convert_compare_fusion
  118.9 0.3 fusion.15
  119.2 0.6 copy.133
  119.8 0.2 fusion.18
  120.1 0.5 copy.125
  120.6 1.0 convert_element_type.185
  121.6 2.2 %fusion.12 = bf16[512,512]{1,0:T(8,128)(2,1)S(1)} fusion(bf16[512,512]{1,0:T(8,128)(2,1)} %convert_element_type.185, f32[512,512]{1,0:T(8,128)} %copy-done.15, bf16[64,8,4,128]{3,2,1,0:T(4,128)(2,1)} %bitcast.91), kind=kOutput, calls=%fused_computation.20 | convolution fusion | flops 269746176 | bytes 2621440 | tf_op jit(solution)/shard_map/dot_general | solution.py:157
  123.9 1.2 fusion.5
  125.1 1.5 copy.126
  126.5 3.9 %reshape.333 = bf16[64,30,512]{2,1,0:T(8,128)(2,1)} reshape(bf16[4,2,240,512]{3,2,1,0:T(8,128)(2,1)} %copy.126) | data formatting | bytes 3932160 | tf_op jit(solution)/shard_map/reshape | solution.py:161
  130.5 3.9 %maximum_maximum_fusion = bf16[64,32,512]{2,1,0:T(8,128)(2,1)} fusion(bf16[64,1,512]{2,1,0:T(2,128)(2,1)S(1)} %broadcast_in_dim.85, bf16[64,30,512]{2,1,0:T(8,128)(2,1)} %reshape.333, bf16[32]{0:T(256)(128)(2,1)S(1)} %pad.17.clone), kind=kLoop, calls=%fused_computation.6 | loop fusion | flops 6291456 | bytes 4128832 | tf_op jit(solution)/shard_map/concatenate | solution.py:164
  134.5 6.5 %all-to-all-start.4 = ((bf16[64,32,512]{2,1,0:T(8,128)(2,1)}), bf16[64,32,512]{2,1,0:T(8,128)(2,1)}, u32[]{:S(2)}, u32[]{:S(2)}) async-start(bf16[64,32,512]{2,1,0:T(8,128)(2,1)} %maximum_maximum_fusion), calls=%async_computation.4 | async-start | bytes 4194304 | tf_op jit(solution)/shard_map/all_to_all | solution.py:13
  141.1 0.2 fusion.33
  141.3 0.6 reshape.331
  142.0 53.1 %all-to-all-done.4 = bf16[64,32,512]{2,1,0:T(8,128)(2,1)} async-done(((bf16[64,32,512]{2,1,0:T(8,128)(2,1)}), bf16[64,32,512]{2,1,0:T(8,128)(2,1)}, u32[]{:S(2)}, u32[]{:S(2)}) %all-to-all-start.4) | async-done | bytes 2097184 | tf_op jit(solution)/shard_map/all_to_all | solution.py:13
  195.1 0.9 slice.48
  196.3 0.6 add_divide_fusion
  196.9 2.6 %convert_reduce_fusion = f32[30,512]{1,0:T(8,128)} fusion(bf16[64,32,512]{2,1,0:T(8,128)(2,1)} %all-to-all-done.4), kind=kLoop, calls=%fused_computation | loop fusion | flops 1950720 | bytes 2027520 | tf_op jit(solution)/shard_map/reduce_sum | solution.py:168
  (91 shorter events, 3.2 us)
Async XLA Ops:
  0.6 26.5 %copy-start = (bf16[1920,512]{1,0:T(8,128)(2,1)S(1)}, bf16[1920,512]{1,0:T(8,128)(2,1)}, u32[]{:S(2)}) copy-start(bf16[1920,512]{1,0:T(8,128)(2,1)} %param.7) | copy-start | bytes 5898244
  0.6 6.5 %copy-start.9 = (s32[4,128]{1,0:T(4,128)S(1)}, s32[4,128]{1,0:T(4,128)}, u32[]{:S(2)}) copy-start(s32[4,128]{1,0:T(4,128)} %param.10) | copy-start | bytes 6148
  0.7 8.4 %copy-start.5 = (f32[4,4,512]{2,1,0:T(4,128)S(1)}, f32[4,4,512]{2,1,0:T(4,128)}, u32[]{:S(2)}) copy-start(f32[4,4,512]{2,1,0:T(4,128)} %param.11) | copy-start | bytes 98308
  0.7 10.5 %copy-start.10 = (s32[4,128,8]{1,2,0:T(8,128)S(1)}, s32[4,128,8]{1,2,0:T(8,128)}, u32[]{:S(2)}) copy-start(s32[4,128,8]{1,2,0:T(8,128)} %param.8) | copy-start | bytes 49156
  2.8 18.7 %all-to-all-start = ((bf16[4,4,240,128]{3,2,1,0:T(8,128)(2,1)}), bf16[4,4,240,128]{3,2,1,0:T(8,128)(2,1)S(1)}, u32[]{:S(2)}, u32[]{:S(2)}) async-start(bf16[4,4,240,128]{3,2,1,0:T(8,128)(2,1)} %broadcast_in_dim.76), calls=%async_computation | async-start | bytes 1966080 | tf_op jit(solution)/shard_map/all_to_all | solution.py:13
  8.5 5.2 %copy-start.7 = (pred[512,4,4]{0,2,1:T(4,128)(4,1)}, pred[512,4,4]{0,2,1:T(4,128)(4,1)S(1)}, u32[]{:S(2)}) copy-start(pred[512,4,4]{0,2,1:T(4,128)(4,1)S(1)} %get-tuple-element.4) | copy-start | bytes 24580
  8.5 0.5 copy-start.11
  11.2 1.2 copy-start.12
  11.2 2.4 %copy-start.14 = (s32[128]{0:T(128)S(1)}, s32[128]{0:T(128)}, u32[]{:S(2)}) copy-start(s32[128]{0:T(128)} %iota_add_fusion) | copy-start | bytes 1540
  12.3 4.2 %copy-start.3 = (f32[512,4]{1,0:T(8,128)S(1)}, f32[512,4]{1,0:T(8,128)}, u32[]{:S(2)}) copy-start(f32[512,4]{1,0:T(8,128)} %copy.113) | copy-start | bytes 24580
  17.2 11.2 %copy-start.4 = (bf16[512,4,128]{2,1,0:T(4,128)(2,1)}, bf16[512,4,128]{2,1,0:T(4,128)(2,1)S(1)}, u32[]{:S(2)}) copy-start(bf16[512,4,128]{2,1,0:T(4,128)(2,1)S(1)} %multiply_convert_fusion) | copy-start | bytes 1572868
  27.1 1.3 copy-start.1
  28.4 1.0 copy-start.15
  39.2 49.2 %all-to-all-start.2 = ((bf16[64,8,1152]{2,1,0:T(8,128)(2,1)}), bf16[64,8,1152]{2,1,0:T(8,128)(2,1)S(1)}, u32[]{:S(2)}, u32[]{:S(2)}) async-start(bf16[64,8,1152]{2,1,0:T(8,128)(2,1)} %fusion.14), calls=%async_computation.2 | async-start | bytes 2359296 | tf_op jit(solution)/shard_map/all_to_all | solution.py:13
  90.2 27.7 %all-to-all-start.3 = ((bf16[64,8,640]{2,1,0:T(8,128)(2,1)}), bf16[64,8,640]{2,1,0:T(8,128)(2,1)S(1)}, u32[]{:S(2)}, u32[]{:S(2)}) async-start(bf16[64,8,640]{2,1,0:T(8,128)(2,1)} %maximum_maximum_fusion.1), calls=%async_computation.3 | async-start | bytes 1310720 | tf_op jit(solution)/shard_map/all_to_all | solution.py:13
  121.6 2.2 %copy-start.2 = (bf16[2,4,4,240,128]{4,3,2,1,0:T(8,128)(2,1)S(1)}, bf16[2,4,4,240,128]{4,3,2,1,0:T(8,128)(2,1)}, u32[]{:S(2)}) copy-start(bf16[2,4,4,240,128]{4,3,2,1,0:T(8,128)(2,1)} %copy-done.1) | copy-start | bytes 5898244
  134.5 6.5 %copy-start.6 = (f32[4,4,512]{2,1,0:T(4,128)S(1)}, f32[4,4,512]{2,1,0:T(4,128)}, u32[]{:S(2)}) copy-start(f32[4,4,512]{2,1,0:T(4,128)} %param.11) | copy-start | bytes 98308
  134.5 6.5 %copy-start.8 = (pred[512,4,4]{0,2,1:T(4,128)(4,1)S(1)}, pred[512,4,4]{0,2,1:T(4,128)(4,1)}, u32[]{:S(2)}) copy-start(pred[512,4,4]{0,2,1:T(4,128)(4,1)} %copy-done.7) | copy-start | bytes 24580
  134.5 6.5 %copy-start.13 = (pred[4,4]{1,0:T(4,128)(4,1)S(1)}, pred[4,4]{1,0:T(4,128)(4,1)}, u32[]{:S(2)}) copy-start(pred[4,4]{1,0:T(4,128)(4,1)} %copy-done.11) | copy-start | bytes 52
  134.5 60.6 %all-to-all-start.4 = ((bf16[64,32,512]{2,1,0:T(8,128)(2,1)}), bf16[64,32,512]{2,1,0:T(8,128)(2,1)}, u32[]{:S(2)}, u32[]{:S(2)}) async-start(bf16[64,32,512]{2,1,0:T(8,128)(2,1)} %maximum_maximum_fusion), calls=%async_computation.4 | async-start | bytes 4194304 | tf_op jit(solution)/shard_map/all_to_all | solution.py:13

commit v2 on v1

v2 whole, which is shorter than its diff:
```python
import jax
import jax.numpy as jnp
import numpy as np
from jax import lax
from jax.experimental import pallas as pl
from jax.experimental.pallas import tpu as pltpu
from jax.sharding import Mesh, PartitionSpec as P

SEQ = ("y", "z")
EVERY = ("y", "z", "x", "c")
F32 = jnp.float32
BF16 = jnp.bfloat16
MIDDLE = 28.28
LANES = 128
VMEM = pl.BlockSpec(memory_space=pltpu.VMEM)
SMEM = pl.BlockSpec(memory_space=pltpu.SMEM)


def exchange(blocks, axes, groups=None):
    return lax.all_to_all(blocks, axes, split_axis=0, concat_axis=0, axis_index_groups=groups, tiled=True)


def gather(block, axes):
    size = lax.axis_size(axes)
    return exchange(jnp.broadcast_to(block[None], (size,) + block.shape), axes)


def mixed_groups(shape):
    ids = np.arange(int(np.prod(shape))).reshape(shape)
    ahead, after = [], []
    for x in range(shape[2]):
        for k in range(shape[0]):
            ahead += [ids[:, k, x, 0].tolist(), ids[k, :, x, 1].tolist()]
            after += [ids[k, :, x, 0].tolist(), ids[:, k, x, 1].tolist()]
    return ahead, after


def spread(counts):
    scaled = counts * (1.0 / MIDDLE)
    for _ in range(4):
        scaled = scaled * scaled
    return scaled


def unspread(coded):
    for _ in range(4):
        coded = jnp.sqrt(coded)
    return coded * MIDDLE


def squared(ratio):
    small = ratio < 2.0**63
    scaled = jnp.where(small, ratio, ratio * 2.0**-96)
    return jnp.where(small, scaled * scaled, -(scaled * scaled))


def rooted(coded):
    root = jnp.sqrt(jnp.abs(coded))
    return jnp.where(coded < 0, root * 2.0**96, root)


def split(values):
    high = values.astype(BF16).astype(F32)
    return high, values - high


def even_rows(shape):
    return lax.broadcasted_iota(jnp.int32, shape, 0) % 2 == 0


def up(values):
    return pltpu.roll(values, values.shape[0] - 1, 0)


def down(values):
    return pltpu.roll(values, 1, 0)


def slot_table(gene_owner, capacity):
    genes = gene_owner.shape[1]
    same = gene_owner[:, :, None] == gene_owner[:, None, :]
    earlier = jnp.arange(genes)[None, :] < jnp.arange(genes)[:, None]
    ahead = jnp.sum((same & earlier[None]).astype(jnp.int32), axis=2)
    return gene_owner * capacity + ahead


def by_place(table, places):
    windows, genes = table.shape[:2]
    held = genes // places
    parts = table.reshape((windows, places, held) + table.shape[2:])
    return jnp.moveaxis(parts, 1, 0).reshape((genes * windows,) + table.shape[2:])


def cover_kernel(windows, held, at_ref, starts_ref, lengths_ref, cover_ref, turned_ref):
    exons, rows = starts_ref.shape
    bins = cover_ref.shape[1] // windows
    position = lax.broadcasted_iota(jnp.int32, (bins, rows), 0) + at_ref[0] * bins
    base = jnp.zeros((bins, rows), F32)
    for e in range(exons):
        past = position - starts_ref[e : e + 1, :]
        base += jnp.where((past >= 0) & (past < lengths_ref[e : e + 1, :]), 1.0, 0.0)
    owner = (lax.broadcasted_iota(jnp.int32, (bins, rows), 1) // held) % windows
    for w in range(windows):
        mine = jnp.where(owner == w, base, 0.0)
        turned_ref[w * bins : (w + 1) * bins, :] = mine.astype(BF16)
        cover_ref[:, w * bins : (w + 1) * bins] = mine.T.astype(BF16)


def forward_kernel(whole_ref, head_ref, cover_ref, target_ref, tsum_ref, sent_ref, slope_ref, pred_ref):
    parts, windows, _, bins = whole_ref.shape
    cores = 2
    places, per_place, tracks = target_ref.shape
    for w in range(windows):
        logits = jnp.zeros((bins, tracks), F32)
        for k in range(parts):
            core, x = divmod(k, parts // cores)
            logits += lax.dot_general(
                whole_ref[k, w], head_ref[x * cores + core], (((0,), (0,)), ((), ())), preferred_element_type=F32
            )
        low = jnp.exp(-jnp.abs(logits))
        pred_ref[w * bins : (w + 1) * bins, :] = (jnp.maximum(logits, 0.0) + jnp.log1p(low)).astype(BF16)
        slope_ref[w * bins : (w + 1) * bins, :] = jnp.where(logits >= 0, 1.0, low) / (1.0 + low)
    partial = jnp.dot(cover_ref[...], pred_ref[...], preferred_element_type=F32)
    partial = partial.reshape(places, per_place, tracks)
    sent_ref[:, :, :tracks] = partial.astype(BF16)
    sent_ref[:, :, tracks : 2 * tracks] = target_ref[...]
    sent_ref[:, :, 2 * tracks :] = jnp.zeros((places, per_place, LANES), BF16)
    total = jnp.sum(partial, axis=0)
    high, low = split(total + up(total))
    total = jnp.where(even_rows(total.shape), high, down(low)).astype(BF16)
    chunks = tracks // LANES
    for j in range(chunks):
        cut = slice(j * LANES, (j + 1) * LANES)
        for i in range(2):
            sent_ref[i * chunks + j, :, 2 * tracks :] = total[:, cut]
            sent_ref[(i + 2) * chunks + j, :, 2 * tracks :] = tsum_ref[:, cut]


def middle_kernel(at_ref, got_ref, sent_ref):
    places, per_place, width = got_ref.shape
    tracks = (width - LANES) // 2
    chunks = tracks // LANES
    got = jnp.sum(got_ref[...].astype(F32), axis=0)
    gene_pred = got[:, :tracks]
    gene_target = unspread(got[:, tracks : 2 * tracks])
    ratio = squared(gene_target / gene_pred).astype(BF16)
    sent_ref[:, :, :tracks] = jnp.broadcast_to(ratio[None], (places, per_place, tracks))
    fit = gene_target * jnp.log(gene_pred)
    fit = fit + down(fit)
    sums = got[:, 2 * tracks :]
    high, low = split(sums + up(sums))
    common = jnp.where(at_ref[0] % (2 * chunks) < chunks, high, low)
    even = even_rows(common.shape)
    common = jnp.where(even, common, 0.0)
    sent_ref[:, :, tracks:] = jnp.broadcast_to(common.astype(BF16)[None], (places, per_place, LANES))
    for j in range(chunks):
        cut = slice(j * LANES, (j + 1) * LANES)
        sent_ref[j * at_ref[1], :, tracks:] = jnp.where(even, common, fit[:, cut]).astype(BF16)


def backward_kernel(genes, block, at_ref, got_ref, turned_ref, slope_ref, whole_ref, sent_ref, total_ref, tsum_ref):
    places, per_place, width = got_ref.shape
    parts, windows, depth, bins = whole_ref.shape
    tracks = width - LANES
    chunks = tracks // LANES
    side = 8
    padded = sent_ref.shape[1]

    def joined(first):
        pieces = [
            got_ref[first + j, :, tracks:].astype(F32) + got_ref[first + chunks + j, :, tracks:].astype(F32)
            for j in range(chunks)
        ]
        row = jnp.concatenate(pieces, axis=1)
        return jnp.where(even_rows(row.shape), row, down(row))

    total = joined(0)
    target_sum = joined(2 * chunks)
    total_ref[...] = total
    tsum_ref[...] = target_sum
    scale = genes / target_sum
    level = scale * (0.2 + 0.8 * target_sum / total)
    ratio = rooted(got_ref[:, :, :tracks].astype(F32))
    gene_grad = (level[None] - scale[None] * ratio).reshape(places * per_place, tracks).astype(BF16)
    bin_grad = jnp.dot(turned_ref[...], gene_grad, preferred_element_type=F32)
    logit_grad = (bin_grad * slope_ref[...]).astype(BF16)

    fit = jnp.sum(got_ref[:, :, tracks:].astype(F32), axis=0)
    high, low = split(fit)
    row = lax.broadcasted_iota(jnp.int32, (padded, LANES), 0)
    holder = at_ref[2] == 1
    spare = []
    for w in range(windows):
        top = jnp.where(row == block, jnp.broadcast_to(high[2 * w + 1 : 2 * w + 2, :], row.shape), 0.0)
        top += jnp.where(row == block + 1, jnp.broadcast_to(low[2 * w + 1 : 2 * w + 2, :], row.shape), 0.0)
        spare.append(top)
    spare = jnp.where(holder, jnp.concatenate(spare, axis=1), 0.0)

    cores = 2
    for k in range(parts):
        core, x = divmod(k, parts // cores)
        lhs = jnp.concatenate([whole_ref[k, w] for w in range(windows)], axis=1)
        grad = jnp.dot(lhs, logit_grad, preferred_element_type=F32)
        for i in range(side):
            upper = x * cores + core
            place = upper * at_ref[3] + i * at_ref[4]
            sent_ref[place] = (grad[i * padded : (i + 1) * padded] + spare).astype(BF16)


def per_device(embeddings, head, exon_starts, exon_lengths, gene_owner, gene_targets):
    places = lax.axis_size(SEQ)
    place = lax.axis_index(SEQ)
    core = lax.axis_index("c")
    side = lax.axis_size("y")
    windows, bin_dev, channels_dev = embeddings.shape
    channels, tracks = head.shape
    genes = gene_owner.shape[1]
    capacity = gene_targets.shape[1]
    held = genes // places
    per_place = windows * held
    rows = places * per_place
    xs, cores = lax.axis_size("x"), lax.axis_size("c")
    parts = xs * cores
    block = channels // places
    padded = -(-block // 16) * 16
    blocks_dev = channels_dev // block
    depth = blocks_dev * padded
    chunks = tracks // LANES

    local = embeddings.transpose(0, 2, 1).reshape(windows, blocks_dev, block, bin_dev)
    local = jnp.pad(local, ((0, 0), (0, 0), (0, padded - block), (0, 0))).reshape(windows, depth, bin_dev)
    ours = gather(local, "x")
    whole = gather(ours, "c").reshape(parts, windows, depth, bin_dev)

    padded_head = jnp.pad(head.reshape(places, block, tracks), ((0, 0), (0, padded - block), (0, 0)))
    padded_head = padded_head.reshape(parts, depth, tracks)

    first = core == 0
    stride = jnp.where(first, 1, side)
    holder = jnp.where(first, place < chunks, (place % side == 0) & (place < chunks * side))
    at = jnp.stack(
        [place, stride, holder.astype(jnp.int32), jnp.where(first, side, 1), jnp.where(first, 1, side)]
    ).astype(jnp.int32)

    cover, turned = pl.pallas_call(
        lambda *refs: cover_kernel(windows, held, *refs),
        out_shape=[
            jax.ShapeDtypeStruct((rows, windows * bin_dev), BF16),
            jax.ShapeDtypeStruct((windows * bin_dev, rows), BF16),
        ],
        in_specs=[SMEM, VMEM, VMEM],
        out_specs=[VMEM, VMEM],
        name="cover",
    )(at, by_place(exon_starts, places).T, by_place(exon_lengths, places).T)

    row_window = (jnp.arange(rows, dtype=jnp.int32) // held) % windows
    in_window = row_window[:, None] == jnp.arange(windows)
    slot_row = by_place(slot_table(gene_owner, capacity), places)
    here = place * capacity + jnp.arange(capacity, dtype=jnp.int32)
    chosen = in_window[..., None] & (slot_row[:, None, None] == here)
    chosen = chosen.reshape(rows, windows * capacity)
    valid_here = jnp.any(chosen, axis=0).astype(F32)[:, None]
    targets_here = gene_targets.reshape(windows * capacity, tracks)
    targets_here = jnp.where(valid_here > 0, targets_here, 1.0)
    target_rows = jnp.dot(chosen.astype(BF16), spread(targets_here).astype(BF16), preferred_element_type=F32)
    target_rows = target_rows.astype(BF16).reshape(places, per_place, tracks)
    target_part = jnp.sum((targets_here * valid_here).reshape(windows, capacity, tracks), axis=1)
    high = lax.reduce_precision(target_part, 8, 7)
    tsum = jnp.stack([high, target_part - high], axis=1).reshape(per_place, tracks).astype(BF16)

    sent, slope = pl.pallas_call(
        forward_kernel,
        out_shape=[
            jax.ShapeDtypeStruct((places, per_place, 2 * tracks + LANES), BF16),
            jax.ShapeDtypeStruct((windows * bin_dev, tracks), F32),
        ],
        in_specs=[VMEM] * 5,
        out_specs=[VMEM] * 2,
        scratch_shapes=[pltpu.VMEM((windows * bin_dev, tracks), BF16)],
        name="forward",
    )(whole, padded_head, cover, target_rows, tsum)

    sent = pl.pallas_call(
        middle_kernel,
        out_shape=jax.ShapeDtypeStruct((places, per_place, tracks + LANES), BF16),
        in_specs=[SMEM, VMEM],
        out_specs=VMEM,
        name="middle",
    )(at, exchange(sent, SEQ))
    got = exchange(sent, SEQ)

    sent, total, target_sum = pl.pallas_call(
        lambda *refs: backward_kernel(genes, block, *refs),
        out_shape=[
            jax.ShapeDtypeStruct((places, padded, tracks), BF16),
            jax.ShapeDtypeStruct((per_place, tracks), F32),
            jax.ShapeDtypeStruct((per_place, tracks), F32),
        ],
        in_specs=[SMEM, VMEM, VMEM, VMEM, VMEM],
        out_specs=[VMEM] * 3,
        name="backward",
    )(at, got, turned, slope, whole)

    ahead, after = mixed_groups((side, places // side, xs, cores))
    summed = exchange(sent.reshape(side, side * padded, tracks), EVERY, ahead)
    summed = jnp.sum(summed.reshape(side, side, padded, tracks).astype(F32), axis=0)
    summed = exchange(summed, EVERY, after)
    grad_head = jnp.sum(summed[:, :block], axis=0)
    fit = jnp.sum(summed[:chunks, block:], axis=1).reshape(chunks, windows, LANES)
    fit = fit.transpose(1, 0, 2).reshape(windows, tracks)
    total = total.reshape(windows, held, tracks)[:, 0]
    target_sum = target_sum.reshape(windows, held, tracks)[:, 0]
    log_total = jnp.log(total)
    loss = (-fit + target_sum * log_total + 0.2 * (total - target_sum * log_total)) / target_sum

    ratios = got[:, :, :tracks].reshape(rows, tracks)
    back = lax.dot_general(chosen.astype(BF16), ratios, (((0,), (0,)), ((), ())), preferred_element_type=F32)
    gene_here = jnp.where(valid_here > 0, targets_here / rooted(jnp.where(valid_here > 0, back, 1.0)), 0.0)
    return (gene_here.reshape(gene_targets.shape), loss, grad_head)


def solution(mesh):
    shape = (8, 8, 4, 2)
    fine = Mesh(mesh.devices.reshape(shape), EVERY)
    return jax.shard_map(
        per_device,
        mesh=fine,
        in_specs=(P(None, SEQ, ("x", "c")), P(None, ("x", "c")), P(), P(), P(), P(None, SEQ, ("x", "c"))),
        out_specs=(P(None, SEQ, ("x", "c")), P(None, ("x", "c")), P(SEQ, ("x", "c"))),
        check_vma=False,
    )
```

time: 200 us -> 174 us (0.87)
  the two profiles are of different devices: /device:TPU:24 before, /device:TPU:2 now
where the time goes in v2:
time: 174 us; the launch traced here: 173 us
  blocking collectives  115 us (66%)
  Pallas kernels  15.7 us (9%)
  starting transfers between devices  13 us (7%)
  waiting for transfers between devices  12.2 us (7%)
  local copies, waits for them, and re-layouts  11.7 us (7%)
  other arithmetic  3.06 us (2%)
    all_to_all x4, blocking collectives, exchange(): lax.all_to_all(blocks, axes, split_axis=0, concat_axis=0, axis_index_grou...  115 us
    all_to_all x2, starting transfers between devices, exchange(): lax.all_to_all(blocks, axes, split_axis=0, concat_axis=0, axis_index_grou...  13 us
    all_to_all x2, waiting for transfers between devices, exchange(): lax.all_to_all(blocks, axes, split_axis=0, concat_axis=0, axis_index_grou...  12.2 us
    pallas_call x1, Pallas kernels, per_device(): pl.pallas_call(lambda *refs: backward_kernel(genes, block, *refs), out_sh...  5.59 us
    pallas_call x1, Pallas kernels, per_device(): pl.pallas_call(forward_kernel, out_shape=[jax.ShapeDtypeStruct((places, p...  5.48 us
  transfers between devices with their start and end apart: 2, of which 1 were waited for; matrix products, arithmetic and copies ran while one was open for 6% of the time, Pallas kernels for 1%

profile of v2, /device:TPU:2, one launch (start us, length us, event | category | flops | bytes accessed | tf_op | source)
XLA Modules:
  0.0 173.4 jit_solution(15579017732292060998)
XLA Ops:
  0.6 1.0 copy.40
  1.7 0.1 pad.8
  1.8 0.0 copy-start.2
  1.8 0.0 copy-start.3
  1.8 1.2 broadcast_in_dim.50
  3.0 9.5 %all-to-all-start = ((bf16[4,4,256,128]{3,2,1,0:T(8,128)(2,1)}), bf16[4,4,256,128]{3,2,1,0:T(8,128)(2,1)S(1)}, u32[]{:S(2)}, u32[]{:S(2)}) async-start(bf16[4,4,256,128]{3,2,1,0:T(8,128)(2,1)} %broadcast_in_dim.50), calls=%async_computation | async-start | bytes 2097152 | tf_op jit(solution)/shard_map/all_to_all | solution.py:20
  12.6 0.0 copy-done.2
  12.6 0.2 convert_reduce_fusion.1
  12.9 0.1 copy.38
  13.0 0.5 copy.39
  13.5 0.2 eq.66
  13.6 0.1 iota_compare_fusion.1
  13.7 0.2 fusion.16
  13.9 0.0 copy-done.3
  13.9 0.1 copy.42
  14.0 0.1 copy.43
  14.1 0.7 copy.44
  14.9 0.0 copy-done.4
  14.9 0.1 copy.45
  15.0 0.1 copy.46
  15.1 0.7 copy.47
  15.8 0.0 copy-done.1
  15.8 0.1 multiply_reduce_fusion
  16.0 0.6 convert_element_type.40.tsum_ref
  16.6 2.6 %reshape.222 = bf16[64,30,512]{2,1,0:T(8,128)(2,1)S(1)} reshape(bf16[1920,512]{1,0:T(8,128)(2,1)} %param.7) | data formatting | bytes 3932160 | tf_op jit(solution)/shard_map/reshape | solution.py:235
  19.2 1.5 pad.9
  20.7 0.7 stack.30.refs_0_.at_ref
  21.4 2.3 %cover.1 = (bf16[512,512]{1,0:T(8,128)(2,1)}, bf16[512,512]{1,0:T(8,128)(2,1)}) custom-call(s32[5]{0:T(128)} %stack.30.refs_0_.at_ref, s32[8,512]{1,0:T(8,128)} %bitcast.69, s32[8,512]{1,0:T(8,128)} %bitcast.70), custom_call_target="tpu_custom_call" | custom-call | tf_op jit(solution)/shard_map/cover/pallas_call | solution.py:245
  23.6 1.2 fusion.1.target_ref
  24.8 0.0 all-to-all-done
  24.8 0.5 broadcast_in_dim.51
  25.3 6.3 %all_to_all.30 = bf16[2,4,4,256,128]{4,3,2,1,0:T(8,128)(2,1)} all-to-all(bf16[2,4,4,256,128]{4,3,2,1,0:T(8,128)(2,1)S(1)} %broadcast_in_dim.51), channel_id=1, replica_groups=mesh['y'=8,'z'=8,'x'=4,'c'=2] {'c'}, dimensions={0} | all-to-all | bytes 4194304 | tf_op jit(solution)/shard_map/all_to_all | solution.py:20
  31.6 5.5 %forward.1 = (bf16[64,8,1152]{2,1,0:T(8,128)(2,1)}, f32[512,512]{1,0:T(8,128)}) custom-call(bf16[8,4,256,128]{3,2,1,0:T(8,128)(2,1)} %bitcast.57, bf16[8,256,512]{2,1,0:T(8,128)(2,1)} %bitcast.59, bf16[512,512]{1,0:T(8,128)(2,1)} %get-tuple-element.10.cover_ref, bf16[64,8,512]{2,1,0:T(8,128)(2,1)} %fusion.1.target_ref, ...), custom_call_target="tpu_custom_call" | custom-call | tf_op jit(solution)/shard_map/forward/pallas_call | solution.py:271
  37.1 45.7 %all_to_all.31.got_ref = bf16[64,8,1152]{2,1,0:T(8,128)(2,1)} all-to-all(bf16[64,8,1152]{2,1,0:T(8,128)(2,1)} %get-tuple-element.11), channel_id=1, replica_groups=mesh['y'=8,'z'=8,'x'=4,'c'=2] {'y','z'}, dimensions={0} | all-to-all | bytes 2359296 | tf_op jit(solution)/shard_map/all_to_all | solution.py:20
  82.8 2.4 %middle.1 = bf16[64,8,640]{2,1,0:T(8,128)(2,1)} custom-call(s32[5]{0:T(128)} %stack.30.refs_0_.at_ref, bf16[64,8,1152]{2,1,0:T(8,128)(2,1)} %all_to_all.31.got_ref), custom_call_target="tpu_custom_call" | custom-call | tf_op jit(solution)/shard_map/middle/pallas_call | solution.py:283
  85.1 28.5 %all_to_all.32.refs_1_ = bf16[64,8,640]{2,1,0:T(8,128)(2,1)} all-to-all(bf16[64,8,640]{2,1,0:T(8,128)(2,1)} %middle.1), channel_id=1, replica_groups=mesh['y'=8,'z'=8,'x'=4,'c'=2] {'y','z'}, dimensions={0} | all-to-all | bytes 1310720 | tf_op jit(solution)/shard_map/all_to_all | solution.py:20
  113.7 5.6 %backward.1 = (bf16[64,32,512]{2,1,0:T(8,128)(2,1)}, f32[8,512]{1,0:T(8,128)}, f32[8,512]{1,0:T(8,128)}) custom-call(s32[5]{0:T(128)} %stack.30.refs_0_.at_ref, bf16[64,8,640]{2,1,0:T(8,128)(2,1)} %all_to_all.32.refs_1_, bf16[512,512]{1,0:T(8,128)(2,1)} %get-tuple-element.12.refs_2_, f32[512,512]{1,0:T(8,128)} %get-tuple-element.13.refs_3_, ...), custom_call_target="tpu_custom_call" | custom-call | tf_op jit(solution)/shard_map/backward/pallas_call | solution.py:292
  119.3 34.8 %all_to_all.33 = bf16[8,256,512]{2,1,0:T(8,128)(2,1)S(1)} all-to-all(bf16[8,256,512]{2,1,0:T(8,128)(2,1)} %bitcast.60), channel_id=1, replica_groups={{0,64,128,192,256,320,384,448},{1,9,17,25,33,41,49,57},{8,72,136,200,26..., dimensions={0} | all-to-all | bytes 4194304 | tf_op jit(solution)/shard_map/all_to_all | solution.py:20
  154.1 1.1 convert_reduce_fusion
  155.2 3.5 %all-to-all-start.5 = ((f32[8,32,512]{2,1,0:T(8,128)}), f32[8,32,512]{2,1,0:T(8,128)S(1)}, u32[]{:S(2)}, u32[]{:S(2)}) async-start(f32[8,32,512]{2,1,0:T(8,128)} %bitcast.23), calls=%async_computation.5 | async-start | bytes 1048576 | tf_op jit(solution)/shard_map/all_to_all | solution.py:20
  158.7 0.1 gt.15
  158.8 0.0 copy-done.6
  158.9 0.0 copy-done.5
  158.9 0.2 fusion.3
  159.2 0.6 reshape.230
  159.8 12.2 %all-to-all-done.5 = f32[8,32,512]{2,1,0:T(8,128)S(1)} async-done(((f32[8,32,512]{2,1,0:T(8,128)}), f32[8,32,512]{2,1,0:T(8,128)S(1)}, u32[]{:S(2)}, u32[]{:S(2)}) %all-to-all-start.5) | async-done | bytes 524320 | tf_op jit(solution)/shard_map/all_to_all | solution.py:20
  172.1 0.6 fusion.9
  172.7 0.7 slice_reduce_fusion
  (23 shorter events, 0.3 us)
Async XLA Ops:
  1.8 10.8 %copy-start.2 = (s32[4,128]{1,0:T(4,128)S(1)}, s32[4,128]{1,0:T(4,128)}, u32[]{:S(2)}) copy-start(s32[4,128]{1,0:T(4,128)} %param.10) | copy-start | bytes 6148
  1.8 12.1 %copy-start.3 = (s32[4,128,8]{1,2,0:T(8,128)S(1)}, s32[4,128,8]{1,2,0:T(8,128)}, u32[]{:S(2)}) copy-start(s32[4,128,8]{1,2,0:T(8,128)} %param.8) | copy-start | bytes 49156
  3.0 11.8 %copy-start.4 = (s32[4,128,8]{1,2,0:T(8,128)S(1)}, s32[4,128,8]{1,2,0:T(8,128)}, u32[]{:S(2)}) copy-start(s32[4,128,8]{1,2,0:T(8,128)} %param.9) | copy-start | bytes 49156
  3.0 12.8 %copy-start.1 = (f32[4,4,512]{2,1,0:T(4,128)S(1)}, f32[4,4,512]{2,1,0:T(4,128)}, u32[]{:S(2)}) copy-start(f32[4,4,512]{2,1,0:T(4,128)} %param.11) | copy-start | bytes 98308
  3.0 21.8 %all-to-all-start = ((bf16[4,4,256,128]{3,2,1,0:T(8,128)(2,1)}), bf16[4,4,256,128]{3,2,1,0:T(8,128)(2,1)S(1)}, u32[]{:S(2)}, u32[]{:S(2)}) async-start(bf16[4,4,256,128]{3,2,1,0:T(8,128)(2,1)} %broadcast_in_dim.50), calls=%async_computation | async-start | bytes 2097152 | tf_op jit(solution)/shard_map/all_to_all | solution.py:20
  154.1 4.8 %copy-start.6 = (f32[8,512]{1,0:T(8,128)S(1)}, f32[8,512]{1,0:T(8,128)}, u32[]{:S(2)}) copy-start(f32[8,512]{1,0:T(8,128)} %get-tuple-element.15) | copy-start | bytes 49156
  154.1 4.8 %copy-start.5 = (f32[8,512]{1,0:T(8,128)S(1)}, f32[8,512]{1,0:T(8,128)}, u32[]{:S(2)}) copy-start(f32[8,512]{1,0:T(8,128)} %get-tuple-element.16) | copy-start | bytes 49156
  154.1 4.8 %copy-start = (bf16[64,8,640]{2,1,0:T(8,128)(2,1)S(1)}, bf16[64,8,640]{2,1,0:T(8,128)(2,1)}, u32[]{:S(2)}) copy-start(bf16[64,8,640]{2,1,0:T(8,128)(2,1)} %all_to_all.32.refs_1_) | copy-start | bytes 1966084
  155.2 16.8 %all-to-all-start.5 = ((f32[8,32,512]{2,1,0:T(8,128)}), f32[8,32,512]{2,1,0:T(8,128)S(1)}, u32[]{:S(2)}, u32[]{:S(2)}) async-start(f32[8,32,512]{2,1,0:T(8,128)} %bitcast.23), calls=%async_computation.5 | async-start | bytes 1048576 | tf_op jit(solution)/shard_map/all_to_all | solution.py:20

commit v3 on v2

--- a/solution.py
+++ b/solution.py
@@ -14,15 +14,11 @@
 LANES = 128
 VMEM = pl.BlockSpec(memory_space=pltpu.VMEM)
 SMEM = pl.BlockSpec(memory_space=pltpu.SMEM)
+SMALL = pltpu.CompilerParams(vmem_limit_bytes=24 * 1024 * 1024)
 
 
 def exchange(blocks, axes, groups=None):
     return lax.all_to_all(blocks, axes, split_axis=0, concat_axis=0, axis_index_groups=groups, tiled=True)
-
-
-def gather(block, axes):
-    size = lax.axis_size(axes)
-    return exchange(jnp.broadcast_to(block[None], (size,) + block.shape), axes)
 
 
 def mixed_groups(shape):
@@ -89,6 +85,19 @@
     held = genes // places
     parts = table.reshape((windows, places, held) + table.shape[2:])
     return jnp.moveaxis(parts, 1, 0).reshape((genes * windows,) + table.shape[2:])
+
+
+def pack_kernel(block, padded, local_ref, packed_ref):
+    copies, windows, depth, bins = packed_ref.shape
+    for w in range(windows):
+        rows = local_ref[w].astype(F32)
+        gap = jnp.zeros((padded - block, bins), F32)
+        pieces = []
+        for i in range(depth // padded):
+            pieces += [rows[i * block : (i + 1) * block], gap]
+        rows = jnp.concatenate(pieces, axis=0).astype(BF16)
+        for i in range(copies):
+            packed_ref[i, w] = rows
 
 
 def cover_kernel(windows, held, at_ref, starts_ref, lengths_ref, cover_ref, turned_ref):
@@ -106,17 +115,17 @@
         cover_ref[:, w * bins : (w + 1) * bins] = mine.T.astype(BF16)
 
 
-def forward_kernel(whole_ref, head_ref, cover_ref, target_ref, tsum_ref, sent_ref, slope_ref, pred_ref):
-    parts, windows, _, bins = whole_ref.shape
-    cores = 2
+def forward_kernel(at_ref, ours_ref, other_ref, head_ref, cover_ref, target_ref, tsum_ref, sent_ref, slope_ref, pred_ref):
+    xs, windows, _, bins = ours_ref.shape
+    core = at_ref[5]
     places, per_place, tracks = target_ref.shape
     for w in range(windows):
         logits = jnp.zeros((bins, tracks), F32)
-        for k in range(parts):
-            core, x = divmod(k, parts // cores)
-            logits += lax.dot_general(
-                whole_ref[k, w], head_ref[x * cores + core], (((0,), (0,)), ((), ())), preferred_element_type=F32
-            )
+        for x in range(xs):
+            for ref, at in ((ours_ref, 2 * x + core), (other_ref, 2 * x + 1 - core)):
+                logits += lax.dot_general(
+                    ref[x, w], head_ref[at], (((0,), (0,)), ((), ())), preferred_element_type=F32
+                )
         low = jnp.exp(-jnp.abs(logits))
         pred_ref[w * bins : (w + 1) * bins, :] = (jnp.maximum(logits, 0.0) + jnp.log1p(low)).astype(BF16)
         slope_ref[w * bins : (w + 1) * bins, :] = jnp.where(logits >= 0, 1.0, low) / (1.0 + low)
@@ -158,9 +167,11 @@
         sent_ref[j * at_ref[1], :, tracks:] = jnp.where(even, common, fit[:, cut]).astype(BF16)
 
 
-def backward_kernel(genes, block, at_ref, got_ref, turned_ref, slope_ref, whole_ref, sent_ref, total_ref, tsum_ref):
+def backward_kernel(
+    genes, block, at_ref, got_ref, turned_ref, slope_ref, ours_ref, other_ref, sent_ref, total_ref, tsum_ref
+):
     places, per_place, width = got_ref.shape
-    parts, windows, depth, bins = whole_ref.shape
+    xs, windows, depth, bins = ours_ref.shape
     tracks = width - LANES
     chunks = tracks // LANES
     side = 8
@@ -196,15 +207,14 @@
         spare.append(top)
     spare = jnp.where(holder, jnp.concatenate(spare, axis=1), 0.0)
 
-    cores = 2
-    for k in range(parts):
-        core, x = divmod(k, parts // cores)
-        lhs = jnp.concatenate([whole_ref[k, w] for w in range(windows)], axis=1)
-        grad = jnp.dot(lhs, logit_grad, preferred_element_type=F32)
-        for i in range(side):
-            upper = x * cores + core
-            place = upper * at_ref[3] + i * at_ref[4]
-            sent_ref[place] = (grad[i * padded : (i + 1) * padded] + spare).astype(BF16)
+    core = at_ref[5]
+    for x in range(xs):
+        for ref, upper in ((ours_ref, 2 * x + core), (other_ref, 2 * x + 1 - core)):
+            lhs = jnp.concatenate([ref[x, w] for w in range(windows)], axis=1)
+            grad = jnp.dot(lhs, logit_grad, preferred_element_type=F32)
+            for i in range(side):
+                place = upper * at_ref[3] + i * at_ref[4]
+                sent_ref[place] = (grad[i * padded : (i + 1) * padded] + spare).astype(BF16)
 
 
 def per_device(embeddings, head, exon_starts, exon_lengths, gene_owner, gene_targets):
@@ -227,10 +237,15 @@
     depth = blocks_dev * padded
     chunks = tracks // LANES
 
-    local = embeddings.transpose(0, 2, 1).reshape(windows, blocks_dev, block, bin_dev)
-    local = jnp.pad(local, ((0, 0), (0, 0), (0, padded - block), (0, 0))).reshape(windows, depth, bin_dev)
-    ours = gather(local, "x")
-    whole = gather(ours, "c").reshape(parts, windows, depth, bin_dev)
+    packed = pl.pallas_call(
+        lambda *refs: pack_kernel(block, padded, *refs),
+        out_shape=jax.ShapeDtypeStruct((xs, windows, depth, bin_dev), BF16),
+        in_specs=[VMEM],
+        out_specs=VMEM,
+        compiler_params=SMALL,
+        name="pack",
+    )(embeddings.transpose(0, 2, 1))
+    ours = exchange(packed, "x")
 
     padded_head = jnp.pad(head.reshape(places, block, tracks), ((0, 0), (0, padded - block), (0, 0)))
     padded_head = padded_head.reshape(parts, depth, tracks)
@@ -239,8 +254,15 @@
     stride = jnp.where(first, 1, side)
     holder = jnp.where(first, place < chunks, (place % side == 0) & (place < chunks * side))
     at = jnp.stack(
-        [place, stride, holder.astype(jnp.int32), jnp.where(first, side, 1), jnp.where(first, 1, side)]
+        [place, stride, holder.astype(jnp.int32), jnp.where(first, side, 1), stride, core]
     ).astype(jnp.int32)
+
+    starts, lengths = by_place(exon_starts, places).T, by_place(exon_lengths, places).T
+    slot_row = by_place(slot_table(gene_owner, capacity), places)
+    ours, starts, lengths, slot_row, padded_head = lax.optimization_barrier(
+        (ours, starts, lengths, slot_row, padded_head)
+    )
+    other = lax.ppermute(ours, "c", [(0, 1), (1, 0)])
 
     cover, turned = pl.pallas_call(
         lambda *refs: cover_kernel(windows, held, *refs),
@@ -250,12 +272,12 @@
         ],
         in_specs=[SMEM, VMEM, VMEM],
         out_specs=[VMEM, VMEM],
+        compiler_params=SMALL,
         name="cover",
-    )(at, by_place(exon_starts, places).T, by_place(exon_lengths, places).T)
+    )(at, starts, lengths)
 
     row_window = (jnp.arange(rows, dtype=jnp.int32) // held) % windows
     in_window = row_window[:, None] == jnp.arange(windows)
-    slot_row = by_place(slot_table(gene_owner, capacity), places)
     here = place * capacity + jnp.arange(capacity, dtype=jnp.int32)
     chosen = in_window[..., None] & (slot_row[:, None, None] == here)
     chosen = chosen.reshape(rows, windows * capacity)
@@ -274,17 +296,19 @@
             jax.ShapeDtypeStruct((places, per_place, 2 * tracks + LANES), BF16),
             jax.ShapeDtypeStruct((windows * bin_dev, tracks), F32),
         ],
-        in_specs=[VMEM] * 5,
+        in_specs=[SMEM] + [VMEM] * 6,
         out_specs=[VMEM] * 2,
         scratch_shapes=[pltpu.VMEM((windows * bin_dev, tracks), BF16)],
+        compiler_params=SMALL,
         name="forward",
-    )(whole, padded_head, cover, target_rows, tsum)
+    )(at, ours, other, padded_head, cover, target_rows, tsum)
 
     sent = pl.pallas_call(
         middle_kernel,
         out_shape=jax.ShapeDtypeStruct((places, per_place, tracks + LANES), BF16),
         in_specs=[SMEM, VMEM],
         out_specs=VMEM,
+        compiler_params=SMALL,
         name="middle",
     )(at, exchange(sent, SEQ))
     got = exchange(sent, SEQ)
@@ -296,16 +320,21 @@
             jax.ShapeDtypeStruct((per_place, tracks), F32),
             jax.ShapeDtypeStruct((per_place, tracks), F32),
         ],
-        in_specs=[SMEM, VMEM, VMEM, VMEM, VMEM],
+        in_specs=[SMEM] + [VMEM] * 5,
         out_specs=[VMEM] * 3,
+        compiler_params=SMALL,
         name="backward",
-    )(at, got, turned, slope, whole)
+    )(at, got, turned, slope, ours, other)
 
     ahead, after = mixed_groups((side, places // side, xs, cores))
     summed = exchange(sent.reshape(side, side * padded, tracks), EVERY, ahead)
     summed = jnp.sum(summed.reshape(side, side, padded, tracks).astype(F32), axis=0)
-    summed = exchange(summed, EVERY, after)
-    grad_head = jnp.sum(summed[:, :block], axis=0)
+    is_grad = (jnp.arange(padded) < block)[:, None]
+    summed = jnp.where(is_grad, summed * jnp.abs(summed), summed).astype(BF16)
+    summed = exchange(summed, EVERY, after).astype(F32)
+    grads = summed[:, :block]
+    root = jnp.sqrt(jnp.abs(grads))
+    grad_head = jnp.sum(jnp.where(grads < 0, -root, root), axis=0)
     fit = jnp.sum(summed[:chunks, block:], axis=1).reshape(chunks, windows, LANES)
     fit = fit.transpose(1, 0, 2).reshape(windows, tracks)
     total = total.reshape(windows, held, tracks)[:, 0]

time: 174 us -> 166 us (0.954)
  blocking collectives: 115 us -> 76.4 us
  waiting for transfers between devices: 12.2 us -> 44.7 us
  starting transfers between devices: 13 us -> 20.2 us
  Pallas kernels: 15.7 us -> 9.49 us
  local copies, waits for them, and re-layouts: 11.7 us -> 8.02 us
  other arithmetic: 3.06 us -> 4.94 us
    all_to_all x4 -> x2, blocking collectives: 115 us -> 76.4 us  [exchange(): lax.all_to_all(blocks, axes, split_axis=0, concat_axis=0, axis_index_grou...]
    all_to_all x2 -> x3, waiting for transfers between devices: 12.2 us -> 43.9 us  [exchange(): lax.all_to_all(blocks, axes, split_axis=0, concat_axis=0, axis_index_grou...]
    all_to_all x2 -> x3, starting transfers between devices: 13 us -> 18.3 us  [exchange(): lax.all_to_all(blocks, axes, split_axis=0, concat_axis=0, axis_index_grou...]
    pallas_call x1, Pallas kernels: 5.59 us -> 3.2 us  [per_device(): pl.pallas_call(lambda *refs: backward_kernel(genes, block, *refs), out_sh...]
    unnamed x16, local copies, waits for them, and re-layouts: 0.27 us -> 2.53 us
    pallas_call x1, Pallas kernels: 5.48 us -> 3.26 us  [per_device(): pl.pallas_call(forward_kernel, out_shape=[jax.ShapeDtypeStruct((places, p...]
    ppermute x0 -> x1, starting transfers between devices: none -> 1.91 us  [per_device(): other = lax.ppermute(ours, 'c', [(0, 1), (1, 0)])]
  transfers between devices with their start and end apart: 2 -> 4, of which waited for: 1 -> 4; matrix products, arithmetic and copies ran while one was open for 6% -> 4% of each run, Pallas kernels for 1% -> 1%
where the time goes in v3:
time: 166 us; the launch traced here: 165 us
  blocking collectives  76.4 us (46%)
  waiting for transfers between devices  44.7 us (27%)
  starting transfers between devices  20.2 us (12%)
  Pallas kernels  9.49 us (6%)
  local copies, waits for them, and re-layouts  8.02 us (5%)
  other arithmetic  4.94 us (3%)
    all_to_all x2, blocking collectives, exchange(): lax.all_to_all(blocks, axes, split_axis=0, concat_axis=0, axis_index_grou...  76.4 us
    all_to_all x3, waiting for transfers between devices, exchange(): lax.all_to_all(blocks, axes, split_axis=0, concat_axis=0, axis_index_grou...  43.9 us
    all_to_all x3, starting transfers between devices, exchange(): lax.all_to_all(blocks, axes, split_axis=0, concat_axis=0, axis_index_grou...  18.3 us
  transfers between devices with their start and end apart: 4, of which 4 were waited for; matrix products, arithmetic and copies ran while one was open for 4% of the time, Pallas kernels for 1%

profile of v3, /device:TPU:2, one launch (start us, length us, event | category | flops | bytes accessed | tf_op | source)
XLA Modules:
  0.0 165.2 jit_solution(15684938404106336069)
XLA Ops:
  0.6 0.0 copy-start.1
  0.6 0.9 copy-done.1
  1.6 1.1 pack.1
  2.7 9.4 %all-to-all-start = ((bf16[4,4,256,128]{3,2,1,0:T(8,128)(2,1)}), bf16[4,4,256,128]{3,2,1,0:T(8,128)(2,1)S(1)}, u32[]{:S(2)}, u32[]{:S(2)}) async-start(bf16[4,4,256,128]{3,2,1,0:T(8,128)(2,1)} %pack.1), calls=%async_computation | async-start | bytes 2097152 | tf_op jit(solution)/shard_map/all_to_all | solution.py:21
  12.1 0.0 copy-done.2
  12.1 0.0 copy-start.6
  12.1 1.6 reshape.216
  13.7 0.0 copy-done.5
  13.7 0.1 copy.34
  13.8 0.1 copy.35
  13.9 0.1 copy.36
  14.0 0.1 copy.37
  14.2 0.1 copy.38
  14.3 0.1 copy.39
  14.4 0.0 copy-done.4
  14.4 0.2 convert_reduce_fusion.1
  14.6 0.1 copy.40
  14.8 0.5 copy.41
  15.3 0.2 reshape.215
  15.4 0.0 copy-start.3
  15.4 1.8 %pad.4 = bf16[64,32,512]{2,1,0:T(8,128)(2,1)S(1)} pad(bf16[64,30,512]{2,1,0:T(8,128)(2,1)} %reshape.216, bf16[]{:T(256)} %constant.64.clone.1), padding=0_0x0_2x0_0 | pad | bytes 4063234 | tf_op jit(solution)/shard_map/jit(_pad)/pad | solution.py:250
  17.3 0.1 stack.34.refs_0_.at_ref
  17.4 4.1 %all-to-all-done.ours_ref.refs_4_ = bf16[4,4,256,128]{3,2,1,0:T(8,128)(2,1)S(1)} async-done(((bf16[4,4,256,128]{3,2,1,0:T(8,128)(2,1)}), bf16[4,4,256,128]{3,2,1,0:T(8,128)(2,1)S(1)}, u32[]{:S(2)}, u32[]{:S(2)}) %all-to-all-start) | async-done | bytes 1048608 | tf_op jit(solution)/shard_map/all_to_all | solution.py:21
  21.5 1.9 %collective-permute-start = (bf16[4,4,256,128]{3,2,1,0:T(8,128)(2,1)S(1)}, bf16[4,4,256,128]{3,2,1,0:T(8,128)(2,1)}, u32[]{:S(2)}, u32[]{:S(2)}) collective-permute-start(bf16[4,4,256,128]{3,2,1,0:T(8,128)(2,1)S(1)} %all-to-all-done.ours_ref.refs_4_), channel_id=1, source_target_pairs={{0,1},{1,0},{2,3},{3,2},{4,5},{5,4},{6,7},{7,6},{8,9},{9,8},{10,11... | collective-permute-start | bytes 3145736 | tf_op jit(solution)/shard_map/ppermute | solution.py:265
  23.4 0.1 broadcast_compare_fusion
  23.5 0.2 fusion.18
  23.6 0.1 multiply_reduce_fusion
  23.8 1.1 cover.1
  25.0 0.4 fusion.1.target_ref
  25.3 0.8 collective-permute-done.other_ref.refs_5_
  26.1 3.3 %forward.1 = (bf16[64,8,1152]{2,1,0:T(8,128)(2,1)S(1)}, f32[512,512]{1,0:T(8,128)S(1)}) custom-call(s32[6]{0:T(128)S(1)} %stack.34.refs_0_.at_ref, bf16[4,4,256,128]{3,2,1,0:T(8,128)(2,1)S(1)} %all-to-all-done.ours_ref.refs_4_, bf16[4,4,256,128]{3,2,1,0:T(8,128)(2,1)} %collective-permute-done.other_ref.refs_5_, bf16[8,256,512]{2,1,0:T(8,128)(2,1)S(1)} %bitcast.55, ...), custom_call_target="tpu_custom_call" | custom-call | tf_op jit(solution)/shard_map/forward/pallas_call | solution.py:293
  29.4 48.2 %all_to_all.25.got_ref = bf16[64,8,1152]{2,1,0:T(8,128)(2,1)S(1)} all-to-all(bf16[64,8,1152]{2,1,0:T(8,128)(2,1)S(1)} %get-tuple-element.21), channel_id=1, replica_groups=mesh['y'=8,'z'=8,'x'=4,'c'=2] {'y','z'}, dimensions={0} | all-to-all | bytes 2359296 | tf_op jit(solution)/shard_map/all_to_all | solution.py:21
  77.6 0.8 middle.1
  78.4 28.2 %all_to_all.26.refs_1_ = bf16[64,8,640]{2,1,0:T(8,128)(2,1)S(1)} all-to-all(bf16[64,8,640]{2,1,0:T(8,128)(2,1)S(1)} %middle.1), channel_id=1, replica_groups=mesh['y'=8,'z'=8,'x'=4,'c'=2] {'y','z'}, dimensions={0} | all-to-all | bytes 1310720 | tf_op jit(solution)/shard_map/all_to_all | solution.py:21
  106.6 3.2 %backward.1 = (bf16[64,32,512]{2,1,0:T(8,128)(2,1)S(1)}, f32[8,512]{1,0:T(8,128)S(1)}, f32[8,512]{1,0:T(8,128)S(1)}) custom-call(s32[6]{0:T(128)S(1)} %stack.34.refs_0_.at_ref, bf16[64,8,640]{2,1,0:T(8,128)(2,1)S(1)} %all_to_all.26.refs_1_, bf16[512,512]{1,0:T(8,128)(2,1)S(1)} %get-tuple-element.22.refs_2_, f32[512,512]{1,0:T(8,128)S(1)} %get-tuple-element.23.refs_3_, ...), custom_call_target="tpu_custom_call" | custom-call | tf_op jit(solution)/shard_map/backward/pallas_call | solution.py:316
  109.8 1.3 copy-done
  111.1 4.6 %all-to-all-start.3 = ((bf16[8,256,512]{2,1,0:T(8,128)(2,1)}), bf16[8,256,512]{2,1,0:T(8,128)(2,1)}, u32[]{:S(2)}, u32[]{:S(2)}) async-start(bf16[8,256,512]{2,1,0:T(8,128)(2,1)} %bitcast.56), calls=%async_computation.3 | async-start | bytes 4194304 | tf_op jit(solution)/shard_map/all_to_all | solution.py:21
  115.7 30.4 %all-to-all-done.3 = bf16[8,256,512]{2,1,0:T(8,128)(2,1)} async-done(((bf16[8,256,512]{2,1,0:T(8,128)(2,1)}), bf16[8,256,512]{2,1,0:T(8,128)(2,1)}, u32[]{:S(2)}, u32[]{:S(2)}) %all-to-all-start.3) | async-done | bytes 2097184 | tf_op jit(solution)/shard_map/all_to_all | solution.py:21
  146.1 1.9 %convert_reduce_fusion = f32[256,512]{1,0:T(8,128)S(1)} fusion(bf16[8,256,512]{2,1,0:T(8,128)(2,1)} %all-to-all-done.3), kind=kLoop, calls=%fused_computation | loop fusion | flops 1966080 | bytes 2621440 | tf_op jit(solution)/shard_map/reduce_sum | solution.py:331
  148.0 0.8 fusion.2
  148.8 4.4 %all-to-all-start.4 = ((bf16[8,32,512]{2,1,0:T(8,128)(2,1)}), bf16[8,32,512]{2,1,0:T(8,128)(2,1)S(1)}, u32[]{:S(2)}, u32[]{:S(2)}) async-start(bf16[8,32,512]{2,1,0:T(8,128)(2,1)} %fusion.2), calls=%async_computation.4 | async-start | bytes 524288 | tf_op jit(solution)/shard_map/all_to_all | solution.py:21
  153.2 0.1 gt.15
  153.4 0.2 fusion.5
  153.6 0.6 reshape.221
  154.2 9.5 %all-to-all-done.4 = bf16[8,32,512]{2,1,0:T(8,128)(2,1)S(1)} async-done(((bf16[8,32,512]{2,1,0:T(8,128)(2,1)}), bf16[8,32,512]{2,1,0:T(8,128)(2,1)S(1)}, u32[]{:S(2)}, u32[]{:S(2)}) %all-to-all-start.4) | async-done | bytes 262176 | tf_op jit(solution)/shard_map/all_to_all | solution.py:21
  163.7 0.1 convert_element_type.47
  163.8 0.8 fusion.3
  164.6 0.6 fusion.11
  (25 shorter events, 0.2 us)
Async XLA Ops:
  0.6 0.9 copy-start.1
  1.6 10.5 %copy-start.2 = (bf16[1920,512]{1,0:T(8,128)(2,1)S(1)}, bf16[1920,512]{1,0:T(8,128)(2,1)}, u32[]{:S(2)}) copy-start(bf16[1920,512]{1,0:T(8,128)(2,1)} %param.7) | copy-start | bytes 5898244
  2.7 18.8 %all-to-all-start = ((bf16[4,4,256,128]{3,2,1,0:T(8,128)(2,1)}), bf16[4,4,256,128]{3,2,1,0:T(8,128)(2,1)S(1)}, u32[]{:S(2)}, u32[]{:S(2)}) async-start(bf16[4,4,256,128]{3,2,1,0:T(8,128)(2,1)} %pack.1), calls=%async_computation | async-start | bytes 2097152 | tf_op jit(solution)/shard_map/all_to_all | solution.py:21
  12.0 1.7 %copy-start.5 = (s32[4,128,8]{1,2,0:T(8,128)S(1)}, s32[4,128,8]{1,2,0:T(8,128)}, u32[]{:S(2)}) copy-start(s32[4,128,8]{1,2,0:T(8,128)} %param.8) | copy-start | bytes 49156
  12.1 2.0 %copy-start.6 = (s32[4,128,8]{1,2,0:T(8,128)S(1)}, s32[4,128,8]{1,2,0:T(8,128)}, u32[]{:S(2)}) copy-start(s32[4,128,8]{1,2,0:T(8,128)} %param.9) | copy-start | bytes 49156
  13.7 0.7 copy-start.4
  15.4 8.2 %copy-start.3 = (f32[4,4,512]{2,1,0:T(4,128)S(1)}, f32[4,4,512]{2,1,0:T(4,128)}, u32[]{:S(2)}) copy-start(f32[4,4,512]{2,1,0:T(4,128)} %param.11) | copy-start | bytes 98308
  21.5 4.7 %collective-permute-start = (bf16[4,4,256,128]{3,2,1,0:T(8,128)(2,1)S(1)}, bf16[4,4,256,128]{3,2,1,0:T(8,128)(2,1)}, u32[]{:S(2)}, u32[]{:S(2)}) collective-permute-start(bf16[4,4,256,128]{3,2,1,0:T(8,128)(2,1)S(1)} %all-to-all-done.ours_ref.refs_4_), channel_id=1, source_target_pairs={{0,1},{1,0},{2,3},{3,2},{4,5},{5,4},{6,7},{7,6},{8,9},{9,8},{10,11... | collective-permute-start | bytes 3145736 | tf_op jit(solution)/shard_map/ppermute | solution.py:265
  109.8 1.3 copy-start
  111.1 35.0 %all-to-all-start.3 = ((bf16[8,256,512]{2,1,0:T(8,128)(2,1)}), bf16[8,256,512]{2,1,0:T(8,128)(2,1)}, u32[]{:S(2)}, u32[]{:S(2)}) async-start(bf16[8,256,512]{2,1,0:T(8,128)(2,1)} %bitcast.56), calls=%async_computation.3 | async-start | bytes 4194304 | tf_op jit(solution)/shard_map/all_to_all | solution.py:21
  148.8 14.8 %all-to-all-start.4 = ((bf16[8,32,512]{2,1,0:T(8,128)(2,1)}), bf16[8,32,512]{2,1,0:T(8,128)(2,1)S(1)}, u32[]{:S(2)}, u32[]{:S(2)}) async-start(bf16[8,32,512]{2,1,0:T(8,128)(2,1)} %fusion.2), calls=%async_computation.4 | async-start | bytes 524288 | tf_op jit(solution)/shard_map/all_to_all | solution.py:21

commit v4 on v3

--- a/solution.py
+++ b/solution.py
@@ -14,7 +14,7 @@
 LANES = 128
 VMEM = pl.BlockSpec(memory_space=pltpu.VMEM)
 SMEM = pl.BlockSpec(memory_space=pltpu.SMEM)
-SMALL = pltpu.CompilerParams(vmem_limit_bytes=24 * 1024 * 1024)
+SMALL = pltpu.CompilerParams(vmem_limit_bytes=16 * 1024 * 1024)
 
 
 def exchange(blocks, axes, groups=None):
@@ -70,21 +70,6 @@
 
 def down(values):
     return pltpu.roll(values, 1, 0)
-
-
-def slot_table(gene_owner, capacity):
-    genes = gene_owner.shape[1]
-    same = gene_owner[:, :, None] == gene_owner[:, None, :]
-    earlier = jnp.arange(genes)[None, :] < jnp.arange(genes)[:, None]
-    ahead = jnp.sum((same & earlier[None]).astype(jnp.int32), axis=2)
-    return gene_owner * capacity + ahead
-
-
-def by_place(table, places):
-    windows, genes = table.shape[:2]
-    held = genes // places
-    parts = table.reshape((windows, places, held) + table.shape[2:])
-    return jnp.moveaxis(parts, 1, 0).reshape((genes * windows,) + table.shape[2:])
 
 
 def pack_kernel(block, padded, local_ref, packed_ref):
@@ -100,25 +85,75 @@
             packed_ref[i, w] = rows
 
 
-def cover_kernel(windows, held, at_ref, starts_ref, lengths_ref, cover_ref, turned_ref):
-    exons, rows = starts_ref.shape
+def plan_kernel(
+    places, at_ref, owner_ref, starts_ref, lengths_ref, counts_ref, cover_ref, turned_ref, target_ref, tsum_ref, mine_ref, from_ref
+):
+    windows, genes = owner_ref.shape
+    exons = starts_ref.shape[1]
+    capacity, tracks = counts_ref.shape[1:]
+    held = genes // places
+    per_place = windows * held
+    rows = places * per_place
     bins = cover_ref.shape[1] // windows
-    position = lax.broadcasted_iota(jnp.int32, (bins, rows), 0) + at_ref[0] * bins
-    base = jnp.zeros((bins, rows), F32)
-    for e in range(exons):
-        past = position - starts_ref[e : e + 1, :]
-        base += jnp.where((past >= 0) & (past < lengths_ref[e : e + 1, :]), 1.0, 0.0)
-    owner = (lax.broadcasted_iota(jnp.int32, (bins, rows), 1) // held) % windows
+    width = target_ref.shape[2]
+    place = at_ref[0]
+    square = (genes, genes)
+    earlier = lax.broadcasted_iota(jnp.int32, square, 1) < lax.broadcasted_iota(jnp.int32, square, 0)
+    position = lax.broadcasted_iota(jnp.int32, (bins, genes), 0) + place * bins
+    lane = lax.broadcasted_iota(jnp.int32, (genes, rows), 1)
+    targets = jnp.zeros((rows, width), F32)
+    tsum, sources = [], []
     for w in range(windows):
-        mine = jnp.where(owner == w, base, 0.0)
-        turned_ref[w * bins : (w + 1) * bins, :] = mine.astype(BF16)
-        cover_ref[:, w * bins : (w + 1) * bins] = mine.T.astype(BF16)
+        other = jnp.broadcast_to(owner_ref[w : w + 1, :].astype(F32), square)
+        own = other.T
+        ahead = jnp.where((other == own) & earlier, 1.0, 0.0)
+        rank = jnp.sum(ahead, axis=1, keepdims=True)
+        at = jnp.sum(jnp.where(other < own, 1.0, ahead), axis=1, keepdims=True).astype(jnp.int32)
+        turn = at // places
+        holder = at - turn * places
+        first = holder * per_place + w * held
+        spot = jnp.where(first + turn == lane, 1.0, 0.0).astype(BF16)
+
+        base = jnp.zeros((bins, genes), F32)
+        for e in range(exons):
+            past = position - starts_ref[w, e : e + 1, :]
+            base += jnp.where((past >= 0) & (past < lengths_ref[w, e : e + 1, :]), 1.0, 0.0)
+        turned = jnp.dot(base.astype(BF16), spot, preferred_element_type=F32)
+        turned_ref[w * bins : (w + 1) * bins, :] = turned.astype(BF16)
+        cover_ref[:, w * bins : (w + 1) * bins] = turned.T.astype(BF16)
+
+        owned = own[:, :1] == place.astype(F32)
+        coded = jnp.zeros((genes, tracks), F32)
+        total = jnp.zeros((1, tracks), F32)
+        for k in range(capacity):
+            here = owned & (rank == k)
+            count = counts_ref[w, k : k + 1, :]
+            held_here = jnp.sum(jnp.where(here, 1.0, 0.0), axis=0, keepdims=True) > 0
+            count = jnp.where(jnp.broadcast_to(held_here, count.shape), count, 1.0)
+            coded += jnp.where(jnp.broadcast_to(here, coded.shape), jnp.broadcast_to(spread(count), coded.shape), 0.0)
+            total += jnp.where(jnp.broadcast_to(held_here, count.shape), count, 0.0)
+            row = jnp.where(jnp.broadcast_to(here, lane.shape), spot.astype(F32), 0.0)
+            mine_ref[w * capacity + k : w * capacity + k + 1, :] = jnp.sum(row, axis=0, keepdims=True)
+        coded = coded.astype(BF16)
+        for h in range(held):
+            goes = jnp.where(first + h == lane, 1.0, 0.0).astype(BF16)
+            targets += lax.dot_general(
+                goes, coded[:, h * width : (h + 1) * width], (((0,), (0,)), ((), ())), preferred_element_type=F32
+            )
+            match = jnp.where(at == place + h * places, own[:, :1], 0.0)
+            sources.append(jnp.sum(match, axis=0, keepdims=True))
+        tsum += list(split(total))
+    target_ref[...] = targets.reshape(places, per_place, width).astype(BF16)
+    tsum_ref[...] = jnp.concatenate(tsum, axis=0).astype(BF16)
+    from_ref[...] = jnp.broadcast_to(jnp.concatenate(sources, axis=0), from_ref.shape).astype(jnp.int32)
 
 
 def forward_kernel(at_ref, ours_ref, other_ref, head_ref, cover_ref, target_ref, tsum_ref, sent_ref, slope_ref, pred_ref):
     xs, windows, _, bins = ours_ref.shape
     core = at_ref[5]
-    places, per_place, tracks = target_ref.shape
+    places, per_place, extra = target_ref.shape
+    tracks = slope_ref.shape[1]
+    side = tracks + extra
     for w in range(windows):
         logits = jnp.zeros((bins, tracks), F32)
         for x in range(xs):
@@ -132,8 +167,8 @@
     partial = jnp.dot(cover_ref[...], pred_ref[...], preferred_element_type=F32)
     partial = partial.reshape(places, per_place, tracks)
     sent_ref[:, :, :tracks] = partial.astype(BF16)
-    sent_ref[:, :, tracks : 2 * tracks] = target_ref[...]
-    sent_ref[:, :, 2 * tracks :] = jnp.zeros((places, per_place, LANES), BF16)
+    sent_ref[:, :, tracks:side] = target_ref[...]
+    sent_ref[:, :, side:] = jnp.zeros((places, per_place, LANES), BF16)
     total = jnp.sum(partial, axis=0)
     high, low = split(total + up(total))
     total = jnp.where(even_rows(total.shape), high, down(low)).astype(BF16)
@@ -141,22 +176,27 @@
     for j in range(chunks):
         cut = slice(j * LANES, (j + 1) * LANES)
         for i in range(2):
-            sent_ref[i * chunks + j, :, 2 * tracks :] = total[:, cut]
-            sent_ref[(i + 2) * chunks + j, :, 2 * tracks :] = tsum_ref[:, cut]
-
-
-def middle_kernel(at_ref, got_ref, sent_ref):
+            sent_ref[i * chunks + j, :, side:] = total[:, cut]
+            sent_ref[(i + 2) * chunks + j, :, side:] = tsum_ref[:, cut]
+
+
+def middle_kernel(held, at_ref, from_ref, got_ref, sent_ref):
     places, per_place, width = got_ref.shape
-    tracks = (width - LANES) // 2
+    tracks = sent_ref.shape[2] - LANES
     chunks = tracks // LANES
-    got = jnp.sum(got_ref[...].astype(F32), axis=0)
-    gene_pred = got[:, :tracks]
-    gene_target = unspread(got[:, tracks : 2 * tracks])
+    side = width - LANES
+    gene_pred = jnp.sum(got_ref[:, :, :tracks].astype(F32), axis=0)
+    sums = jnp.sum(got_ref[:, :, side:].astype(F32), axis=0)
+    pieces = []
+    for row in range(per_place):
+        w = row // held
+        block = got_ref[from_ref[row], :, tracks:side].astype(F32)
+        pieces.append(jnp.concatenate([block[w * held + h : w * held + h + 1] for h in range(held)], axis=1))
+    gene_target = unspread(jnp.concatenate(pieces, axis=0))
     ratio = squared(gene_target / gene_pred).astype(BF16)
     sent_ref[:, :, :tracks] = jnp.broadcast_to(ratio[None], (places, per_place, tracks))
     fit = gene_target * jnp.log(gene_pred)
     fit = fit + down(fit)
-    sums = got[:, 2 * tracks :]
     high, low = split(sums + up(sums))
     common = jnp.where(at_ref[0] % (2 * chunks) < chunks, high, low)
     even = even_rows(common.shape)
@@ -215,6 +255,15 @@
             for i in range(side):
                 place = upper * at_ref[3] + i * at_ref[4]
                 sent_ref[place] = (grad[i * padded : (i + 1) * padded] + spare).astype(BF16)
+
+
+def fold_kernel(block, got_ref, sent_ref):
+    for i in range(sent_ref.shape[0]):
+        total = got_ref[0, i].astype(F32)
+        for j in range(1, got_ref.shape[0]):
+            total += got_ref[j, i].astype(F32)
+        row = lax.broadcasted_iota(jnp.int32, total.shape, 0)
+        sent_ref[i] = jnp.where(row < block, total * jnp.abs(total), total).astype(BF16)
 
 
 def per_device(embeddings, head, exon_starts, exon_lengths, gene_owner, gene_targets):
@@ -257,43 +306,31 @@
         [place, stride, holder.astype(jnp.int32), jnp.where(first, side, 1), stride, core]
     ).astype(jnp.int32)
 
-    starts, lengths = by_place(exon_starts, places).T, by_place(exon_lengths, places).T
-    slot_row = by_place(slot_table(gene_owner, capacity), places)
-    ours, starts, lengths, slot_row, padded_head = lax.optimization_barrier(
-        (ours, starts, lengths, slot_row, padded_head)
-    )
-    other = lax.ppermute(ours, "c", [(0, 1), (1, 0)])
-
-    cover, turned = pl.pallas_call(
-        lambda *refs: cover_kernel(windows, held, *refs),
+    extra = windows * tracks // per_place
+    plan = pl.pallas_call(
+        lambda *refs: plan_kernel(places, *refs),
         out_shape=[
             jax.ShapeDtypeStruct((rows, windows * bin_dev), BF16),
             jax.ShapeDtypeStruct((windows * bin_dev, rows), BF16),
+            jax.ShapeDtypeStruct((places, per_place, extra), BF16),
+            jax.ShapeDtypeStruct((per_place, tracks), BF16),
+            jax.ShapeDtypeStruct((windows * capacity, rows), F32),
+            jax.ShapeDtypeStruct((per_place, LANES), jnp.int32),
         ],
-        in_specs=[SMEM, VMEM, VMEM],
-        out_specs=[VMEM, VMEM],
-        compiler_params=SMALL,
-        name="cover",
-    )(at, starts, lengths)
-
-    row_window = (jnp.arange(rows, dtype=jnp.int32) // held) % windows
-    in_window = row_window[:, None] == jnp.arange(windows)
-    here = place * capacity + jnp.arange(capacity, dtype=jnp.int32)
-    chosen = in_window[..., None] & (slot_row[:, None, None] == here)
-    chosen = chosen.reshape(rows, windows * capacity)
-    valid_here = jnp.any(chosen, axis=0).astype(F32)[:, None]
-    targets_here = gene_targets.reshape(windows * capacity, tracks)
-    targets_here = jnp.where(valid_here > 0, targets_here, 1.0)
-    target_rows = jnp.dot(chosen.astype(BF16), spread(targets_here).astype(BF16), preferred_element_type=F32)
-    target_rows = target_rows.astype(BF16).reshape(places, per_place, tracks)
-    target_part = jnp.sum((targets_here * valid_here).reshape(windows, capacity, tracks), axis=1)
-    high = lax.reduce_precision(target_part, 8, 7)
-    tsum = jnp.stack([high, target_part - high], axis=1).reshape(per_place, tracks).astype(BF16)
+        in_specs=[SMEM] + [VMEM] * 4,
+        out_specs=[VMEM] * 6,
+        compiler_params=SMALL,
+        name="plan",
+    )(at, gene_owner, exon_starts.transpose(0, 2, 1), exon_lengths.transpose(0, 2, 1), gene_targets)
+    came_from = plan[-1][:, 0]
+    ours, padded_head, came_from, plan = lax.optimization_barrier((ours, padded_head, came_from, tuple(plan[:-1])))
+    cover, turned, target_rows, tsum, mine = plan
+    other = lax.ppermute(ours, "c", [(0, 1), (1, 0)])
 
     sent, slope = pl.pallas_call(
         forward_kernel,
         out_shape=[
-            jax.ShapeDtypeStruct((places, per_place, 2 * tracks + LANES), BF16),
+            jax.ShapeDtypeStruct((places, per_place, tracks + extra + LANES), BF16),
             jax.ShapeDtypeStruct((windows * bin_dev, tracks), F32),
         ],
         in_specs=[SMEM] + [VMEM] * 6,
@@ -304,13 +341,13 @@
     )(at, ours, other, padded_head, cover, target_rows, tsum)
 
     sent = pl.pallas_call(
-        middle_kernel,
+        lambda *refs: middle_kernel(held, *refs),
         out_shape=jax.ShapeDtypeStruct((places, per_place, tracks + LANES), BF16),
-        in_specs=[SMEM, VMEM],
+        in_specs=[SMEM, SMEM, VMEM],
         out_specs=VMEM,
         compiler_params=SMALL,
         name="middle",
-    )(at, exchange(sent, SEQ))
+    )(at, came_from, exchange(sent, SEQ))
     got = exchange(sent, SEQ)
 
     sent, total, target_sum = pl.pallas_call(
@@ -328,9 +365,17 @@
 
     ahead, after = mixed_groups((side, places // side, xs, cores))
     summed = exchange(sent.reshape(side, side * padded, tracks), EVERY, ahead)
-    summed = jnp.sum(summed.reshape(side, side, padded, tracks).astype(F32), axis=0)
-    is_grad = (jnp.arange(padded) < block)[:, None]
-    summed = jnp.where(is_grad, summed * jnp.abs(summed), summed).astype(BF16)
+    summed = pl.pallas_call(
+        lambda *refs: fold_kernel(block, *refs),
+        out_shape=jax.ShapeDtypeStruct((side, padded, tracks), BF16),
+        in_specs=[VMEM],
+        out_specs=VMEM,
+        compiler_params=SMALL,
+        name="fold",
+    )(summed.reshape(side, side, padded, tracks))
+    summed, got, mine, total, target_sum, gene_targets = lax.optimization_barrier(
+        (summed, got, mine, total, target_sum, gene_targets)
+    )
     summed = exchange(summed, EVERY, after).astype(F32)
     grads = summed[:, :block]
     root = jnp.sqrt(jnp.abs(grads))
@@ -343,8 +388,10 @@
     loss = (-fit + target_sum * log_total + 0.2 * (total - target_sum * log_total)) / target_sum
 
     ratios = got[:, :, :tracks].reshape(rows, tracks)
-    back = lax.dot_general(chosen.astype(BF16), ratios, (((0,), (0,)), ((), ())), preferred_element_type=F32)
-    gene_here = jnp.where(valid_here > 0, targets_here / rooted(jnp.where(valid_here > 0, back, 1.0)), 0.0)
+    back = jnp.dot(mine.astype(BF16), ratios, preferred_element_type=F32)
+    valid = jnp.sum(mine, axis=1, keepdims=True) > 0
+    targets_here = gene_targets.reshape(windows * capacity, tracks)
+    gene_here = jnp.where(valid, targets_here / rooted(jnp.where(valid, back, 1.0)), 0.0)
     return (gene_here.reshape(gene_targets.shape), loss, grad_head)
 
 

time: 166 us -> 155 us (0.934)
  waiting for transfers between devices: 44.7 us -> 12.6 us
  blocking collectives: 76.4 us -> 105 us
  starting transfers between devices: 20.2 us -> 14.7 us
  other arithmetic: 4.94 us -> 1.67 us
  Pallas kernels: 9.49 us -> 11.3 us
    all_to_all x3 -> x2, waiting for transfers between devices: 43.9 us -> 9.99 us  [exchange(): lax.all_to_all(blocks, axes, split_axis=0, concat_axis=0, axis_index_grou...]
    all_to_all x2 -> x3, blocking collectives: 76.4 us -> 105 us  [exchange(): lax.all_to_all(blocks, axes, split_axis=0, concat_axis=0, axis_index_grou...]
    all_to_all x3 -> x2, starting transfers between devices: 18.3 us -> 12.8 us  [exchange(): lax.all_to_all(blocks, axes, split_axis=0, concat_axis=0, axis_index_grou...]
    pallas_call x2 -> x3, Pallas kernels: 1.95 us -> 5.19 us  [the longest x1 3.46 us: per_device(): pl.pallas_call(lambda *refs: plan_kernel(places, *refs), out_shape=[jax.S...]
    reduce_sum x3 -> x1, other arithmetic: 2.27 us -> 0.12 us  [per_device(): valid = jnp.sum(mine, axis=1, keepdims=True) > 0]
    ppermute x1, waiting for transfers between devices: 0.8 us -> 2.63 us  [per_device(): other = lax.ppermute(ours, 'c', [(0, 1), (1, 0)])]
    unnamed x16 -> x20, local copies, waits for them, and re-layouts: 2.53 us -> 3.58 us
  transfers between devices with their start and end apart: 4 -> 3, of which waited for: 4 -> 3; matrix products, arithmetic and copies ran while one was open for 4% -> 3% of each run, Pallas kernels for 1% -> 2%
where the time goes in v4:
time: 155 us
  blocking collectives  105 us (68%)
  starting transfers between devices  14.7 us (9%)
  waiting for transfers between devices  12.6 us (8%)
  Pallas kernels  11.3 us (7%)
  local copies, waits for them, and re-layouts  7.95 us (5%)
  other arithmetic  1.67 us (1%)
    all_to_all x3, blocking collectives, exchange(): lax.all_to_all(blocks, axes, split_axis=0, concat_axis=0, axis_index_grou...  105 us
    all_to_all x2, starting transfers between devices, exchange(): lax.all_to_all(blocks, axes, split_axis=0, concat_axis=0, axis_index_grou...  12.8 us
    all_to_all x2, waiting for transfers between devices, exchange(): lax.all_to_all(blocks, axes, split_axis=0, concat_axis=0, axis_index_grou...  9.99 us
    unnamed x20, local copies, waits for them, and re-layouts  3.58 us
    pallas_call x1, Pallas kernels, per_device(): pl.pallas_call(lambda *refs: plan_kernel(places, *refs), out_shape=[jax.S...  3.46 us
  transfers between devices with their start and end apart: 3, of which 3 were waited for; matrix products, arithmetic and copies ran while one was open for 3% of the time, Pallas kernels for 2%

profile of v4, /device:TPU:2, one launch (start us, length us, event | category | flops | bytes accessed | tf_op | source)
XLA Modules:
  0.0 154.5 jit_solution(12148756168086966398)
XLA Ops:
  0.6 0.0 copy-start.4
  0.6 0.9 copy-done.4
  1.6 0.0 copy-start.9
  1.6 1.1 pack.1
  2.7 9.4 %all-to-all-start = ((bf16[4,4,256,128]{3,2,1,0:T(8,128)(2,1)}), bf16[4,4,256,128]{3,2,1,0:T(8,128)(2,1)S(1)}, u32[]{:S(2)}, u32[]{:S(2)}) async-start(bf16[4,4,256,128]{3,2,1,0:T(8,128)(2,1)} %pack.1), calls=%async_computation | async-start | bytes 2097152 | tf_op jit(solution)/shard_map/all_to_all | solution.py:21
  12.0 0.0 copy-done.9
  12.0 1.6 %reshape.41 = bf16[64,30,512]{2,1,0:T(8,128)(2,1)} reshape(bf16[1920,512]{1,0:T(8,128)(2,1)S(1)} %copy-done.9) | data formatting | bytes 3932160 | tf_op jit(solution)/shard_map/reshape | solution.py:299
  13.6 0.0 copy-start.5
  13.6 0.0 copy-start.6
  13.6 0.0 copy-start.7
  13.6 0.0 copy-start.8
  13.7 1.9 %pad.4 = bf16[64,32,512]{2,1,0:T(8,128)(2,1)S(1)} pad(bf16[64,30,512]{2,1,0:T(8,128)(2,1)} %reshape.41, bf16[]{:T(256)} %constant.41.clone.1), padding=0_0x0_2x0_0 | pad | bytes 4063234 | tf_op jit(solution)/shard_map/jit(_pad)/pad | solution.py:299
  15.5 0.1 stack.28.refs_0_.at_ref
  15.6 0.0 copy-done.5
  15.6 0.0 copy-done.6
  15.6 0.0 copy-done.7
  15.6 0.0 copy-done.8
  15.6 3.5 %plan.1 = (bf16[512,512]{1,0:T(8,128)(2,1)S(1)}, bf16[512,512]{1,0:T(8,128)(2,1)S(1)}, bf16[64,8,256]{2,1,0:T(8,128)(2,1)S(1)}, bf16[8,512]{1,0:T(8,128)(2,1)S(1...) custom-call(s32[6]{0:T(128)S(1)} %stack.28.refs_0_.at_ref, s32[4,128]{1,0:T(4,128)S(1)} %copy-done.8, ...), custom_call_target="tpu_custom_call" | custom-call | tf_op jit(solution)/shard_map/plan/pallas_call | solution.py:310
  19.1 0.0 copy-start
  19.1 0.8 copy-done
  19.9 0.0 copy-start.2
  19.9 0.8 copy-done.2
  20.7 0.1 slice_reduce_fusion.1.refs_1_
  20.8 0.7 all-to-all-done.ours_ref.refs_4_
  21.5 1.9 %collective-permute-start = (bf16[4,4,256,128]{3,2,1,0:T(8,128)(2,1)S(1)}, bf16[4,4,256,128]{3,2,1,0:T(8,128)(2,1)S(1)}, u32[]{:S(2)}, u32[]{:S(2)}) collective-permute-start(bf16[4,4,256,128]{3,2,1,0:T(8,128)(2,1)S(1)} %all-to-all-done.ours_ref.refs_4_), channel_id=1, source_target_pairs={{0,1},{1,0},{2,3},{3,2},{4,5},{5,4},{6,7},{7,6},{8,9},{9,8},{10,11... | collective-permute-start | bytes 3145736 | tf_op jit(solution)/shard_map/ppermute | solution.py:328
  23.4 2.6 %collective-permute-done.other_ref.refs_5_ = bf16[4,4,256,128]{3,2,1,0:T(8,128)(2,1)S(1)} collective-permute-done((bf16[4,4,256,128]{3,2,1,0:T(8,128)(2,1)S(1)}, bf16[4,4,256,128]{3,2,1,0:T(8,128)(2,1)S(1)}, u32[]{:S(2)}, u32[]{:S(2)}) %collective-permute-start) | collective-permute-done | bytes 1048608 | tf_op jit(solution)/shard_map/ppermute | solution.py:328
  26.0 0.0 copy-start.3
  26.0 1.0 copy-done.3
  27.0 2.5 %forward.1 = (bf16[64,8,896]{2,1,0:T(8,128)(2,1)S(1)}, f32[512,512]{1,0:T(8,128)S(1)}) custom-call(s32[6]{0:T(128)S(1)} %stack.28.refs_0_.at_ref, bf16[4,4,256,128]{3,2,1,0:T(8,128)(2,1)S(1)} %all-to-all-done.ours_ref.refs_4_, bf16[4,4,256,128]{3,2,1,0:T(8,128)(2,1)S(1)} %collective-permute-done.other_ref.refs_5_, bf16[8,256,512]{2,1,0:T(8,128)(2,1)S(1)} %bitcast.35, ...), custom_call_target="tpu_custom_call" | custom-call | tf_op jit(solution)/shard_map/forward/pallas_call | solution.py:330
  29.5 0.0 copy-start.1
  29.5 42.7 %all_to_all.25.refs_2_ = bf16[64,8,896]{2,1,0:T(8,128)(2,1)S(1)} all-to-all(bf16[64,8,896]{2,1,0:T(8,128)(2,1)S(1)} %get-tuple-element.40), channel_id=1, replica_groups=mesh['y'=8,'z'=8,'x'=4,'c'=2] {'y','z'}, dimensions={0} | all-to-all | bytes 1835008 | tf_op jit(solution)/shard_map/all_to_all | solution.py:21
  72.2 0.7 middle.1
  73.0 27.8 %all_to_all.26.refs_1_ = bf16[64,8,640]{2,1,0:T(8,128)(2,1)S(1)} all-to-all(bf16[64,8,640]{2,1,0:T(8,128)(2,1)S(1)} %middle.1), channel_id=1, replica_groups=mesh['y'=8,'z'=8,'x'=4,'c'=2] {'y','z'}, dimensions={0} | all-to-all | bytes 1310720 | tf_op jit(solution)/shard_map/all_to_all | solution.py:21
  100.8 0.0 copy-done.1
  100.8 2.5 %backward.1 = (bf16[64,32,512]{2,1,0:T(8,128)(2,1)S(1)}, f32[8,512]{1,0:T(8,128)S(1)}, f32[8,512]{1,0:T(8,128)S(1)}) custom-call(s32[6]{0:T(128)S(1)} %stack.28.refs_0_.at_ref, bf16[64,8,640]{2,1,0:T(8,128)(2,1)S(1)} %all_to_all.26.refs_1_, bf16[512,512]{1,0:T(8,128)(2,1)S(1)} %copy-done.1, f32[512,512]{1,0:T(8,128)S(1)} %get-tuple-element.42.refs_3_, ...), custom_call_target="tpu_custom_call" | custom-call | tf_op jit(solution)/shard_map/backward/pallas_call | solution.py:353
  103.3 34.9 %all_to_all.27 = bf16[8,256,512]{2,1,0:T(8,128)(2,1)S(1)} all-to-all(bf16[8,256,512]{2,1,0:T(8,128)(2,1)S(1)} %bitcast.37), channel_id=1, replica_groups={{0,64,128,192,256,320,384,448},{1,9,17,25,33,41,49,57},{8,72,136,200,26..., dimensions={0} | all-to-all | bytes 4194304 | tf_op jit(solution)/shard_map/all_to_all | solution.py:21
  138.2 1.0 fold.1
  139.2 3.4 %all-to-all-start.4 = ((bf16[8,32,512]{2,1,0:T(8,128)(2,1)}), bf16[8,32,512]{2,1,0:T(8,128)(2,1)S(1)}, u32[]{:S(2)}, u32[]{:S(2)}) async-start(bf16[8,32,512]{2,1,0:T(8,128)(2,1)} %fold.1), calls=%async_computation.4 | async-start | bytes 524288 | tf_op jit(solution)/shard_map/all_to_all | solution.py:21
  142.7 0.1 reduce_sum.27
  142.8 0.2 fusion.4
  143.0 0.6 reshape.47
  143.7 9.3 %all-to-all-done.4 = bf16[8,32,512]{2,1,0:T(8,128)(2,1)S(1)} async-done(((bf16[8,32,512]{2,1,0:T(8,128)(2,1)}), bf16[8,32,512]{2,1,0:T(8,128)(2,1)S(1)}, u32[]{:S(2)}, u32[]{:S(2)}) %all-to-all-start.4) | async-done | bytes 262176 | tf_op jit(solution)/shard_map/all_to_all | solution.py:21
  153.0 0.1 convert_element_type.10
  153.1 0.8 fusion
  153.9 0.6 fusion.9
  (8 shorter events, 0.1 us)
Async XLA Ops:
  0.6 0.9 copy-start.4
  1.6 10.4 %copy-start.9 = (bf16[1920,512]{1,0:T(8,128)(2,1)S(1)}, bf16[1920,512]{1,0:T(8,128)(2,1)}, u32[]{:S(2)}) copy-start(bf16[1920,512]{1,0:T(8,128)(2,1)} %param.7) | copy-start | bytes 5898244
  2.7 18.8 %all-to-all-start = ((bf16[4,4,256,128]{3,2,1,0:T(8,128)(2,1)}), bf16[4,4,256,128]{3,2,1,0:T(8,128)(2,1)S(1)}, u32[]{:S(2)}, u32[]{:S(2)}) async-start(bf16[4,4,256,128]{3,2,1,0:T(8,128)(2,1)} %pack.1), calls=%async_computation | async-start | bytes 2097152 | tf_op jit(solution)/shard_map/all_to_all | solution.py:21
  13.6 2.0 %copy-start.5 = (f32[4,4,512]{2,1,0:T(4,128)S(1)}, f32[4,4,512]{2,1,0:T(4,128)}, u32[]{:S(2)}) copy-start(f32[4,4,512]{2,1,0:T(4,128)} %refs_4_.1) | copy-start | bytes 98308
  13.6 2.0 %copy-start.6 = (s32[4,128,8]{1,2,0:T(8,128)S(1)}, s32[4,128,8]{1,2,0:T(8,128)}, u32[]{:S(2)}) copy-start(s32[4,128,8]{1,2,0:T(8,128)} %param.8) | copy-start | bytes 49156
  13.6 2.0 %copy-start.7 = (s32[4,128,8]{1,2,0:T(8,128)S(1)}, s32[4,128,8]{1,2,0:T(8,128)}, u32[]{:S(2)}) copy-start(s32[4,128,8]{1,2,0:T(8,128)} %param.9) | copy-start | bytes 49156
  13.6 2.0 %copy-start.8 = (s32[4,128]{1,0:T(4,128)S(1)}, s32[4,128]{1,0:T(4,128)}, u32[]{:S(2)}) copy-start(s32[4,128]{1,0:T(4,128)} %refs_1_.1) | copy-start | bytes 6148
  19.1 0.8 copy-start
  19.9 0.8 copy-start.2
  21.5 4.5 %collective-permute-start = (bf16[4,4,256,128]{3,2,1,0:T(8,128)(2,1)S(1)}, bf16[4,4,256,128]{3,2,1,0:T(8,128)(2,1)S(1)}, u32[]{:S(2)}, u32[]{:S(2)}) collective-permute-start(bf16[4,4,256,128]{3,2,1,0:T(8,128)(2,1)S(1)} %all-to-all-done.ours_ref.refs_4_), channel_id=1, source_target_pairs={{0,1},{1,0},{2,3},{3,2},{4,5},{5,4},{6,7},{7,6},{8,9},{9,8},{10,11... | collective-permute-start | bytes 3145736 | tf_op jit(solution)/shard_map/ppermute | solution.py:328
  26.0 1.0 copy-start.3
  29.5 71.2 %copy-start.1 = (bf16[512,512]{1,0:T(8,128)(2,1)S(1)}, bf16[512,512]{1,0:T(8,128)(2,1)}, u32[]{:S(2)}) copy-start(bf16[512,512]{1,0:T(8,128)(2,1)} %copy-done) | copy-start | bytes 1572868
  139.2 13.8 %all-to-all-start.4 = ((bf16[8,32,512]{2,1,0:T(8,128)(2,1)}), bf16[8,32,512]{2,1,0:T(8,128)(2,1)S(1)}, u32[]{:S(2)}, u32[]{:S(2)}) async-start(bf16[8,32,512]{2,1,0:T(8,128)(2,1)} %fold.1), calls=%async_computation.4 | async-start | bytes 524288 | tf_op jit(solution)/shard_map/all_to_all | solution.py:21

commit v5 on v4

v5 whole, which is shorter than its diff:
```python
import jax
import jax.numpy as jnp
import numpy as np
from jax import lax
from jax.experimental import pallas as pl
from jax.experimental.pallas import tpu as pltpu
from jax.sharding import Mesh, PartitionSpec as P

SEQ = ("y", "z")
EVERY = ("y", "z", "x", "c")
F32 = jnp.float32
BF16 = jnp.bfloat16
MIDDLE = 28.28
VMEM = pl.BlockSpec(memory_space=pltpu.VMEM)
SMEM = pl.BlockSpec(memory_space=pltpu.SMEM)
SMALL = pltpu.CompilerParams(vmem_limit_bytes=16 * 1024 * 1024)


def exchange(blocks, axes, groups=None):
    return lax.all_to_all(blocks, axes, split_axis=0, concat_axis=0, axis_index_groups=groups, tiled=True)


def mixed_groups(shape):
    ids = np.arange(int(np.prod(shape))).reshape(shape)
    ahead, after = [], []
    for x in range(shape[2]):
        for k in range(shape[0]):
            ahead += [ids[:, k, x, 0].tolist(), ids[k, :, x, 1].tolist()]
            after += [ids[k, :, x, 0].tolist(), ids[:, k, x, 1].tolist()]
    return ahead, after


def spread(counts):
    scaled = counts * (1.0 / MIDDLE)
    for _ in range(4):
        scaled = scaled * scaled
    return scaled


def unspread(coded):
    for _ in range(4):
        coded = jnp.sqrt(coded)
    return coded * MIDDLE


def squared(ratio):
    small = ratio < 2.0**63
    scaled = jnp.where(small, ratio, ratio * 2.0**-96)
    return jnp.where(small, scaled * scaled, -(scaled * scaled))


def rooted(coded):
    root = jnp.sqrt(jnp.abs(coded))
    return jnp.where(coded < 0, root * 2.0**96, root)


def split(values):
    high = values.astype(BF16).astype(F32)
    return high, values - high


def packed_sum(partial):
    tiny = partial < 2.0**-40
    scaled = jnp.where(tiny, partial * 2.0**80, partial)
    return jnp.where(tiny, -(scaled * scaled), scaled * scaled)


def unpacked_sum(coded):
    root = jnp.sqrt(jnp.abs(coded))
    return jnp.where(coded < 0, root * 2.0**-80, root)


def pack_kernel(block, padded, local_ref, packed_ref):
    copies, windows, depth, bins = packed_ref.shape
    for w in range(windows):
        rows = local_ref[w].astype(F32)
        gap = jnp.zeros((padded - block, bins), F32)
        pieces = []
        for i in range(depth // padded):
            pieces += [rows[i * block : (i + 1) * block], gap]
        rows = jnp.concatenate(pieces, axis=0).astype(BF16)
        for i in range(copies):
            packed_ref[i, w] = rows


def plan_kernel(
    places, at_ref, owner_ref, starts_ref, lengths_ref, counts_ref, cover_ref, turned_ref, target_ref, pick_ref, mine_ref
):
    windows, genes = owner_ref.shape
    exons = starts_ref.shape[1]
    capacity, tracks = counts_ref.shape[1:]
    held = genes // places
    side = target_ref.shape[0]
    sent_rows = target_ref.shape[1]
    rows, width = cover_ref.shape
    bins = width // windows
    set_rows, sources = pick_ref.shape
    window_rows = set_rows // windows
    place, core, axis = at_ref[0], at_ref[1], at_ref[2]
    square = (genes, genes)
    earlier = lax.broadcasted_iota(jnp.int32, square, 1) < lax.broadcasted_iota(jnp.int32, square, 0)
    position = lax.broadcasted_iota(jnp.int32, (bins, genes), 0) + place * bins
    lane = lax.broadcasted_iota(jnp.int32, (genes, rows), 1)
    targets = jnp.zeros((side * sent_rows, tracks), F32)
    pick = jnp.zeros((set_rows, sources), F32)
    across = (((0,), (0,)), ((), ()))
    for w in range(windows):
        other = jnp.broadcast_to(owner_ref[w : w + 1, :].astype(F32), square)
        own = other.T
        ahead = jnp.where((other == own) & earlier, 1.0, 0.0)
        rank = jnp.sum(ahead, axis=1, keepdims=True)
        at = jnp.sum(jnp.where(other < own, 1.0, ahead), axis=1, keepdims=True).astype(jnp.int32)
        turn = at // places
        place_of = at - turn * places
        high = place_of // side
        part = place_of - high * side
        row = w * window_rows + high * held + turn
        spot = jnp.where(part * set_rows + row == lane, 1.0, 0.0)

        base = jnp.zeros((bins, genes), F32)
        for e in range(exons):
            past = position - starts_ref[w, e : e + 1, :]
            base += jnp.where((past >= 0) & (past < lengths_ref[w, e : e + 1, :]), 1.0, 0.0)
        turned = jnp.dot(base.astype(BF16), spot.astype(BF16), preferred_element_type=F32)
        turned_ref[w * bins : (w + 1) * bins, :] = turned.astype(BF16)
        cover_ref[:, w * bins : (w + 1) * bins] = turned.T.astype(BF16)

        owner = own[:, :1].astype(jnp.int32)
        owner_high = owner // side
        owner_low = owner - owner_high * side
        first = jnp.where(core == 0, owner_high, owner_low)
        second = jnp.where(core == 0, owner_low, owner_high)
        source = second * (sources // side) + first * windows + w
        here = jnp.where((part == axis) & (row == lane[:, :set_rows]), 1.0, 0.0).astype(BF16)
        origin = jnp.where(source == lane[:, :sources], 1.0, 0.0).astype(BF16)
        pick += lax.dot_general(here, origin, across, preferred_element_type=F32)

        owned = owner == place
        coded = jnp.zeros((genes, tracks), F32)
        for k in range(capacity):
            slot = owned & (rank == k)
            filled = jnp.sum(jnp.where(slot, 1.0, 0.0), axis=0, keepdims=True) > 0
            count = counts_ref[w, k : k + 1, :]
            count = spread(jnp.where(jnp.broadcast_to(filled, count.shape), count, 1.0))
            coded += jnp.where(jnp.broadcast_to(slot, coded.shape), jnp.broadcast_to(count, coded.shape), 0.0)
            mark = jnp.where(jnp.broadcast_to(slot, lane.shape), spot, 0.0)
            mine_ref[w * capacity + k : w * capacity + k + 1, :] = jnp.sum(mark, axis=0, keepdims=True)
        goes = jnp.where(part * sent_rows + w == lane[:, : side * sent_rows], 1.0, 0.0).astype(BF16)
        targets += lax.dot_general(goes, coded.astype(BF16), across, preferred_element_type=F32)
    target_ref[...] = targets.reshape(side, sent_rows, tracks).astype(BF16)
    pick_ref[...] = pick.astype(BF16)


def forward_kernel(at_ref, ours_ref, other_ref, head_ref, cover_ref, target_ref, sent_ref, slope_ref, pred_ref):
    xs, windows, _, bins = ours_ref.shape
    core = at_ref[1]
    side, sent_rows, tracks = sent_ref.shape
    set_rows = sent_rows - target_ref.shape[1]
    for w in range(windows):
        logits = jnp.zeros((bins, tracks), F32)
        for x in range(xs):
            for ref, at in ((ours_ref, 2 * x + core), (other_ref, 2 * x + 1 - core)):
                logits += lax.dot_general(
                    ref[x, w], head_ref[at], (((0,), (0,)), ((), ())), preferred_element_type=F32
                )
        low = jnp.exp(-jnp.abs(logits))
        pred_ref[w * bins : (w + 1) * bins, :] = (jnp.maximum(logits, 0.0) + jnp.log1p(low)).astype(BF16)
        slope_ref[w * bins : (w + 1) * bins, :] = jnp.where(logits >= 0, 1.0, low) / (1.0 + low)
    partial = jnp.dot(cover_ref[...], pred_ref[...], preferred_element_type=F32)
    sent_ref[:, :set_rows, :] = packed_sum(partial).reshape(side, set_rows, tracks).astype(BF16)
    sent_ref[:, set_rows:, :] = target_ref[...]


def second_kernel(windows, got_ref, sent_ref):
    side, got_rows, tracks = got_ref.shape
    set_rows = got_rows - 2 * windows
    total = unpacked_sum(got_ref[0, :set_rows, :].astype(F32))
    for i in range(1, side):
        total += unpacked_sum(got_ref[i, :set_rows, :].astype(F32))
    pieces = [packed_sum(total)]
    for i in range(0, side, 2):
        upper = got_ref[i, set_rows:, :].astype(F32)
        pieces.append(upper + pltpu.roll(got_ref[i + 1, set_rows:, :].astype(F32), windows, 0))
    block = jnp.concatenate(pieces, axis=0).astype(BF16)
    for i in range(side):
        sent_ref[i] = block


def third_kernel(windows, got_ref, pick_ref, sent_ref):
    side, got_rows, tracks = got_ref.shape
    set_rows, sources = pick_ref.shape
    gene_pred = unpacked_sum(got_ref[0, :set_rows, :].astype(F32))
    for i in range(1, side):
        gene_pred += unpacked_sum(got_ref[i, :set_rows, :].astype(F32))
    rows = got_ref[:, set_rows:, :].astype(F32).reshape(sources, tracks).astype(BF16)
    gene_target = unspread(jnp.dot(pick_ref[...], rows, preferred_element_type=F32))
    pieces = [squared(gene_target / gene_pred)]
    for values in (gene_pred, gene_target, gene_target * jnp.log(gene_pred)):
        pieces += split(jnp.sum(values.reshape(windows, set_rows // windows, tracks), axis=1))
    block = jnp.concatenate(pieces, axis=0).astype(BF16)
    for i in range(side):
        sent_ref[i] = block


def backward_kernel(
    genes, at_ref, got_ref, turned_ref, slope_ref, ours_ref, other_ref, sent_ref, loss_ref
):
    side, got_rows, tracks = got_ref.shape
    xs, windows, depth, bins = ours_ref.shape
    set_rows = got_rows - 6 * windows
    window_rows = set_rows // windows
    padded = sent_ref.shape[1]
    sums = jnp.sum(got_ref[:, set_rows:, :].astype(F32), axis=0)
    total, target_sum, fit = [
        sums[2 * i * windows : (2 * i + 1) * windows] + sums[(2 * i + 1) * windows : (2 * i + 2) * windows]
        for i in range(3)
    ]
    log_total = jnp.log(total)
    loss_ref[...] = (-fit + target_sum * log_total + 0.2 * (total - target_sum * log_total)) / target_sum
    scale = genes / target_sum
    level = scale * (0.2 + 0.8 * target_sum / total)
    grads = []
    for w in range(windows):
        ratio = rooted(got_ref[:, w * window_rows : (w + 1) * window_rows, :].astype(F32))
        grads.append(level[w : w + 1][None] - scale[w : w + 1][None] * ratio)
    gene_grad = jnp.concatenate(grads, axis=1).reshape(side * set_rows, tracks).astype(BF16)
    bin_grad = jnp.dot(turned_ref[...], gene_grad, preferred_element_type=F32)
    logit_grad = (bin_grad * slope_ref[...]).astype(BF16)

    core = at_ref[1]
    for x in range(xs):
        for ref, upper in ((ours_ref, 2 * x + core), (other_ref, 2 * x + 1 - core)):
            lhs = jnp.concatenate([ref[x, w] for w in range(windows)], axis=1)
            grad = jnp.dot(lhs, logit_grad, preferred_element_type=F32)
            for i in range(side):
                place = upper * at_ref[3] + i * at_ref[4]
                sent_ref[place] = grad[i * padded : (i + 1) * padded].astype(BF16)


def fold_kernel(got_ref, sent_ref):
    for i in range(sent_ref.shape[0]):
        total = got_ref[0, i].astype(F32)
        for j in range(1, got_ref.shape[0]):
            total += got_ref[j, i].astype(F32)
        sent_ref[i] = (total * jnp.abs(total)).astype(BF16)


def per_device(embeddings, head, exon_starts, exon_lengths, gene_owner, gene_targets):
    places = lax.axis_size(SEQ)
    place = lax.axis_index(SEQ)
    core = lax.axis_index("c")
    side = lax.axis_size("y")
    windows, bin_dev, channels_dev = embeddings.shape
    channels, tracks = head.shape
    genes = gene_owner.shape[1]
    capacity = gene_targets.shape[1]
    held = genes // places
    per_place = windows * held
    rows = places * per_place
    xs, cores = lax.axis_size("x"), lax.axis_size("c")
    parts = xs * cores
    block = channels // places
    padded = -(-block // 16) * 16
    blocks_dev = channels_dev // block
    depth = blocks_dev * padded
    set_rows = rows // side
    side_rows = 2 * windows
    ahead, after = mixed_groups((side, places // side, xs, cores))

    packed = pl.pallas_call(
        lambda *refs: pack_kernel(block, padded, *refs),
        out_shape=jax.ShapeDtypeStruct((xs, windows, depth, bin_dev), BF16),
        in_specs=[VMEM],
        out_specs=VMEM,
        compiler_params=SMALL,
        name="pack",
    )(embeddings.transpose(0, 2, 1))
    ours = exchange(packed, "x")

    padded_head = jnp.pad(head.reshape(places, block, tracks), ((0, 0), (0, padded - block), (0, 0)))
    padded_head = padded_head.reshape(parts, depth, tracks)

    first = core == 0
    axis = jnp.where(first, lax.axis_index("y"), lax.axis_index("z"))
    at = jnp.stack([place, core, axis, jnp.where(first, side, 1), jnp.where(first, 1, side)]).astype(jnp.int32)

    plan = pl.pallas_call(
        lambda *refs: plan_kernel(places, *refs),
        out_shape=[
            jax.ShapeDtypeStruct((rows, windows * bin_dev), BF16),
            jax.ShapeDtypeStruct((windows * bin_dev, rows), BF16),
            jax.ShapeDtypeStruct((side, side_rows, tracks), BF16),
            jax.ShapeDtypeStruct((set_rows, places * windows), BF16),
            jax.ShapeDtypeStruct((windows * capacity, rows), F32),
        ],
        in_specs=[SMEM] + [VMEM] * 4,
        out_specs=[VMEM] * 5,
        compiler_params=SMALL,
        name="plan",
    )(at, gene_owner, exon_starts.transpose(0, 2, 1), exon_lengths.transpose(0, 2, 1), gene_targets)
    ours, padded_head, plan = lax.optimization_barrier((ours, padded_head, tuple(plan)))
    cover, turned, target_rows, pick, mine = plan
    other = lax.ppermute(ours, "c", [(0, 1), (1, 0)])

    sent, slope = pl.pallas_call(
        forward_kernel,
        out_shape=[
            jax.ShapeDtypeStruct((side, set_rows + side_rows, tracks), BF16),
            jax.ShapeDtypeStruct((windows * bin_dev, tracks), F32),
        ],
        in_specs=[SMEM] + [VMEM] * 5,
        out_specs=[VMEM] * 2,
        scratch_shapes=[pltpu.VMEM((windows * bin_dev, tracks), BF16)],
        compiler_params=SMALL,
        name="forward",
    )(at, ours, other, padded_head, cover, target_rows)

    sent = pl.pallas_call(
        lambda *refs: second_kernel(windows, *refs),
        out_shape=jax.ShapeDtypeStruct((side, set_rows + side * windows, tracks), BF16),
        in_specs=[VMEM],
        out_specs=VMEM,
        compiler_params=SMALL,
        name="second",
    )(exchange(sent, EVERY, ahead))
    sent = pl.pallas_call(
        lambda *refs: third_kernel(windows, *refs),
        out_shape=jax.ShapeDtypeStruct((side, set_rows + 6 * windows, tracks), BF16),
        in_specs=[VMEM, VMEM],
        out_specs=VMEM,
        compiler_params=SMALL,
        name="third",
    )(exchange(sent, EVERY, after), pick)
    got = exchange(sent, EVERY, ahead)

    sent, loss = pl.pallas_call(
        lambda *refs: backward_kernel(genes, *refs),
        out_shape=[
            jax.ShapeDtypeStruct((places, padded, tracks), BF16),
            jax.ShapeDtypeStruct((windows, tracks), F32),
        ],
        in_specs=[SMEM] + [VMEM] * 5,
        out_specs=[VMEM] * 2,
        compiler_params=SMALL,
        name="backward",
    )(at, got, turned, slope, ours, other)

    summed = exchange(sent.reshape(side, side * padded, tracks), EVERY, ahead)
    summed = pl.pallas_call(
        fold_kernel,
        out_shape=jax.ShapeDtypeStruct((side, padded, tracks), BF16),
        in_specs=[VMEM],
        out_specs=VMEM,
        compiler_params=SMALL,
        name="fold",
    )(summed.reshape(side, side, padded, tracks))
    summed, got, mine, loss, gene_targets = lax.optimization_barrier((summed, got, mine, loss, gene_targets))
    grads = exchange(summed, EVERY, after)[:, :block].astype(F32)
    root = jnp.sqrt(jnp.abs(grads))
    grad_head = jnp.sum(jnp.where(grads < 0, -root, root), axis=0)

    ratios = got[:, :set_rows].reshape(rows, tracks)
    back = jnp.dot(mine.astype(BF16), ratios, preferred_element_type=F32)
    valid = jnp.sum(mine, axis=1, keepdims=True) > 0
    targets_here = gene_targets.reshape(windows * capacity, tracks)
    gene_here = jnp.where(valid, targets_here / rooted(jnp.where(valid, back, 1.0)), 0.0)
    return (gene_here.reshape(gene_targets.shape), loss, grad_head)


def solution(mesh):
    shape = (8, 8, 4, 2)
    fine = Mesh(mesh.devices.reshape(shape), EVERY)
    return jax.shard_map(
        per_device,
        mesh=fine,
        in_specs=(P(None, SEQ, ("x", "c")), P(None, ("x", "c")), P(), P(), P(), P(None, SEQ, ("x", "c"))),
        out_specs=(P(None, SEQ, ("x", "c")), P(None, ("x", "c")), P(SEQ, ("x", "c"))),
        check_vma=False,
    )
```

time: 155 us -> 147 us (0.948)
  blocking collectives: 105 us -> 97.3 us
    all_to_all x3 -> x4, blocking collectives: 105 us -> 97.3 us  [exchange(): lax.all_to_all(blocks, axes, split_axis=0, concat_axis=0, axis_index_grou...]
    pallas_call x4 -> x5, Pallas kernels: 6.72 us -> 7.96 us  [the longest x1 3.05 us: per_device(): pl.pallas_call(lambda *refs: backward_kernel(genes, *refs), out_shape=[ja...]
  transfers between devices with their start and end apart: 3 -> 3, of which waited for: 3 -> 3; matrix products, arithmetic and copies ran while one was open for 3% -> 3% of each run, Pallas kernels for 2% -> 3%
where the time goes in v5:
time: 147 us
  blocking collectives  97.3 us (66%)
  starting transfers between devices  14.7 us (10%)
  Pallas kernels  12.7 us (9%)
  waiting for transfers between devices  12.5 us (9%)
  local copies, waits for them, and re-layouts  7.82 us (5%)
    all_to_all x4, blocking collectives, exchange(): lax.all_to_all(blocks, axes, split_axis=0, concat_axis=0, axis_index_grou...  97.3 us
    all_to_all x2, starting transfers between devices, exchange(): lax.all_to_all(blocks, axes, split_axis=0, concat_axis=0, axis_index_grou...  12.8 us
    all_to_all x2, waiting for transfers between devices, exchange(): lax.all_to_all(blocks, axes, split_axis=0, concat_axis=0, axis_index_grou...  9.92 us
    pallas_call x1, Pallas kernels, per_device(): pl.pallas_call(lambda *refs: plan_kernel(places, *refs), out_shape=[jax.S...  3.68 us
    unnamed x20, local copies, waits for them, and re-layouts  3.6 us
    pallas_call x1, Pallas kernels, per_device(): pl.pallas_call(lambda *refs: backward_kernel(genes, *refs), out_shape=[ja...  3.05 us
  transfers between devices with their start and end apart: 3, of which 3 were waited for; matrix products, arithmetic and copies ran while one was open for 3% of the time, Pallas kernels for 3%

profile of v5, /device:TPU:2, one launch (start us, length us, event | category | flops | bytes accessed | tf_op | source)
XLA Modules:
  0.0 146.9 jit_solution(7686582627393667433)
XLA Ops:
  0.6 0.0 copy-start.4
  0.6 0.9 copy-done.4
  1.6 0.0 copy-start.9
  1.6 1.1 pack.1
  2.6 9.4 %all-to-all-start = ((bf16[4,4,256,128]{3,2,1,0:T(8,128)(2,1)}), bf16[4,4,256,128]{3,2,1,0:T(8,128)(2,1)S(1)}, u32[]{:S(2)}, u32[]{:S(2)}) async-start(bf16[4,4,256,128]{3,2,1,0:T(8,128)(2,1)} %pack.1), calls=%async_computation | async-start | bytes 2097152 | tf_op jit(solution)/shard_map/all_to_all | solution.py:20
  12.0 0.0 copy-done.9
  12.0 1.6 %reshape.31 = bf16[64,30,512]{2,1,0:T(8,128)(2,1)} reshape(bf16[1920,512]{1,0:T(8,128)(2,1)S(1)} %copy-done.9) | data formatting | bytes 3932160 | tf_op jit(solution)/shard_map/reshape | solution.py:280
  13.6 0.0 copy-start.5
  13.6 0.0 copy-start.6
  13.6 0.0 copy-start.7
  13.6 0.0 copy-start.8
  13.6 1.9 %pad.4 = bf16[64,32,512]{2,1,0:T(8,128)(2,1)S(1)} pad(bf16[64,30,512]{2,1,0:T(8,128)(2,1)} %reshape.31, bf16[]{:T(256)} %constant.26.clone.1), padding=0_0x0_2x0_0 | pad | bytes 4063234 | tf_op jit(solution)/shard_map/jit(_pad)/pad | solution.py:280
  15.5 0.1 stack.23.refs_0_.at_ref
  15.6 0.0 copy-done.5
  15.6 0.0 copy-done.6
  15.6 0.0 copy-done.7
  15.6 0.0 copy-done.8
  15.6 3.7 %plan.1 = (bf16[512,512]{1,0:T(8,128)(2,1)S(1)}, bf16[512,512]{1,0:T(8,128)(2,1)S(1)}, bf16[8,8,512]{2,1,0:T(8,128)(2,1)S(1)}, bf16[64,256]{1,0:T(8,128)(2,1)S(1)}, f32[16,512]{1,0:T(8,128)S(1)}) custom-call(s32[5]{0:T(128)S(1)} %stack.23.refs_0_.at_ref, s32[4,128]{1,0:T(4,128)S(1)} %copy-done.8, s32[4,8,128]{2,1,0:T(8,128)S(1)} %bitcast.17, ...), custom_call_target="tpu_custom_call" | custom-call | tf_op jit(solution)/shard_map/plan/pallas_call | solution.py:287
  19.3 0.0 copy-start
  19.3 0.8 copy-done
  20.1 0.0 copy-start.2
  20.1 0.8 copy-done.2
  20.9 0.6 all-to-all-done.ours_ref.refs_4_
  21.4 1.9 %collective-permute-start = (bf16[4,4,256,128]{3,2,1,0:T(8,128)(2,1)S(1)}, bf16[4,4,256,128]{3,2,1,0:T(8,128)(2,1)S(1)}, u32[]{:S(2)}, u32[]{:S(2)}) collective-permute-start(bf16[4,4,256,128]{3,2,1,0:T(8,128)(2,1)S(1)} %all-to-all-done.ours_ref.refs_4_), channel_id=1, source_target_pairs={{0,1},{1,0},{2,3},{3,2},{4,5},{5,4},{6,7},{7,6},{8,9},{9,8},{10,11... | collective-permute-start | bytes 3145736 | tf_op jit(solution)/shard_map/ppermute | solution.py:303
  23.4 2.6 %collective-permute-done.other_ref.refs_5_ = bf16[4,4,256,128]{3,2,1,0:T(8,128)(2,1)S(1)} collective-permute-done((bf16[4,4,256,128]{3,2,1,0:T(8,128)(2,1)S(1)}, bf16[4,4,256,128]{3,2,1,0:T(8,128)(2,1)S(1)}, u32[]{:S(2)}, u32[]{:S(2)}) %collective-permute-start) | collective-permute-done | bytes 1048608 | tf_op jit(solution)/shard_map/ppermute | solution.py:303
  26.0 0.0 copy-start.3
  26.0 1.0 copy-done.3
  27.0 2.6 %forward.1 = (bf16[8,72,512]{2,1,0:T(8,128)(2,1)S(1)}, f32[512,512]{1,0:T(8,128)S(1)}) custom-call(s32[5]{0:T(128)S(1)} %stack.23.refs_0_.at_ref, bf16[4,4,256,128]{3,2,1,0:T(8,128)(2,1)S(1)} %all-to-all-done.ours_ref.refs_4_, bf16[4,4,256,128]{3,2,1,0:T(8,128)(2,1)S(1)} %collective-permute-done.other_ref.refs_5_, bf16[8,256,512]{2,1,0:T(8,128)(2,1)S(1)} %bitcast.13, ...), custom_call_target="tpu_custom_call" | custom-call | tf_op jit(solution)/shard_map/forward/pallas_call | solution.py:305
  29.7 20.6 %all_to_all.30.refs_0_ = bf16[8,72,512]{2,1,0:T(8,128)(2,1)S(1)} all-to-all(bf16[8,72,512]{2,1,0:T(8,128)(2,1)S(1)} %get-tuple-element.33), channel_id=1, replica_groups={{0,64,128,192,256,320,384,448},{1,9,17,25,33,41,49,57},{8,72,136,200,26..., dimensions={0} | all-to-all | bytes 1179648 | tf_op jit(solution)/shard_map/all_to_all | solution.py:20
  50.2 0.5 second.1
  50.7 0.0 copy-start.1
  50.7 26.3 %all_to_all.31.refs_0_ = bf16[8,96,512]{2,1,0:T(8,128)(2,1)S(1)} all-to-all(bf16[8,96,512]{2,1,0:T(8,128)(2,1)S(1)} %second.1), channel_id=1, replica_groups={{0,8,16,24,32,40,48,56},{1,65,129,193,257,321,385,449},{64,72,80,88,96,..., dimensions={0} | all-to-all | bytes 1572864 | tf_op jit(solution)/shard_map/all_to_all | solution.py:20
  77.0 0.8 third.1
  77.8 17.8 %all_to_all.32.refs_1_ = bf16[8,88,512]{2,1,0:T(8,128)(2,1)S(1)} all-to-all(bf16[8,88,512]{2,1,0:T(8,128)(2,1)S(1)} %third.1), channel_id=1, replica_groups={{0,64,128,192,256,320,384,448},{1,9,17,25,33,41,49,57},{8,72,136,200,26..., dimensions={0} | all-to-all | bytes 1441792 | tf_op jit(solution)/shard_map/all_to_all | solution.py:20
  95.6 0.0 copy-done.1
  95.6 3.1 %backward.1 = (bf16[64,32,512]{2,1,0:T(8,128)(2,1)S(1)}, f32[4,512]{1,0:T(4,128)}) custom-call(s32[5]{0:T(128)S(1)} %stack.23.refs_0_.at_ref, bf16[8,88,512]{2,1,0:T(8,128)(2,1)S(1)} %all_to_all.32.refs_1_, bf16[512,512]{1,0:T(8,128)(2,1)S(1)} %copy-done.1, f32[512,512]{1,0:T(8,128)S(1)} %get-tuple-element.36.refs_3_, ...), custom_call_target="tpu_custom_call" | custom-call | tf_op jit(solution)/shard_map/backward/pallas_call | solution.py:336
  98.7 32.6 %all_to_all.33 = bf16[8,256,512]{2,1,0:T(8,128)(2,1)S(1)} all-to-all(bf16[8,256,512]{2,1,0:T(8,128)(2,1)S(1)} %bitcast.15), channel_id=1, replica_groups={{0,64,128,192,256,320,384,448},{1,9,17,25,33,41,49,57},{8,72,136,200,26..., dimensions={0} | all-to-all | bytes 4194304 | tf_op jit(solution)/shard_map/all_to_all | solution.py:20
  131.3 1.0 fold.1
  132.3 3.4 %all-to-all-start.5 = ((bf16[8,32,512]{2,1,0:T(8,128)(2,1)}), bf16[8,32,512]{2,1,0:T(8,128)(2,1)S(1)}, u32[]{:S(2)}, u32[]{:S(2)}) async-start(bf16[8,32,512]{2,1,0:T(8,128)(2,1)} %fold.1), calls=%async_computation.5 | async-start | bytes 524288 | tf_op jit(solution)/shard_map/all_to_all | solution.py:20
  135.8 0.1 reduce_sum.18
  135.9 0.2 fusion.3
  136.1 0.6 reshape.37
  136.7 9.4 %all-to-all-done.5 = bf16[8,32,512]{2,1,0:T(8,128)(2,1)S(1)} async-done(((bf16[8,32,512]{2,1,0:T(8,128)(2,1)}), bf16[8,32,512]{2,1,0:T(8,128)(2,1)S(1)}, u32[]{:S(2)}, u32[]{:S(2)}) %all-to-all-start.5) | async-done | bytes 262176 | tf_op jit(solution)/shard_map/all_to_all | solution.py:20
  146.1 0.9 fusion.1
  (3 shorter events, 0.1 us)
Async XLA Ops:
  0.6 0.9 copy-start.4
  1.6 10.4 %copy-start.9 = (bf16[1920,512]{1,0:T(8,128)(2,1)S(1)}, bf16[1920,512]{1,0:T(8,128)(2,1)}, u32[]{:S(2)}) copy-start(bf16[1920,512]{1,0:T(8,128)(2,1)} %param.7) | copy-start | bytes 5898244
  2.6 18.8 %all-to-all-start = ((bf16[4,4,256,128]{3,2,1,0:T(8,128)(2,1)}), bf16[4,4,256,128]{3,2,1,0:T(8,128)(2,1)S(1)}, u32[]{:S(2)}, u32[]{:S(2)}) async-start(bf16[4,4,256,128]{3,2,1,0:T(8,128)(2,1)} %pack.1), calls=%async_computation | async-start | bytes 2097152 | tf_op jit(solution)/shard_map/all_to_all | solution.py:20
  13.6 2.0 %copy-start.5 = (f32[4,4,512]{2,1,0:T(4,128)S(1)}, f32[4,4,512]{2,1,0:T(4,128)}, u32[]{:S(2)}) copy-start(f32[4,4,512]{2,1,0:T(4,128)} %refs_4_.1) | copy-start | bytes 98308
  13.6 2.0 %copy-start.6 = (s32[4,128,8]{1,2,0:T(8,128)S(1)}, s32[4,128,8]{1,2,0:T(8,128)}, u32[]{:S(2)}) copy-start(s32[4,128,8]{1,2,0:T(8,128)} %param.8) | copy-start | bytes 49156
  13.6 2.0 %copy-start.7 = (s32[4,128,8]{1,2,0:T(8,128)S(1)}, s32[4,128,8]{1,2,0:T(8,128)}, u32[]{:S(2)}) copy-start(s32[4,128,8]{1,2,0:T(8,128)} %param.9) | copy-start | bytes 49156
  13.6 2.0 %copy-start.8 = (s32[4,128]{1,0:T(4,128)S(1)}, s32[4,128]{1,0:T(4,128)}, u32[]{:S(2)}) copy-start(s32[4,128]{1,0:T(4,128)} %refs_1_.1) | copy-start | bytes 6148
  19.3 0.8 copy-start
  20.1 0.8 copy-start.2
  21.4 4.5 %collective-permute-start = (bf16[4,4,256,128]{3,2,1,0:T(8,128)(2,1)S(1)}, bf16[4,4,256,128]{3,2,1,0:T(8,128)(2,1)S(1)}, u32[]{:S(2)}, u32[]{:S(2)}) collective-permute-start(bf16[4,4,256,128]{3,2,1,0:T(8,128)(2,1)S(1)} %all-to-all-done.ours_ref.refs_4_), channel_id=1, source_target_pairs={{0,1},{1,0},{2,3},{3,2},{4,5},{5,4},{6,7},{7,6},{8,9},{9,8},{10,11... | collective-permute-start | bytes 3145736 | tf_op jit(solution)/shard_map/ppermute | solution.py:303
  26.0 1.0 copy-start.3
  50.7 45.0 %copy-start.1 = (bf16[512,512]{1,0:T(8,128)(2,1)S(1)}, bf16[512,512]{1,0:T(8,128)(2,1)}, u32[]{:S(2)}) copy-start(bf16[512,512]{1,0:T(8,128)(2,1)} %copy-done) | copy-start | bytes 1572868
  132.3 13.8 %all-to-all-start.5 = ((bf16[8,32,512]{2,1,0:T(8,128)(2,1)}), bf16[8,32,512]{2,1,0:T(8,128)(2,1)S(1)}, u32[]{:S(2)}, u32[]{:S(2)}) async-start(bf16[8,32,512]{2,1,0:T(8,128)(2,1)} %fold.1), calls=%async_computation.5 | async-start | bytes 524288 | tf_op jit(solution)/shard_map/all_to_all | solution.py:20

commit v6 on v5

v6 whole, which is shorter than its diff:
```python
import jax
import jax.numpy as jnp
import numpy as np
from jax import lax
from jax.experimental import pallas as pl
from jax.experimental.pallas import tpu as pltpu
from jax.sharding import Mesh, PartitionSpec as P

SEQ = ("y", "z")
EVERY = ("y", "z", "x", "c")
F32 = jnp.float32
BF16 = jnp.bfloat16
MIDDLE = 28.28
VMEM = pl.BlockSpec(memory_space=pltpu.VMEM)
SMEM = pl.BlockSpec(memory_space=pltpu.SMEM)
HBM = pl.BlockSpec(memory_space=pltpu.HBM)
SMALL = pltpu.CompilerParams(vmem_limit_bytes=16 * 1024 * 1024)


def exchange(blocks, axes, groups=None):
    return lax.all_to_all(blocks, axes, split_axis=0, concat_axis=0, axis_index_groups=groups, tiled=True)


def mixed_groups(shape):
    ids = np.arange(int(np.prod(shape))).reshape(shape)
    ahead, after = [], []
    for x in range(shape[2]):
        for k in range(shape[0]):
            ahead += [ids[:, k, x, 0].tolist(), ids[k, :, x, 1].tolist()]
            after += [ids[k, :, x, 0].tolist(), ids[:, k, x, 1].tolist()]
    return ahead, after


def spread(counts, middle=MIDDLE):
    scaled = counts * (1.0 / middle)
    for _ in range(4):
        scaled = scaled * scaled
    return scaled


def unspread(coded, middle=MIDDLE):
    for _ in range(4):
        coded = jnp.sqrt(coded)
    return coded * middle


def squared(ratio):
    small = ratio < 2.0**63
    scaled = jnp.where(small, ratio, ratio * 2.0**-96)
    return jnp.where(small, scaled * scaled, -(scaled * scaled))


def rooted(coded):
    root = jnp.sqrt(jnp.abs(coded))
    return jnp.where(coded < 0, root * 2.0**96, root)


def split(values):
    high = values.astype(BF16).astype(F32)
    return high, values - high


def packed_sum(partial):
    tiny = partial < 2.0**-40
    scaled = jnp.where(tiny, partial * 2.0**80, partial)
    return jnp.where(tiny, -(scaled * scaled), scaled * scaled)


def unpacked_sum(coded):
    root = jnp.sqrt(jnp.abs(coded))
    return jnp.where(coded < 0, root * 2.0**-80, root)


def pack_kernel(block, padded, local_ref, packed_ref, raw_ref, rows_ref, arrived, left):
    copies, windows, depth, bins = packed_ref.shape
    reads = [pltpu.make_async_copy(local_ref.at[w], raw_ref.at[w], arrived.at[w]) for w in range(windows)]
    for read in reads:
        read.start()
    writes = []
    for w in range(windows):
        reads[w].wait()
        rows = raw_ref[w].astype(F32)
        gap = jnp.zeros((padded - block, bins), F32)
        pieces = []
        for i in range(depth // padded):
            pieces += [rows[i * block : (i + 1) * block], gap]
        rows_ref[w] = jnp.concatenate(pieces, axis=0).astype(BF16)
        for i in range(copies):
            write = pltpu.make_async_copy(rows_ref.at[w], packed_ref.at[i, w], left.at[w, i])
            write.start()
            writes.append(write)
    for write in writes:
        write.wait()


def ordering(at_ref, owner_ref, w, places, side, set_rows):
    windows, genes = owner_ref.shape
    square = (genes, genes)
    owner = owner_ref[w : w + 1, :]
    high = owner // side
    key = jnp.where(at_ref[1] == 0, (owner - high * side) * side + high, owner)
    other = jnp.broadcast_to(key.astype(F32), square)
    own = other.T
    earlier = lax.broadcasted_iota(jnp.int32, square, 1) < lax.broadcasted_iota(jnp.int32, square, 0)
    ahead = jnp.where((other == own) & earlier, 1.0, 0.0)
    rank = jnp.sum(ahead, axis=1, keepdims=True)
    at = jnp.sum(jnp.where(other < own, 1.0, ahead), axis=1, keepdims=True).astype(jnp.int32)
    turn = at // places
    place_of = at - turn * places
    high = place_of // side
    part = place_of - high * side
    row = w * (set_rows // windows) + high * (genes // places) + turn
    return own[:, :1].astype(jnp.int32), rank, at, part, row


def cover_kernel(places, side, at_ref, owner_ref, starts_ref, lengths_ref, cover_ref, turned_ref):
    windows, genes = owner_ref.shape
    exons = starts_ref.shape[1]
    rows, width = cover_ref.shape
    bins = width // windows
    set_rows = rows // side
    position = lax.broadcasted_iota(jnp.int32, (bins, genes), 0) + at_ref[0] * bins
    lane = lax.broadcasted_iota(jnp.int32, (genes, rows), 1)
    for w in range(windows):
        _, _, _, part, row = ordering(at_ref, owner_ref, w, places, side, set_rows)
        spot = jnp.where(part * set_rows + row == lane, 1.0, 0.0).astype(BF16)
        base = jnp.zeros((bins, genes), F32)
        for e in range(exons):
            past = position - starts_ref[w, e : e + 1, :]
            base += jnp.where((past >= 0) & (past < lengths_ref[w, e : e + 1, :]), 1.0, 0.0)
        turned = jnp.dot(base.astype(BF16), spot, preferred_element_type=F32)
        turned_ref[w * bins : (w + 1) * bins, :] = turned.astype(BF16)
        cover_ref[:, w * bins : (w + 1) * bins] = turned.T.astype(BF16)


def plan_kernel(places, at_ref, owner_ref, counts_ref, target_ref, keep_ref, pick_ref, mine_ref):
    windows, genes = owner_ref.shape
    capacity, tracks = counts_ref.shape[1:]
    side, sent_rows = target_ref.shape[:2]
    rows = mine_ref.shape[1]
    set_rows, sources = pick_ref.shape
    axis, column = at_ref[2], at_ref[5]
    lane = lax.broadcasted_iota(jnp.int32, (genes, rows), 1)
    targets = jnp.zeros((side * sent_rows, tracks), F32)
    keep = jnp.zeros(keep_ref.shape, F32)
    pick = jnp.zeros((set_rows, sources), F32)
    across = (((0,), (0,)), ((), ()))
    for w in range(windows):
        key, rank, at, part, row = ordering(at_ref, owner_ref, w, places, side, set_rows)
        spot = jnp.where(part * set_rows + row == lane, 1.0, 0.0)
        second = key // side
        first = key - second * side
        spare = w * capacity + (at // side) % capacity
        ours = part == axis
        here = jnp.where(ours & (row == lane[:, :set_rows]), 1.0, 0.0).astype(BF16)
        source = second * (sources // side) + spare
        origin = jnp.where(source == lane[:, :sources], 1.0, 0.0).astype(BF16)
        pick += lax.dot_general(here, origin, across, preferred_element_type=F32)
        room = lane[:, : keep_ref.shape[0]]
        here = jnp.where(ours & (second == column) & (spare == room), 1.0, 0.0).astype(BF16)
        origin = jnp.where(first * sent_rows + w == lane[:, : side * sent_rows], 1.0, 0.0).astype(BF16)
        keep += lax.dot_general(here, origin, across, preferred_element_type=F32)

        owned = (first == axis) & (second == column)
        coded = jnp.zeros((genes, tracks), F32)
        for k in range(capacity):
            slot = owned & (rank == k)
            filled = jnp.sum(jnp.where(slot, 1.0, 0.0), axis=0, keepdims=True) > 0
            count = counts_ref[w, k : k + 1, :]
            count = spread(jnp.where(jnp.broadcast_to(filled, count.shape), count, 1.0))
            coded += jnp.where(jnp.broadcast_to(slot, coded.shape), jnp.broadcast_to(count, coded.shape), 0.0)
            mark = jnp.where(jnp.broadcast_to(slot, lane.shape), spot, 0.0)
            mine_ref[w * capacity + k : w * capacity + k + 1, :] = jnp.sum(mark, axis=0, keepdims=True)
        goes = jnp.where(part * sent_rows + w == lane[:, : side * sent_rows], 1.0, 0.0).astype(BF16)
        targets += lax.dot_general(goes, coded.astype(BF16), across, preferred_element_type=F32)
    target_ref[...] = targets.reshape(side, sent_rows, tracks).astype(BF16)
    keep_ref[...] = keep.astype(BF16)
    pick_ref[...] = pick.astype(BF16)


def forward_kernel(
    at_ref, ours_ref, theirs_ref, head_ref, cover_ref, target_ref, sent_ref, slope_ref, pred_ref, other_ref, arrived
):
    xs, windows, _, bins = ours_ref.shape
    core = at_ref[1]
    side, sent_rows, tracks = sent_ref.shape
    set_rows = sent_rows - target_ref.shape[1]
    copy = pltpu.make_async_copy(theirs_ref, other_ref, arrived)
    copy.start()

    def product(ref, w, core):
        logits = jnp.zeros((bins, tracks), F32)
        for x in range(xs):
            logits += lax.dot_general(
                ref[x, w], head_ref[2 * x + core], (((0,), (0,)), ((), ())), preferred_element_type=F32
            )
        return logits

    for w in range(windows):
        slope_ref[w * bins : (w + 1) * bins, :] = product(ours_ref, w, core)
    copy.wait()
    for w in range(windows):
        logits = slope_ref[w * bins : (w + 1) * bins, :] + product(other_ref, w, 1 - core)
        low = jnp.exp(-jnp.abs(logits))
        pred_ref[w * bins : (w + 1) * bins, :] = (jnp.maximum(logits, 0.0) + jnp.log1p(low)).astype(BF16)
        slope_ref[w * bins : (w + 1) * bins, :] = jnp.where(logits >= 0, 1.0, low) / (1.0 + low)
    partial = jnp.dot(cover_ref[...], pred_ref[...], preferred_element_type=F32)
    sent_ref[:, :set_rows, :] = packed_sum(partial).reshape(side, set_rows, tracks).astype(BF16)
    sent_ref[:, set_rows:, :] = target_ref[...]


def second_kernel(windows, got_ref, keep_ref, sent_ref):
    side, got_rows, tracks = got_ref.shape
    set_rows = got_rows - 2 * windows
    total = unpacked_sum(got_ref[0, :set_rows, :].astype(F32))
    for i in range(1, side):
        total += unpacked_sum(got_ref[i, :set_rows, :].astype(F32))
    rows = got_ref[:, set_rows:, :].astype(F32).reshape(keep_ref.shape[1], tracks).astype(BF16)
    kept = jnp.dot(keep_ref[...], rows, preferred_element_type=F32)
    block = jnp.concatenate([packed_sum(total), kept], axis=0).astype(BF16)
    for i in range(side):
        sent_ref[i] = block


def third_kernel(windows, got_ref, pick_ref, sent_ref):
    side, got_rows, tracks = got_ref.shape
    set_rows, sources = pick_ref.shape
    gene_pred = unpacked_sum(got_ref[0, :set_rows, :].astype(F32))
    for i in range(1, side):
        gene_pred += unpacked_sum(got_ref[i, :set_rows, :].astype(F32))
    rows = got_ref[:, set_rows:, :].astype(F32).reshape(sources, tracks).astype(BF16)
    gene_target = unspread(jnp.dot(pick_ref[...], rows, preferred_element_type=F32))
    total, target_sum, fit = [
        jnp.sum(values.reshape(windows, set_rows // windows, tracks), axis=1)
        for values in (gene_pred, gene_target, gene_target * jnp.log(gene_pred))
    ]
    target_sum = spread(target_sum, MIDDLE * (set_rows // windows))
    pieces = [squared(gene_target / gene_pred), *split(total), target_sum, fit]
    block = jnp.concatenate(pieces, axis=0).astype(BF16)
    for i in range(side):
        sent_ref[i] = block


def backward_kernel(
    genes, at_ref, got_ref, turned_ref, slope_ref, ours_ref, other_ref, mine_ref, counts_ref, sent_ref, loss_ref, gene_ref
):
    side, got_rows, tracks = got_ref.shape
    xs, windows, depth, bins = ours_ref.shape
    set_rows = got_rows - 4 * windows
    window_rows = set_rows // windows
    padded = sent_ref.shape[1]
    sums = got_ref[:, set_rows:, :].astype(F32)
    high, low, target_sum, fit = [sums[:, i * windows : (i + 1) * windows, :] for i in range(4)]
    total = jnp.sum(high, axis=0) + jnp.sum(low, axis=0)
    target_sum = jnp.sum(unspread(target_sum, MIDDLE * window_rows), axis=0)
    fit = jnp.sum(fit, axis=0)
    log_total = jnp.log(total)
    loss_ref[...] = (-fit + target_sum * log_total + 0.2 * (total - target_sum * log_total)) / target_sum
    scale = genes / target_sum
    level = scale * (0.2 + 0.8 * target_sum / total)
    grads = []
    for w in range(windows):
        ratio = rooted(got_ref[:, w * window_rows : (w + 1) * window_rows, :].astype(F32))
        grads.append(level[w : w + 1][None] - scale[w : w + 1][None] * ratio)
    gene_grad = jnp.concatenate(grads, axis=1).reshape(side * set_rows, tracks).astype(BF16)
    bin_grad = jnp.dot(turned_ref[...], gene_grad, preferred_element_type=F32)
    logit_grad = (bin_grad * slope_ref[...]).astype(BF16)

    capacity = counts_ref.shape[1]
    ratios = got_ref[:, :set_rows, :].reshape(side * set_rows, tracks)
    back = jnp.dot(mine_ref[...].astype(BF16), ratios, preferred_element_type=F32)
    filled = jnp.sum(mine_ref[...], axis=1, keepdims=True) > 0
    back = rooted(jnp.where(jnp.broadcast_to(filled, back.shape), back, 1.0))
    back = jnp.where(jnp.broadcast_to(filled, back.shape), 1.0 / back, 0.0)
    for w in range(windows):
        here = back[w * capacity : (w + 1) * capacity]
        gene_ref[w] = jnp.where(here > 0, counts_ref[w] * here, 0.0)

    core = at_ref[1]
    for x in range(xs):
        for ref, upper in ((ours_ref, 2 * x + core), (other_ref, 2 * x + 1 - core)):
            lhs = jnp.concatenate([ref[x, w] for w in range(windows)], axis=1)
            grad = jnp.dot(lhs, logit_grad, preferred_element_type=F32)
            for i in range(side):
                place = upper * at_ref[3] + i * at_ref[4]
                sent_ref[place] = grad[i * padded : (i + 1) * padded].astype(BF16)


def fold_kernel(got_ref, sent_ref):
    for i in range(sent_ref.shape[0]):
        total = got_ref[0, i].astype(F32)
        for j in range(1, got_ref.shape[0]):
            total += got_ref[j, i].astype(F32)
        sent_ref[i] = (total * jnp.abs(total)).astype(BF16)


def per_device(embeddings, head, exon_starts, exon_lengths, gene_owner, gene_targets):
    places = lax.axis_size(SEQ)
    place = lax.axis_index(SEQ)
    core = lax.axis_index("c")
    side = lax.axis_size("y")
    windows, bin_dev, channels_dev = embeddings.shape
    channels, tracks = head.shape
    genes = gene_owner.shape[1]
    capacity = gene_targets.shape[1]
    held = genes // places
    per_place = windows * held
    rows = places * per_place
    xs, cores = lax.axis_size("x"), lax.axis_size("c")
    parts = xs * cores
    block = channels // places
    padded = -(-block // 16) * 16
    blocks_dev = channels_dev // block
    depth = blocks_dev * padded
    set_rows = rows // side
    side_rows = 2 * windows
    ahead, after = mixed_groups((side, places // side, xs, cores))

    packed = pl.pallas_call(
        lambda *refs: pack_kernel(block, padded, *refs),
        out_shape=jax.ShapeDtypeStruct((xs, windows, depth, bin_dev), BF16),
        in_specs=[HBM],
        out_specs=HBM,
        scratch_shapes=[
            pltpu.VMEM((windows, channels_dev, bin_dev), BF16),
            pltpu.VMEM((windows, depth, bin_dev), BF16),
            pltpu.SemaphoreType.DMA((windows,)),
            pltpu.SemaphoreType.DMA((windows, xs)),
        ],
        name="pack",
    )(embeddings.transpose(0, 2, 1))
    ours = exchange(packed, "x")

    padded_head = jnp.pad(head.reshape(places, block, tracks), ((0, 0), (0, padded - block), (0, 0)))
    padded_head = padded_head.reshape(parts, depth, tracks)

    first = core == 0
    y, z = lax.axis_index("y"), lax.axis_index("z")
    axis, column = jnp.where(first, y, z), jnp.where(first, z, y)
    at = jnp.stack([place, core, axis, jnp.where(first, side, 1), jnp.where(first, 1, side), column])
    at = at.astype(jnp.int32)

    plan = pl.pallas_call(
        lambda *refs: plan_kernel(places, *refs),
        out_shape=[
            jax.ShapeDtypeStruct((side, side_rows, tracks), BF16),
            jax.ShapeDtypeStruct((windows * capacity, side * side_rows), BF16),
            jax.ShapeDtypeStruct((set_rows, side * windows * capacity), BF16),
            jax.ShapeDtypeStruct((windows * capacity, rows), F32),
        ],
        in_specs=[SMEM, VMEM, VMEM],
        out_specs=[VMEM] * 4,
        compiler_params=SMALL,
        name="plan",
    )(at, gene_owner, gene_targets)
    ours, padded_head, plan, starts, lengths = lax.optimization_barrier(
        (ours, padded_head, tuple(plan), exon_starts.transpose(0, 2, 1), exon_lengths.transpose(0, 2, 1))
    )
    target_rows, keep, pick, mine = plan
    other = lax.ppermute(ours, "c", [(0, 1), (1, 0)])
    cover, turned = pl.pallas_call(
        lambda *refs: cover_kernel(places, side, *refs),
        out_shape=[
            jax.ShapeDtypeStruct((rows, windows * bin_dev), BF16),
            jax.ShapeDtypeStruct((windows * bin_dev, rows), BF16),
        ],
        in_specs=[SMEM] + [VMEM] * 3,
        out_specs=[VMEM] * 2,
        compiler_params=SMALL,
        name="cover",
    )(at, gene_owner, starts, lengths)

    sent, slope = pl.pallas_call(
        forward_kernel,
        out_shape=[
            jax.ShapeDtypeStruct((side, set_rows + side_rows, tracks), BF16),
            jax.ShapeDtypeStruct((windows * bin_dev, tracks), F32),
        ],
        in_specs=[SMEM, VMEM, HBM, VMEM, VMEM, VMEM],
        out_specs=[VMEM] * 2,
        scratch_shapes=[
            pltpu.VMEM((windows * bin_dev, tracks), BF16),
            pltpu.VMEM((xs, windows, depth, bin_dev), BF16),
            pltpu.SemaphoreType.DMA,
        ],
        compiler_params=SMALL,
        name="forward",
    )(at, ours, other, padded_head, cover, target_rows)

    sent = pl.pallas_call(
        lambda *refs: second_kernel(windows, *refs),
        out_shape=jax.ShapeDtypeStruct((side, set_rows + windows * capacity, tracks), BF16),
        in_specs=[VMEM, VMEM],
        out_specs=VMEM,
        compiler_params=SMALL,
        name="second",
    )(exchange(sent, EVERY, ahead), keep)
    sent = pl.pallas_call(
        lambda *refs: third_kernel(windows, *refs),
        out_shape=jax.ShapeDtypeStruct((side, set_rows + 4 * windows, tracks), BF16),
        in_specs=[VMEM, VMEM],
        out_specs=VMEM,
        compiler_params=SMALL,
        name="third",
    )(exchange(sent, EVERY, after), pick)
    got = exchange(sent, EVERY, ahead)

    sent, loss, gene_here = pl.pallas_call(
        lambda *refs: backward_kernel(genes, *refs),
        out_shape=[
            jax.ShapeDtypeStruct((places, padded, tracks), BF16),
            jax.ShapeDtypeStruct((windows, tracks), F32),
            jax.ShapeDtypeStruct(gene_targets.shape, F32),
        ],
        in_specs=[SMEM] + [VMEM] * 7,
        out_specs=[VMEM] * 3,
        compiler_params=SMALL,
        name="backward",
    )(at, got, turned, slope, ours, other, mine, gene_targets)

    summed = exchange(sent.reshape(side, side * padded, tracks), EVERY, ahead)
    summed = pl.pallas_call(
        fold_kernel,
        out_shape=jax.ShapeDtypeStruct((side, padded, tracks), BF16),
        in_specs=[VMEM],
        out_specs=VMEM,
        compiler_params=SMALL,
        name="fold",
    )(summed.reshape(side, side, padded, tracks))
    grads = exchange(summed, EVERY, after)[:, :block].astype(F32)
    root = jnp.sqrt(jnp.abs(grads))
    grad_head = jnp.sum(jnp.where(grads < 0, -root, root), axis=0)

    return (gene_here, loss, grad_head)


def solution(mesh):
    shape = (8, 8, 4, 2)
    fine = Mesh(mesh.devices.reshape(shape), EVERY)
    return jax.shard_map(
        per_device,
        mesh=fine,
        in_specs=(P(None, SEQ, ("x", "c")), P(None, ("x", "c")), P(), P(), P(), P(None, SEQ, ("x", "c"))),
        out_specs=(P(None, SEQ, ("x", "c")), P(None, ("x", "c")), P(SEQ, ("x", "c"))),
        check_vma=False,
    )
```

time: 147 us -> 143 us (0.973)
  blocking collectives: 97.3 us -> 108 us
  waiting for transfers between devices: 12.5 us -> 3.55 us
  local copies, waits for them, and re-layouts: 7.82 us -> 3.57 us
  starting transfers between devices: 14.7 us -> 11.3 us
  Pallas kernels: 12.7 us -> 14.9 us
    all_to_all x4 -> x5, blocking collectives: 97.3 us -> 108 us  [exchange(): lax.all_to_all(blocks, axes, split_axis=0, concat_axis=0, axis_index_grou...]
    all_to_all x2 -> x1, waiting for transfers between devices: 9.92 us -> 2.77 us  [exchange(): lax.all_to_all(blocks, axes, split_axis=0, concat_axis=0, axis_index_grou...]
    unnamed x20 -> x10, local copies, waits for them, and re-layouts: 3.6 us -> 0.02 us
    all_to_all x2 -> x1, starting transfers between devices: 12.8 us -> 9.37 us  [exchange(): lax.all_to_all(blocks, axes, split_axis=0, concat_axis=0, axis_index_grou...]
    ppermute x1, waiting for transfers between devices: 2.63 us -> 0.78 us  [per_device(): other = lax.ppermute(ours, 'c', [(0, 1), (1, 0)])]
    pallas_call x0 -> x1, Pallas kernels: none -> 1.82 us  [per_device(): pl.pallas_call(lambda *refs: cover_kernel(places, side, *refs), out_shape...]
  transfers between devices with their start and end apart: 3 -> 2, of which waited for: 3 -> 2; matrix products, arithmetic and copies ran while one was open for 3% -> 2% of each run, Pallas kernels for 3% -> 3%
where the time goes in v6:
time: 143 us
  blocking collectives  108 us (76%)
  Pallas kernels  14.9 us (10%)
  starting transfers between devices  11.3 us (8%)
  local copies, waits for them, and re-layouts  3.57 us (2%)
  waiting for transfers between devices  3.55 us (2%)
    all_to_all x5, blocking collectives, exchange(): lax.all_to_all(blocks, axes, split_axis=0, concat_axis=0, axis_index_grou...  108 us
    all_to_all x1, starting transfers between devices, exchange(): lax.all_to_all(blocks, axes, split_axis=0, concat_axis=0, axis_index_grou...  9.37 us
    pallas_call x1, Pallas kernels, per_device(): pl.pallas_call(lambda *refs: backward_kernel(genes, *refs), out_shape=[ja...  3.23 us
    pallas_call x1, Pallas kernels, per_device(): pl.pallas_call(lambda *refs: plan_kernel(places, *refs), out_shape=[jax.S...  3.08 us
  transfers between devices with their start and end apart: 2, of which 2 were waited for; matrix products, arithmetic and copies ran while one was open for 2% of the time, Pallas kernels for 3%

profile of v6, /device:TPU:2, one launch (start us, length us, event | category | flops | bytes accessed | tf_op | source)
XLA Modules:
  0.0 142.8 jit_solution(4381591357491907840)
XLA Ops:
  0.6 0.0 copy-start.4
  0.6 2.2 %pack.1 = bf16[4,4,256,128]{3,2,1,0:T(8,128)(2,1)} custom-call(bf16[4,240,128]{2,1,0:T(8,128)(2,1)} %bitcast.17), custom_call_target="tpu_custom_call" | custom-call | tf_op jit(solution)/shard_map/pack/pallas_call | solution.py:319
  2.8 9.4 %all-to-all-start = ((bf16[4,4,256,128]{3,2,1,0:T(8,128)(2,1)}), bf16[4,4,256,128]{3,2,1,0:T(8,128)(2,1)S(1)}, u32[]{:S(2)}, u32[]{:S(2)}) async-start(bf16[4,4,256,128]{3,2,1,0:T(8,128)(2,1)} %pack.1), calls=%async_computation | async-start | bytes 2097152 | tf_op jit(solution)/shard_map/all_to_all | solution.py:21
  12.2 0.0 copy-done.4
  12.2 1.6 %reshape.18 = bf16[64,30,512]{2,1,0:T(8,128)(2,1)} reshape(bf16[1920,512]{1,0:T(8,128)(2,1)S(1)} %copy-done.4) | data formatting | bytes 3932160 | tf_op jit(solution)/shard_map/reshape | solution.py:334
  13.8 0.0 copy-start
  13.8 0.0 copy-start.3
  13.8 0.0 copy-start.1
  13.8 0.0 copy-start.2
  13.8 1.9 %pad.4 = bf16[64,32,512]{2,1,0:T(8,128)(2,1)S(1)} pad(bf16[64,30,512]{2,1,0:T(8,128)(2,1)} %reshape.18, bf16[]{:T(256)} %constant.22.clone.1), padding=0_0x0_2x0_0 | pad | bytes 4063234 | tf_op jit(solution)/shard_map/jit(_pad)/pad | solution.py:334
  15.7 0.1 stack.27.refs_0_.at_ref
  15.8 0.0 copy-done
  15.8 0.0 copy-done.3
  15.8 3.1 %plan.1 = (bf16[8,8,512]{2,1,0:T(8,128)(2,1)S(1)}, bf16[16,64]{1,0:T(8,128)(2,1)S(1)}, bf16[64,128]{1,0:T(8,128)(2,1)S(1)}, f32[16,512]{1,0:T(8,128)S(1)}) custom-call(s32[6]{0:T(128)S(1)} %stack.27.refs_0_.at_ref, s32[4,128]{1,0:T(4,128)S(1)} %copy-done.3, f32[4,4,512]{2,1,0:T(4,128)S(1)} %copy-done), custom_call_target="tpu_custom_call" | custom-call | tf_op jit(solution)/shard_map/plan/pallas_call | solution.py:343
  18.8 2.8 %all-to-all-done.ours_ref.refs_4_ = bf16[4,4,256,128]{3,2,1,0:T(8,128)(2,1)S(1)} async-done(((bf16[4,4,256,128]{3,2,1,0:T(8,128)(2,1)}), bf16[4,4,256,128]{3,2,1,0:T(8,128)(2,1)S(1)}, u32[]{:S(2)}, u32[]{:S(2)}) %all-to-all-start) | async-done | bytes 1048608 | tf_op jit(solution)/shard_map/all_to_all | solution.py:21
  21.6 1.9 %collective-permute-start = (bf16[4,4,256,128]{3,2,1,0:T(8,128)(2,1)S(1)}, bf16[4,4,256,128]{3,2,1,0:T(8,128)(2,1)S(1)}, u32[]{:S(2)}, u32[]{:S(2)}) collective-permute-start(bf16[4,4,256,128]{3,2,1,0:T(8,128)(2,1)S(1)} %all-to-all-done.ours_ref.refs_4_), channel_id=1, source_target_pairs={{0,1},{1,0},{2,3},{3,2},{4,5},{5,4},{6,7},{7,6},{8,9},{9,8},{10,11... | collective-permute-start | bytes 3145736 | tf_op jit(solution)/shard_map/ppermute | solution.py:360
  23.5 0.0 copy-done.1
  23.5 0.0 copy-done.2
  23.6 1.8 %cover.1 = (bf16[512,512]{1,0:T(8,128)(2,1)S(1)}, bf16[512,512]{1,0:T(8,128)(2,1)S(1)}) custom-call(s32[6]{0:T(128)S(1)} %stack.27.refs_0_.at_ref, s32[4,128]{1,0:T(4,128)S(1)} %copy-done.3, s32[4,8,128]{2,1,0:T(8,128)S(1)} %bitcast.15, s32[4,8,128]{2,1,0:T(8,128)S(1)} %bitcast.16), custom_call_target="tpu_custom_call" | custom-call | tf_op jit(solution)/shard_map/cover/pallas_call | solution.py:361
  25.4 0.8 collective-permute-done.theirs_ref.refs_5_
  26.2 2.8 %forward.1 = (bf16[8,72,512]{2,1,0:T(8,128)(2,1)S(1)}, f32[512,512]{1,0:T(8,128)S(1)}) custom-call(s32[6]{0:T(128)S(1)} %stack.27.refs_0_.at_ref, bf16[4,4,256,128]{3,2,1,0:T(8,128)(2,1)S(1)} %all-to-all-done.ours_ref.refs_4_, bf16[4,4,256,128]{3,2,1,0:T(8,128)(2,1)S(1)} %collective-permute-done.theirs_ref.refs_5_, bf16[8,256,512]{2,1,0:T(8,128)(2,1)S(1)} %bitcast.12, ...), custom_call_target="tpu_custom_call" | custom-call | tf_op jit(solution)/shard_map/forward/pallas_call | solution.py:373
  29.0 20.6 %all_to_all.30.refs_0_ = bf16[8,72,512]{2,1,0:T(8,128)(2,1)S(1)} all-to-all(bf16[8,72,512]{2,1,0:T(8,128)(2,1)S(1)} %get-tuple-element.32), channel_id=1, replica_groups={{0,64,128,192,256,320,384,448},{1,9,17,25,33,41,49,57},{8,72,136,200,26..., dimensions={0} | all-to-all | bytes 1179648 | tf_op jit(solution)/shard_map/all_to_all | solution.py:21
  49.5 0.6 second.1
  50.2 24.8 %all_to_all.31.refs_0_ = bf16[8,80,512]{2,1,0:T(8,128)(2,1)S(1)} all-to-all(bf16[8,80,512]{2,1,0:T(8,128)(2,1)S(1)} %second.1), channel_id=1, replica_groups={{0,8,16,24,32,40,48,56},{1,65,129,193,257,321,385,449},{64,72,80,88,96,..., dimensions={0} | all-to-all | bytes 1310720 | tf_op jit(solution)/shard_map/all_to_all | solution.py:21
  75.0 0.9 third.1
  75.8 17.1 %all_to_all.32.refs_1_ = bf16[8,80,512]{2,1,0:T(8,128)(2,1)S(1)} all-to-all(bf16[8,80,512]{2,1,0:T(8,128)(2,1)S(1)} %third.1), channel_id=1, replica_groups={{0,64,128,192,256,320,384,448},{1,9,17,25,33,41,49,57},{8,72,136,200,26..., dimensions={0} | all-to-all | bytes 1310720 | tf_op jit(solution)/shard_map/all_to_all | solution.py:21
  92.9 3.2 %backward.1 = (bf16[64,32,512]{2,1,0:T(8,128)(2,1)S(1)}, f32[4,512]{1,0:T(4,128)}, f32[4,4,512]{2,1,0:T(4,128)}) custom-call(s32[6]{0:T(128)S(1)} %stack.27.refs_0_.at_ref, bf16[8,80,512]{2,1,0:T(8,128)(2,1)S(1)} %all_to_all.32.refs_1_, bf16[512,512]{1,0:T(8,128)(2,1)S(1)} %get-tuple-element.35.refs_2_, f32[512,512]{1,0:T(8,128)S(1)} %get-tuple-element.36.refs_3_, ...), custom_call_target="tpu_custom_call" | custom-call | tf_op jit(solution)/shard_map/backward/pallas_call | solution.py:408
  96.2 32.6 %all_to_all.33 = bf16[8,256,512]{2,1,0:T(8,128)(2,1)S(1)} all-to-all(bf16[8,256,512]{2,1,0:T(8,128)(2,1)S(1)} %bitcast.14), channel_id=1, replica_groups={{0,64,128,192,256,320,384,448},{1,9,17,25,33,41,49,57},{8,72,136,200,26..., dimensions={0} | all-to-all | bytes 4194304 | tf_op jit(solution)/shard_map/all_to_all | solution.py:21
  128.7 0.3 fold.1
  129.0 12.9 %all_to_all.34 = bf16[8,32,512]{2,1,0:T(8,128)(2,1)S(1)} all-to-all(bf16[8,32,512]{2,1,0:T(8,128)(2,1)S(1)} %fold.1), channel_id=1, replica_groups={{0,8,16,24,32,40,48,56},{1,65,129,193,257,321,385,449},{64,72,80,88,96,..., dimensions={0} | all-to-all | bytes 524288 | tf_op jit(solution)/shard_map/all_to_all | solution.py:21
  141.9 0.9 fusion.1
Async XLA Ops:
  0.6 11.6 %copy-start.4 = (bf16[1920,512]{1,0:T(8,128)(2,1)S(1)}, bf16[1920,512]{1,0:T(8,128)(2,1)}, u32[]{:S(2)}) copy-start(bf16[1920,512]{1,0:T(8,128)(2,1)} %param.7) | copy-start | bytes 5898244
  2.8 18.8 %all-to-all-start = ((bf16[4,4,256,128]{3,2,1,0:T(8,128)(2,1)}), bf16[4,4,256,128]{3,2,1,0:T(8,128)(2,1)S(1)}, u32[]{:S(2)}, u32[]{:S(2)}) async-start(bf16[4,4,256,128]{3,2,1,0:T(8,128)(2,1)} %pack.1), calls=%async_computation | async-start | bytes 2097152 | tf_op jit(solution)/shard_map/all_to_all | solution.py:21
  13.8 2.0 %copy-start = (f32[4,4,512]{2,1,0:T(4,128)S(1)}, f32[4,4,512]{2,1,0:T(4,128)}, u32[]{:S(2)}) copy-start(f32[4,4,512]{2,1,0:T(4,128)} %refs_7_.1) | copy-start | bytes 98308
  13.8 2.0 %copy-start.3 = (s32[4,128]{1,0:T(4,128)S(1)}, s32[4,128]{1,0:T(4,128)}, u32[]{:S(2)}) copy-start(s32[4,128]{1,0:T(4,128)} %refs_1_.3) | copy-start | bytes 6148
  13.8 9.7 %copy-start.1 = (s32[4,128,8]{1,2,0:T(8,128)S(1)}, s32[4,128,8]{1,2,0:T(8,128)}, u32[]{:S(2)}) copy-start(s32[4,128,8]{1,2,0:T(8,128)} %param.8) | copy-start | bytes 49156
  13.8 9.8 %copy-start.2 = (s32[4,128,8]{1,2,0:T(8,128)S(1)}, s32[4,128,8]{1,2,0:T(8,128)}, u32[]{:S(2)}) copy-start(s32[4,128,8]{1,2,0:T(8,128)} %param.9) | copy-start | bytes 49156
  21.6 4.5 %collective-permute-start = (bf16[4,4,256,128]{3,2,1,0:T(8,128)(2,1)S(1)}, bf16[4,4,256,128]{3,2,1,0:T(8,128)(2,1)S(1)}, u32[]{:S(2)}, u32[]{:S(2)}) collective-permute-start(bf16[4,4,256,128]{3,2,1,0:T(8,128)(2,1)S(1)} %all-to-all-done.ours_ref.refs_4_), channel_id=1, source_target_pairs={{0,1},{1,0},{2,3},{3,2},{4,5},{5,4},{6,7},{7,6},{8,9},{9,8},{10,11... | collective-permute-start | bytes 3145736 | tf_op jit(solution)/shard_map/ppermute | solution.py:360

commit v7 on v6

--- a/solution.py
+++ b/solution.py
@@ -113,17 +113,14 @@
     return own[:, :1].astype(jnp.int32), rank, at, part, row
 
 
-def cover_kernel(places, side, at_ref, owner_ref, starts_ref, lengths_ref, cover_ref, turned_ref):
-    windows, genes = owner_ref.shape
-    exons = starts_ref.shape[1]
+def cover_kernel(at_ref, spots_ref, starts_ref, lengths_ref, cover_ref, turned_ref):
+    windows, exons, genes = starts_ref.shape
     rows, width = cover_ref.shape
     bins = width // windows
-    set_rows = rows // side
     position = lax.broadcasted_iota(jnp.int32, (bins, genes), 0) + at_ref[0] * bins
     lane = lax.broadcasted_iota(jnp.int32, (genes, rows), 1)
     for w in range(windows):
-        _, _, _, part, row = ordering(at_ref, owner_ref, w, places, side, set_rows)
-        spot = jnp.where(part * set_rows + row == lane, 1.0, 0.0).astype(BF16)
+        spot = jnp.where(spots_ref[:, w : w + 1] == lane, 1.0, 0.0).astype(BF16)
         base = jnp.zeros((bins, genes), F32)
         for e in range(exons):
             past = position - starts_ref[w, e : e + 1, :]
@@ -133,7 +130,7 @@
         cover_ref[:, w * bins : (w + 1) * bins] = turned.T.astype(BF16)
 
 
-def plan_kernel(places, at_ref, owner_ref, counts_ref, target_ref, keep_ref, pick_ref, mine_ref):
+def plan_kernel(places, at_ref, owner_ref, counts_ref, target_ref, keep_ref, pick_ref, mine_ref, spots_ref):
     windows, genes = owner_ref.shape
     capacity, tracks = counts_ref.shape[1:]
     side, sent_rows = target_ref.shape[:2]
@@ -148,6 +145,7 @@
     for w in range(windows):
         key, rank, at, part, row = ordering(at_ref, owner_ref, w, places, side, set_rows)
         spot = jnp.where(part * set_rows + row == lane, 1.0, 0.0)
+        spots_ref[:, w : w + 1] = part * set_rows + row
         second = key // side
         first = key - second * side
         spare = w * capacity + (at // side) % capacity
@@ -178,32 +176,31 @@
     pick_ref[...] = pick.astype(BF16)
 
 
+def half_product(core, ref, head_ref):
+    xs, windows, _, bins = ref.shape
+    columns = [jnp.concatenate([ref[x, w] for w in range(windows)], axis=1) for x in range(xs)]
+    weights = [head_ref[2 * x + core] for x in range(xs)]
+    return lax.dot_general(
+        jnp.concatenate(columns, axis=0),
+        jnp.concatenate(weights, axis=0),
+        (((0,), (0,)), ((), ())),
+        preferred_element_type=F32,
+    )
+
+
+def half_kernel(at_ref, ours_ref, head_ref, logits_ref):
+    logits_ref[...] = half_product(at_ref[1], ours_ref, head_ref)
+
+
 def forward_kernel(
-    at_ref, ours_ref, theirs_ref, head_ref, cover_ref, target_ref, sent_ref, slope_ref, pred_ref, other_ref, arrived
+    at_ref, half_ref, other_ref, head_ref, cover_ref, target_ref, sent_ref, slope_ref, pred_ref
 ):
-    xs, windows, _, bins = ours_ref.shape
-    core = at_ref[1]
     side, sent_rows, tracks = sent_ref.shape
     set_rows = sent_rows - target_ref.shape[1]
-    copy = pltpu.make_async_copy(theirs_ref, other_ref, arrived)
-    copy.start()
-
-    def product(ref, w, core):
-        logits = jnp.zeros((bins, tracks), F32)
-        for x in range(xs):
-            logits += lax.dot_general(
-                ref[x, w], head_ref[2 * x + core], (((0,), (0,)), ((), ())), preferred_element_type=F32
-            )
-        return logits
-
-    for w in range(windows):
-        slope_ref[w * bins : (w + 1) * bins, :] = product(ours_ref, w, core)
-    copy.wait()
-    for w in range(windows):
-        logits = slope_ref[w * bins : (w + 1) * bins, :] + product(other_ref, w, 1 - core)
-        low = jnp.exp(-jnp.abs(logits))
-        pred_ref[w * bins : (w + 1) * bins, :] = (jnp.maximum(logits, 0.0) + jnp.log1p(low)).astype(BF16)
-        slope_ref[w * bins : (w + 1) * bins, :] = jnp.where(logits >= 0, 1.0, low) / (1.0 + low)
+    logits = half_ref[...] + half_product(1 - at_ref[1], other_ref, head_ref)
+    low = jnp.exp(-jnp.abs(logits))
+    pred_ref[...] = (jnp.maximum(logits, 0.0) + jnp.log1p(low)).astype(BF16)
+    slope_ref[...] = jnp.where(logits >= 0, 1.0, low) / (1.0 + low)
     partial = jnp.dot(cover_ref[...], pred_ref[...], preferred_element_type=F32)
     sent_ref[:, :set_rows, :] = packed_sum(partial).reshape(side, set_rows, tracks).astype(BF16)
     sent_ref[:, set_rows:, :] = target_ref[...]
@@ -277,13 +274,14 @@
         gene_ref[w] = jnp.where(here > 0, counts_ref[w] * here, 0.0)
 
     core = at_ref[1]
-    for x in range(xs):
-        for ref, upper in ((ours_ref, 2 * x + core), (other_ref, 2 * x + 1 - core)):
-            lhs = jnp.concatenate([ref[x, w] for w in range(windows)], axis=1)
-            grad = jnp.dot(lhs, logit_grad, preferred_element_type=F32)
+    for ref, low in ((ours_ref, core), (other_ref, 1 - core)):
+        lhs = [jnp.concatenate([ref[x, w] for w in range(windows)], axis=1) for x in range(xs)]
+        grad = jnp.dot(jnp.concatenate(lhs, axis=0), logit_grad, preferred_element_type=F32).astype(BF16)
+        for x in range(xs):
             for i in range(side):
-                place = upper * at_ref[3] + i * at_ref[4]
-                sent_ref[place] = grad[i * padded : (i + 1) * padded].astype(BF16)
+                place = (2 * x + low) * at_ref[3] + i * at_ref[4]
+                row = x * depth + i * padded
+                sent_ref[place] = grad[row : row + padded]
 
 
 def fold_kernel(got_ref, sent_ref):
@@ -292,6 +290,16 @@
         for j in range(1, got_ref.shape[0]):
             total += got_ref[j, i].astype(F32)
         sent_ref[i] = (total * jnp.abs(total)).astype(BF16)
+
+
+def finish_kernel(got_ref, grad_ref):
+    block = grad_ref.shape[0]
+    total = jnp.zeros(got_ref.shape[1:], F32)
+    for i in range(got_ref.shape[0]):
+        grad = got_ref[i].astype(F32)
+        root = jnp.sqrt(jnp.abs(grad))
+        total += jnp.where(grad < 0, -root, root)
+    grad_ref[...] = total[:block]
 
 
 def per_device(embeddings, head, exon_starts, exon_lengths, gene_owner, gene_targets):
@@ -347,19 +355,20 @@
             jax.ShapeDtypeStruct((windows * capacity, side * side_rows), BF16),
             jax.ShapeDtypeStruct((set_rows, side * windows * capacity), BF16),
             jax.ShapeDtypeStruct((windows * capacity, rows), F32),
+            jax.ShapeDtypeStruct((genes, 128), jnp.int32),
         ],
         in_specs=[SMEM, VMEM, VMEM],
-        out_specs=[VMEM] * 4,
+        out_specs=[VMEM] * 5,
         compiler_params=SMALL,
         name="plan",
     )(at, gene_owner, gene_targets)
     ours, padded_head, plan, starts, lengths = lax.optimization_barrier(
         (ours, padded_head, tuple(plan), exon_starts.transpose(0, 2, 1), exon_lengths.transpose(0, 2, 1))
     )
-    target_rows, keep, pick, mine = plan
+    target_rows, keep, pick, mine, spots = plan
     other = lax.ppermute(ours, "c", [(0, 1), (1, 0)])
     cover, turned = pl.pallas_call(
-        lambda *refs: cover_kernel(places, side, *refs),
+        cover_kernel,
         out_shape=[
             jax.ShapeDtypeStruct((rows, windows * bin_dev), BF16),
             jax.ShapeDtypeStruct((windows * bin_dev, rows), BF16),
@@ -368,7 +377,16 @@
         out_specs=[VMEM] * 2,
         compiler_params=SMALL,
         name="cover",
-    )(at, gene_owner, starts, lengths)
+    )(at, spots, starts, lengths)
+
+    half = pl.pallas_call(
+        half_kernel,
+        out_shape=jax.ShapeDtypeStruct((windows * bin_dev, tracks), F32),
+        in_specs=[SMEM, VMEM, VMEM],
+        out_specs=VMEM,
+        compiler_params=SMALL,
+        name="half",
+    )(at, ours, padded_head)
 
     sent, slope = pl.pallas_call(
         forward_kernel,
@@ -376,16 +394,12 @@
             jax.ShapeDtypeStruct((side, set_rows + side_rows, tracks), BF16),
             jax.ShapeDtypeStruct((windows * bin_dev, tracks), F32),
         ],
-        in_specs=[SMEM, VMEM, HBM, VMEM, VMEM, VMEM],
+        in_specs=[SMEM] + [VMEM] * 5,
         out_specs=[VMEM] * 2,
-        scratch_shapes=[
-            pltpu.VMEM((windows * bin_dev, tracks), BF16),
-            pltpu.VMEM((xs, windows, depth, bin_dev), BF16),
-            pltpu.SemaphoreType.DMA,
-        ],
+        scratch_shapes=[pltpu.VMEM((windows * bin_dev, tracks), BF16)],
         compiler_params=SMALL,
         name="forward",
-    )(at, ours, other, padded_head, cover, target_rows)
+    )(at, half, other, padded_head, cover, target_rows)
 
     sent = pl.pallas_call(
         lambda *refs: second_kernel(windows, *refs),
@@ -427,10 +441,14 @@
         compiler_params=SMALL,
         name="fold",
     )(summed.reshape(side, side, padded, tracks))
-    grads = exchange(summed, EVERY, after)[:, :block].astype(F32)
-    root = jnp.sqrt(jnp.abs(grads))
-    grad_head = jnp.sum(jnp.where(grads < 0, -root, root), axis=0)
-
+    grad_head = pl.pallas_call(
+        finish_kernel,
+        out_shape=jax.ShapeDtypeStruct((block, tracks), F32),
+        in_specs=[VMEM],
+        out_specs=VMEM,
+        compiler_params=SMALL,
+        name="finish",
+    )(exchange(summed, EVERY, after))
     return (gene_here, loss, grad_head)
 
 

time: 143 us -> 143 us (level)
    pallas_call x1 -> x3, Pallas kernels: 1.82 us -> 3.36 us  [the longest x1 1.28 us: per_device(): pl.pallas_call(half_kernel, out_shape=jax.ShapeDtypeStruct((windows * bin...]
  transfers between devices with their start and end apart: 2 -> 2, of which waited for: 2 -> 2; matrix products, arithmetic and copies ran while one was open for 2% -> 2% of each run, Pallas kernels for 3% -> 4%
where the time goes in v7:
time: 143 us; the launch traced here: 142 us
  blocking collectives  108 us (76%)
  Pallas kernels  15.9 us (11%)
  starting transfers between devices  11.4 us (8%)
  local copies, waits for them, and re-layouts  3.52 us (2%)
  waiting for transfers between devices  2.9 us (2%)
    all_to_all x5, blocking collectives, exchange(): lax.all_to_all(blocks, axes, split_axis=0, concat_axis=0, axis_index_grou...  108 us
    all_to_all x1, starting transfers between devices, exchange(): lax.all_to_all(blocks, axes, split_axis=0, concat_axis=0, axis_index_grou...  9.37 us
    pallas_call x1, Pallas kernels, per_device(): pl.pallas_call(lambda *refs: backward_kernel(genes, *refs), out_shape=[ja...  3.23 us
    pallas_call x1, Pallas kernels, per_device(): pl.pallas_call(lambda *refs: plan_kernel(places, *refs), out_shape=[jax.S...  3.1 us
  transfers between devices with their start and end apart: 2, of which 2 were waited for; matrix products, arithmetic and copies ran while one was open for 2% of the time, Pallas kernels for 4%

profile of v7, /device:TPU:2, one launch (start us, length us, event | category | flops | bytes accessed | tf_op | source)
XLA Modules:
  0.0 142.4 jit_solution(17243447475379219726)
XLA Ops:
  0.6 0.0 copy-start.4
  0.6 2.2 %pack.1 = bf16[4,4,256,128]{3,2,1,0:T(8,128)(2,1)} custom-call(bf16[4,240,128]{2,1,0:T(8,128)(2,1)} %bitcast.18), custom_call_target="tpu_custom_call" | custom-call | tf_op jit(solution)/shard_map/pack/pallas_call | solution.py:327
  2.8 9.4 %all-to-all-start = ((bf16[4,4,256,128]{3,2,1,0:T(8,128)(2,1)}), bf16[4,4,256,128]{3,2,1,0:T(8,128)(2,1)S(1)}, u32[]{:S(2)}, u32[]{:S(2)}) async-start(bf16[4,4,256,128]{3,2,1,0:T(8,128)(2,1)} %pack.1), calls=%async_computation | async-start | bytes 2097152 | tf_op jit(solution)/shard_map/all_to_all | solution.py:21
  12.2 0.0 copy-done.4
  12.2 1.6 %reshape.18 = bf16[64,30,512]{2,1,0:T(8,128)(2,1)} reshape(bf16[1920,512]{1,0:T(8,128)(2,1)S(1)} %copy-done.4) | data formatting | bytes 3932160 | tf_op jit(solution)/shard_map/reshape | solution.py:342
  13.8 0.0 copy-start
  13.8 0.0 copy-start.3
  13.8 1.8 %pad.4 = bf16[64,32,512]{2,1,0:T(8,128)(2,1)S(1)} pad(bf16[64,30,512]{2,1,0:T(8,128)(2,1)} %reshape.18, bf16[]{:T(256)} %constant.20.clone.1), padding=0_0x0_2x0_0 | pad | bytes 4063234 | tf_op jit(solution)/shard_map/jit(_pad)/pad | solution.py:342
  15.6 0.1 stack.27.refs_0_.at_ref
  15.7 0.0 copy-done
  15.7 0.0 copy-done.3
  15.7 3.1 %plan.1 = (bf16[8,8,512]{2,1,0:T(8,128)(2,1)S(1)}, bf16[16,64]{1,0:T(8,128)(2,1)S(1)}, bf16[64,128]{1,0:T(8,128)(2,1)S(1)}, f32[16,512]{1,0:T(8,128)S(1)}, s32[128,128]{1,0:T(8,128)S(1)}) custom-call(s32[6]{0:T(128)S(1)} %stack.27.refs_0_.at_ref, s32[4,128]{1,0:T(4,128)S(1)} %copy-done.3, f32[4,4,512]{2,1,0:T(4,128)S(1)} %copy-done), custom_call_target="tpu_custom_call" | custom-call | tf_op jit(solution)/shard_map/plan/pallas_call | solution.py:351
  18.8 2.8 %all-to-all-done.ours_ref.refs_4_ = bf16[4,4,256,128]{3,2,1,0:T(8,128)(2,1)S(1)} async-done(((bf16[4,4,256,128]{3,2,1,0:T(8,128)(2,1)}), bf16[4,4,256,128]{3,2,1,0:T(8,128)(2,1)S(1)}, u32[]{:S(2)}, u32[]{:S(2)}) %all-to-all-start) | async-done | bytes 1048608 | tf_op jit(solution)/shard_map/all_to_all | solution.py:21
  21.6 0.0 copy-start.1
  21.6 0.0 copy-start.2
  21.6 2.0 %collective-permute-start = (bf16[4,4,256,128]{3,2,1,0:T(8,128)(2,1)S(1)}, bf16[4,4,256,128]{3,2,1,0:T(8,128)(2,1)S(1)}, u32[]{:S(2)}, u32[]{:S(2)}) collective-permute-start(bf16[4,4,256,128]{3,2,1,0:T(8,128)(2,1)S(1)} %all-to-all-done.ours_ref.refs_4_), channel_id=1, source_target_pairs={{0,1},{1,0},{2,3},{3,2},{4,5},{5,4},{6,7},{7,6},{8,9},{9,8},{10,11... | collective-permute-start | bytes 3145736 | tf_op jit(solution)/shard_map/ppermute | solution.py:369
  23.7 1.3 half.1.half_ref
  25.0 0.0 copy-done.1
  25.0 0.0 copy-done.2
  25.0 1.2 cover.1
  26.2 0.1 collective-permute-done.other_ref.refs_5_
  26.3 2.3 %forward.1 = (bf16[8,72,512]{2,1,0:T(8,128)(2,1)S(1)}, f32[512,512]{1,0:T(8,128)S(1)}) custom-call(s32[6]{0:T(128)S(1)} %stack.27.refs_0_.at_ref, f32[512,512]{1,0:T(8,128)S(1)} %half.1.half_ref, bf16[4,4,256,128]{3,2,1,0:T(8,128)(2,1)S(1)} %collective-permute-done.other_ref.refs_5_, bf16[8,256,512]{2,1,0:T(8,128)(2,1)S(1)} %bitcast.13, ...), custom_call_target="tpu_custom_call" | custom-call | tf_op jit(solution)/shard_map/forward/pallas_call | solution.py:391
  28.6 20.6 %all_to_all.30.refs_0_ = bf16[8,72,512]{2,1,0:T(8,128)(2,1)S(1)} all-to-all(bf16[8,72,512]{2,1,0:T(8,128)(2,1)S(1)} %get-tuple-element.36), channel_id=1, replica_groups={{0,64,128,192,256,320,384,448},{1,9,17,25,33,41,49,57},{8,72,136,200,26..., dimensions={0} | all-to-all | bytes 1179648 | tf_op jit(solution)/shard_map/all_to_all | solution.py:21
  49.1 0.6 second.1
  49.8 24.8 %all_to_all.31.refs_0_ = bf16[8,80,512]{2,1,0:T(8,128)(2,1)S(1)} all-to-all(bf16[8,80,512]{2,1,0:T(8,128)(2,1)S(1)} %second.1), channel_id=1, replica_groups={{0,8,16,24,32,40,48,56},{1,65,129,193,257,321,385,449},{64,72,80,88,96,..., dimensions={0} | all-to-all | bytes 1310720 | tf_op jit(solution)/shard_map/all_to_all | solution.py:21
  74.6 0.9 third.1
  75.5 17.1 %all_to_all.32.refs_1_ = bf16[8,80,512]{2,1,0:T(8,128)(2,1)S(1)} all-to-all(bf16[8,80,512]{2,1,0:T(8,128)(2,1)S(1)} %third.1), channel_id=1, replica_groups={{0,64,128,192,256,320,384,448},{1,9,17,25,33,41,49,57},{8,72,136,200,26..., dimensions={0} | all-to-all | bytes 1310720 | tf_op jit(solution)/shard_map/all_to_all | solution.py:21
  92.5 3.2 %backward.1 = (bf16[64,32,512]{2,1,0:T(8,128)(2,1)S(1)}, f32[4,512]{1,0:T(4,128)}, f32[4,4,512]{2,1,0:T(4,128)}) custom-call(s32[6]{0:T(128)S(1)} %stack.27.refs_0_.at_ref, bf16[8,80,512]{2,1,0:T(8,128)(2,1)S(1)} %all_to_all.32.refs_1_, bf16[512,512]{1,0:T(8,128)(2,1)S(1)} %get-tuple-element.39.refs_2_, f32[512,512]{1,0:T(8,128)S(1)} %get-tuple-element.40.refs_3_, ...), custom_call_target="tpu_custom_call" | custom-call | tf_op jit(solution)/shard_map/backward/pallas_call | solution.py:422
  95.8 32.6 %all_to_all.33 = bf16[8,256,512]{2,1,0:T(8,128)(2,1)S(1)} all-to-all(bf16[8,256,512]{2,1,0:T(8,128)(2,1)S(1)} %bitcast.15), channel_id=1, replica_groups={{0,64,128,192,256,320,384,448},{1,9,17,25,33,41,49,57},{8,72,136,200,26..., dimensions={0} | all-to-all | bytes 4194304 | tf_op jit(solution)/shard_map/all_to_all | solution.py:21
  128.3 0.3 fold.1
  128.6 12.9 %all_to_all.34.got_ref = bf16[8,32,512]{2,1,0:T(8,128)(2,1)S(1)} all-to-all(bf16[8,32,512]{2,1,0:T(8,128)(2,1)S(1)} %fold.1), channel_id=1, replica_groups={{0,8,16,24,32,40,48,56},{1,65,129,193,257,321,385,449},{64,72,80,88,96,..., dimensions={0} | all-to-all | bytes 524288 | tf_op jit(solution)/shard_map/all_to_all | solution.py:21
  141.5 0.9 finish.1
Async XLA Ops:
  0.6 11.6 %copy-start.4 = (bf16[1920,512]{1,0:T(8,128)(2,1)S(1)}, bf16[1920,512]{1,0:T(8,128)(2,1)}, u32[]{:S(2)}) copy-start(bf16[1920,512]{1,0:T(8,128)(2,1)} %param.7) | copy-start | bytes 5898244
  2.8 18.8 %all-to-all-start = ((bf16[4,4,256,128]{3,2,1,0:T(8,128)(2,1)}), bf16[4,4,256,128]{3,2,1,0:T(8,128)(2,1)S(1)}, u32[]{:S(2)}, u32[]{:S(2)}) async-start(bf16[4,4,256,128]{3,2,1,0:T(8,128)(2,1)} %pack.1), calls=%async_computation | async-start | bytes 2097152 | tf_op jit(solution)/shard_map/all_to_all | solution.py:21
  13.8 1.9 %copy-start = (f32[4,4,512]{2,1,0:T(4,128)S(1)}, f32[4,4,512]{2,1,0:T(4,128)}, u32[]{:S(2)}) copy-start(f32[4,4,512]{2,1,0:T(4,128)} %refs_7_.1) | copy-start | bytes 98308
  13.8 1.9 %copy-start.3 = (s32[4,128]{1,0:T(4,128)S(1)}, s32[4,128]{1,0:T(4,128)}, u32[]{:S(2)}) copy-start(s32[4,128]{1,0:T(4,128)} %refs_1_.1) | copy-start | bytes 6148
  21.6 3.3 %copy-start.1 = (s32[4,128,8]{1,2,0:T(8,128)S(1)}, s32[4,128,8]{1,2,0:T(8,128)}, u32[]{:S(2)}) copy-start(s32[4,128,8]{1,2,0:T(8,128)} %param.8) | copy-start | bytes 49156
  21.6 3.4 %copy-start.2 = (s32[4,128,8]{1,2,0:T(8,128)S(1)}, s32[4,128,8]{1,2,0:T(8,128)}, u32[]{:S(2)}) copy-start(s32[4,128,8]{1,2,0:T(8,128)} %param.9) | copy-start | bytes 49156
  21.6 4.7 %collective-permute-start = (bf16[4,4,256,128]{3,2,1,0:T(8,128)(2,1)S(1)}, bf16[4,4,256,128]{3,2,1,0:T(8,128)(2,1)S(1)}, u32[]{:S(2)}, u32[]{:S(2)}) collective-permute-start(bf16[4,4,256,128]{3,2,1,0:T(8,128)(2,1)S(1)} %all-to-all-done.ours_ref.refs_4_), channel_id=1, source_target_pairs={{0,1},{1,0},{2,3},{3,2},{4,5},{5,4},{6,7},{7,6},{8,9},{9,8},{10,11... | collective-permute-start | bytes 3145736 | tf_op jit(solution)/shard_map/ppermute | solution.py:369

commit v8 on v7

--- a/solution.py
+++ b/solution.py
@@ -199,8 +199,11 @@
     set_rows = sent_rows - target_ref.shape[1]
     logits = half_ref[...] + half_product(1 - at_ref[1], other_ref, head_ref)
     low = jnp.exp(-jnp.abs(logits))
-    pred_ref[...] = (jnp.maximum(logits, 0.0) + jnp.log1p(low)).astype(BF16)
-    slope_ref[...] = jnp.where(logits >= 0, 1.0, low) / (1.0 + low)
+    above = 1.0 + low
+    series = low * (1.0 - low * (0.5 - low * (1.0 / 3.0)))
+    tail = jnp.where(low < 2.0**-7, series, jnp.log(above))
+    pred_ref[...] = (jnp.maximum(logits, 0.0) + tail).astype(BF16)
+    slope_ref[...] = jnp.where(logits >= 0, 1.0, low) / above
     partial = jnp.dot(cover_ref[...], pred_ref[...], preferred_element_type=F32)
     sent_ref[:, :set_rows, :] = packed_sum(partial).reshape(side, set_rows, tracks).astype(BF16)
     sent_ref[:, set_rows:, :] = target_ref[...]

time: 143 us -> 143 us (level)
  no operation moved by 1% of the time
where the time goes in v8:
time: 143 us; the launch traced here: 142 us
  blocking collectives  108 us (76%)
  Pallas kernels  15.9 us (11%)
  starting transfers between devices  11.4 us (8%)
  local copies, waits for them, and re-layouts  3.52 us (2%)
  waiting for transfers between devices  2.9 us (2%)
    all_to_all x5, blocking collectives, exchange(): lax.all_to_all(blocks, axes, split_axis=0, concat_axis=0, axis_index_grou...  108 us
    all_to_all x1, starting transfers between devices, exchange(): lax.all_to_all(blocks, axes, split_axis=0, concat_axis=0, axis_index_grou...  9.37 us
    pallas_call x1, Pallas kernels, per_device(): pl.pallas_call(lambda *refs: backward_kernel(genes, *refs), out_shape=[ja...  3.22 us
    pallas_call x1, Pallas kernels, per_device(): pl.pallas_call(lambda *refs: plan_kernel(places, *refs), out_shape=[jax.S...  3.1 us
  transfers between devices with their start and end apart: 2, of which 2 were waited for; matrix products, arithmetic and copies ran while one was open for 2% of the time, Pallas kernels for 4%

profile of v8, /device:TPU:2, one launch (start us, length us, event | category | flops | bytes accessed | tf_op | source)
XLA Modules:
  0.0 142.4 jit_solution(12195338000045594196)
XLA Ops:
  0.6 0.0 copy-start.4
  0.6 2.2 %pack.1 = bf16[4,4,256,128]{3,2,1,0:T(8,128)(2,1)} custom-call(bf16[4,240,128]{2,1,0:T(8,128)(2,1)} %bitcast.18), custom_call_target="tpu_custom_call" | custom-call | tf_op jit(solution)/shard_map/pack/pallas_call | solution.py:330
  2.8 9.4 %all-to-all-start = ((bf16[4,4,256,128]{3,2,1,0:T(8,128)(2,1)}), bf16[4,4,256,128]{3,2,1,0:T(8,128)(2,1)S(1)}, u32[]{:S(2)}, u32[]{:S(2)}) async-start(bf16[4,4,256,128]{3,2,1,0:T(8,128)(2,1)} %pack.1), calls=%async_computation | async-start | bytes 2097152 | tf_op jit(solution)/shard_map/all_to_all | solution.py:21
  12.2 0.0 copy-done.4
  12.2 1.6 %reshape.18 = bf16[64,30,512]{2,1,0:T(8,128)(2,1)} reshape(bf16[1920,512]{1,0:T(8,128)(2,1)S(1)} %copy-done.4) | data formatting | bytes 3932160 | tf_op jit(solution)/shard_map/reshape | solution.py:345
  13.8 0.0 copy-start
  13.8 0.0 copy-start.3
  13.8 1.8 %pad.4 = bf16[64,32,512]{2,1,0:T(8,128)(2,1)S(1)} pad(bf16[64,30,512]{2,1,0:T(8,128)(2,1)} %reshape.18, bf16[]{:T(256)} %constant.20.clone.1), padding=0_0x0_2x0_0 | pad | bytes 4063234 | tf_op jit(solution)/shard_map/jit(_pad)/pad | solution.py:345
  15.6 0.1 stack.27.refs_0_.at_ref
  15.7 0.0 copy-done
  15.7 0.0 copy-done.3
  15.7 3.1 %plan.1 = (bf16[8,8,512]{2,1,0:T(8,128)(2,1)S(1)}, bf16[16,64]{1,0:T(8,128)(2,1)S(1)}, bf16[64,128]{1,0:T(8,128)(2,1)S(1)}, f32[16,512]{1,0:T(8,128)S(1)}, s32[128,128]{1,0:T(8,128)S(1)}) custom-call(s32[6]{0:T(128)S(1)} %stack.27.refs_0_.at_ref, s32[4,128]{1,0:T(4,128)S(1)} %copy-done.3, f32[4,4,512]{2,1,0:T(4,128)S(1)} %copy-done), custom_call_target="tpu_custom_call" | custom-call | tf_op jit(solution)/shard_map/plan/pallas_call | solution.py:354
  18.8 2.8 %all-to-all-done.ours_ref.refs_4_ = bf16[4,4,256,128]{3,2,1,0:T(8,128)(2,1)S(1)} async-done(((bf16[4,4,256,128]{3,2,1,0:T(8,128)(2,1)}), bf16[4,4,256,128]{3,2,1,0:T(8,128)(2,1)S(1)}, u32[]{:S(2)}, u32[]{:S(2)}) %all-to-all-start) | async-done | bytes 1048608 | tf_op jit(solution)/shard_map/all_to_all | solution.py:21
  21.6 0.0 copy-start.1
  21.6 0.0 copy-start.2
  21.6 2.0 %collective-permute-start = (bf16[4,4,256,128]{3,2,1,0:T(8,128)(2,1)S(1)}, bf16[4,4,256,128]{3,2,1,0:T(8,128)(2,1)S(1)}, u32[]{:S(2)}, u32[]{:S(2)}) collective-permute-start(bf16[4,4,256,128]{3,2,1,0:T(8,128)(2,1)S(1)} %all-to-all-done.ours_ref.refs_4_), channel_id=1, source_target_pairs={{0,1},{1,0},{2,3},{3,2},{4,5},{5,4},{6,7},{7,6},{8,9},{9,8},{10,11... | collective-permute-start | bytes 3145736 | tf_op jit(solution)/shard_map/ppermute | solution.py:372
  23.7 1.3 half.1.half_ref
  25.0 0.0 copy-done.1
  25.0 0.0 copy-done.2
  25.0 1.2 cover.1
  26.2 0.1 collective-permute-done.other_ref.refs_5_
  26.3 2.3 %forward.1 = (bf16[8,72,512]{2,1,0:T(8,128)(2,1)S(1)}, f32[512,512]{1,0:T(8,128)S(1)}) custom-call(s32[6]{0:T(128)S(1)} %stack.27.refs_0_.at_ref, f32[512,512]{1,0:T(8,128)S(1)} %half.1.half_ref, bf16[4,4,256,128]{3,2,1,0:T(8,128)(2,1)S(1)} %collective-permute-done.other_ref.refs_5_, bf16[8,256,512]{2,1,0:T(8,128)(2,1)S(1)} %bitcast.13, ...), custom_call_target="tpu_custom_call" | custom-call | tf_op jit(solution)/shard_map/forward/pallas_call | solution.py:394
  28.6 20.6 %all_to_all.30.refs_0_ = bf16[8,72,512]{2,1,0:T(8,128)(2,1)S(1)} all-to-all(bf16[8,72,512]{2,1,0:T(8,128)(2,1)S(1)} %get-tuple-element.36), channel_id=1, replica_groups={{0,64,128,192,256,320,384,448},{1,9,17,25,33,41,49,57},{8,72,136,200,26..., dimensions={0} | all-to-all | bytes 1179648 | tf_op jit(solution)/shard_map/all_to_all | solution.py:21
  49.1 0.6 second.1
  49.8 24.8 %all_to_all.31.refs_0_ = bf16[8,80,512]{2,1,0:T(8,128)(2,1)S(1)} all-to-all(bf16[8,80,512]{2,1,0:T(8,128)(2,1)S(1)} %second.1), channel_id=1, replica_groups={{0,8,16,24,32,40,48,56},{1,65,129,193,257,321,385,449},{64,72,80,88,96,..., dimensions={0} | all-to-all | bytes 1310720 | tf_op jit(solution)/shard_map/all_to_all | solution.py:21
  74.6 0.9 third.1
  75.5 17.1 %all_to_all.32.refs_1_ = bf16[8,80,512]{2,1,0:T(8,128)(2,1)S(1)} all-to-all(bf16[8,80,512]{2,1,0:T(8,128)(2,1)S(1)} %third.1), channel_id=1, replica_groups={{0,64,128,192,256,320,384,448},{1,9,17,25,33,41,49,57},{8,72,136,200,26..., dimensions={0} | all-to-all | bytes 1310720 | tf_op jit(solution)/shard_map/all_to_all | solution.py:21
  92.6 3.2 %backward.1 = (bf16[64,32,512]{2,1,0:T(8,128)(2,1)S(1)}, f32[4,512]{1,0:T(4,128)}, f32[4,4,512]{2,1,0:T(4,128)}) custom-call(s32[6]{0:T(128)S(1)} %stack.27.refs_0_.at_ref, bf16[8,80,512]{2,1,0:T(8,128)(2,1)S(1)} %all_to_all.32.refs_1_, bf16[512,512]{1,0:T(8,128)(2,1)S(1)} %get-tuple-element.39.refs_2_, f32[512,512]{1,0:T(8,128)S(1)} %get-tuple-element.40.refs_3_, ...), custom_call_target="tpu_custom_call" | custom-call | tf_op jit(solution)/shard_map/backward/pallas_call | solution.py:425
  95.8 32.6 %all_to_all.33 = bf16[8,256,512]{2,1,0:T(8,128)(2,1)S(1)} all-to-all(bf16[8,256,512]{2,1,0:T(8,128)(2,1)S(1)} %bitcast.15), channel_id=1, replica_groups={{0,64,128,192,256,320,384,448},{1,9,17,25,33,41,49,57},{8,72,136,200,26..., dimensions={0} | all-to-all | bytes 4194304 | tf_op jit(solution)/shard_map/all_to_all | solution.py:21
  128.3 0.3 fold.1
  128.6 12.9 %all_to_all.34.got_ref = bf16[8,32,512]{2,1,0:T(8,128)(2,1)S(1)} all-to-all(bf16[8,32,512]{2,1,0:T(8,128)(2,1)S(1)} %fold.1), channel_id=1, replica_groups={{0,8,16,24,32,40,48,56},{1,65,129,193,257,321,385,449},{64,72,80,88,96,..., dimensions={0} | all-to-all | bytes 524288 | tf_op jit(solution)/shard_map/all_to_all | solution.py:21
  141.5 0.9 finish.1
Async XLA Ops:
  0.6 11.6 %copy-start.4 = (bf16[1920,512]{1,0:T(8,128)(2,1)S(1)}, bf16[1920,512]{1,0:T(8,128)(2,1)}, u32[]{:S(2)}) copy-start(bf16[1920,512]{1,0:T(8,128)(2,1)} %param.7) | copy-start | bytes 5898244
  2.8 18.8 %all-to-all-start = ((bf16[4,4,256,128]{3,2,1,0:T(8,128)(2,1)}), bf16[4,4,256,128]{3,2,1,0:T(8,128)(2,1)S(1)}, u32[]{:S(2)}, u32[]{:S(2)}) async-start(bf16[4,4,256,128]{3,2,1,0:T(8,128)(2,1)} %pack.1), calls=%async_computation | async-start | bytes 2097152 | tf_op jit(solution)/shard_map/all_to_all | solution.py:21
  13.8 1.9 %copy-start = (f32[4,4,512]{2,1,0:T(4,128)S(1)}, f32[4,4,512]{2,1,0:T(4,128)}, u32[]{:S(2)}) copy-start(f32[4,4,512]{2,1,0:T(4,128)} %refs_7_.1) | copy-start | bytes 98308
  13.8 1.9 %copy-start.3 = (s32[4,128]{1,0:T(4,128)S(1)}, s32[4,128]{1,0:T(4,128)}, u32[]{:S(2)}) copy-start(s32[4,128]{1,0:T(4,128)} %refs_1_.1) | copy-start | bytes 6148
  21.6 3.3 %copy-start.1 = (s32[4,128,8]{1,2,0:T(8,128)S(1)}, s32[4,128,8]{1,2,0:T(8,128)}, u32[]{:S(2)}) copy-start(s32[4,128,8]{1,2,0:T(8,128)} %param.8) | copy-start | bytes 49156
  21.6 3.4 %copy-start.2 = (s32[4,128,8]{1,2,0:T(8,128)S(1)}, s32[4,128,8]{1,2,0:T(8,128)}, u32[]{:S(2)}) copy-start(s32[4,128,8]{1,2,0:T(8,128)} %param.9) | copy-start | bytes 49156
  21.6 4.7 %collective-permute-start = (bf16[4,4,256,128]{3,2,1,0:T(8,128)(2,1)S(1)}, bf16[4,4,256,128]{3,2,1,0:T(8,128)(2,1)S(1)}, u32[]{:S(2)}, u32[]{:S(2)}) collective-permute-start(bf16[4,4,256,128]{3,2,1,0:T(8,128)(2,1)S(1)} %all-to-all-done.ours_ref.refs_4_), channel_id=1, source_target_pairs={{0,1},{1,0},{2,3},{3,2},{4,5},{5,4},{6,7},{7,6},{8,9},{9,8},{10,11... | collective-permute-start | bytes 3145736 | tf_op jit(solution)/shard_map/ppermute | solution.py:372

commit v9 on v8

--- a/solution.py
+++ b/solution.py
@@ -31,6 +31,10 @@
     return ahead, after
 
 
+def root_of(values):
+    return values * lax.rsqrt(jnp.maximum(values, 2.0**-126))
+
+
 def spread(counts, middle=MIDDLE):
     scaled = counts * (1.0 / middle)
     for _ in range(4):
@@ -51,7 +55,7 @@
 
 
 def rooted(coded):
-    root = jnp.sqrt(jnp.abs(coded))
+    root = root_of(jnp.abs(coded))
     return jnp.where(coded < 0, root * 2.0**96, root)
 
 
@@ -67,7 +71,7 @@
 
 
 def unpacked_sum(coded):
-    root = jnp.sqrt(jnp.abs(coded))
+    root = root_of(jnp.abs(coded))
     return jnp.where(coded < 0, root * 2.0**-80, root)
 
 
@@ -300,7 +304,7 @@
     total = jnp.zeros(got_ref.shape[1:], F32)
     for i in range(got_ref.shape[0]):
         grad = got_ref[i].astype(F32)
-        root = jnp.sqrt(jnp.abs(grad))
+        root = root_of(jnp.abs(grad))
         total += jnp.where(grad < 0, -root, root)
     grad_ref[...] = total[:block]
 

time: 143 us -> 142 us (level)
  no operation moved by 1% of the time
where the time goes in v9:
time: 142 us
  blocking collectives  108 us (76%)
  Pallas kernels  15.3 us (11%)
  starting transfers between devices  11.4 us (8%)
  local copies, waits for them, and re-layouts  3.52 us (2%)
  waiting for transfers between devices  2.9 us (2%)
    all_to_all x5, blocking collectives, exchange(): lax.all_to_all(blocks, axes, split_axis=0, concat_axis=0, axis_index_grou...  108 us
    all_to_all x1, starting transfers between devices, exchange(): lax.all_to_all(blocks, axes, split_axis=0, concat_axis=0, axis_index_grou...  9.37 us
    pallas_call x1, Pallas kernels, per_device(): pl.pallas_call(lambda *refs: backward_kernel(genes, *refs), out_shape=[ja...  3.11 us
    pallas_call x1, Pallas kernels, per_device(): pl.pallas_call(lambda *refs: plan_kernel(places, *refs), out_shape=[jax.S...  3.1 us
  transfers between devices with their start and end apart: 2, of which 2 were waited for; matrix products, arithmetic and copies ran while one was open for 2% of the time, Pallas kernels for 4%

profile of v9, /device:TPU:2, one launch (start us, length us, event | category | flops | bytes accessed | tf_op | source)
XLA Modules:
  0.0 141.8 jit_solution(15145567247121688064)
XLA Ops:
  0.6 0.0 copy-start.4
  0.6 2.2 %pack.1 = bf16[4,4,256,128]{3,2,1,0:T(8,128)(2,1)} custom-call(bf16[4,240,128]{2,1,0:T(8,128)(2,1)} %bitcast.18), custom_call_target="tpu_custom_call" | custom-call | tf_op jit(solution)/shard_map/pack/pallas_call | solution.py:334
  2.8 9.4 %all-to-all-start = ((bf16[4,4,256,128]{3,2,1,0:T(8,128)(2,1)}), bf16[4,4,256,128]{3,2,1,0:T(8,128)(2,1)S(1)}, u32[]{:S(2)}, u32[]{:S(2)}) async-start(bf16[4,4,256,128]{3,2,1,0:T(8,128)(2,1)} %pack.1), calls=%async_computation | async-start | bytes 2097152 | tf_op jit(solution)/shard_map/all_to_all | solution.py:21
  12.2 0.0 copy-done.4
  12.2 1.6 %reshape.18 = bf16[64,30,512]{2,1,0:T(8,128)(2,1)} reshape(bf16[1920,512]{1,0:T(8,128)(2,1)S(1)} %copy-done.4) | data formatting | bytes 3932160 | tf_op jit(solution)/shard_map/reshape | solution.py:349
  13.8 0.0 copy-start
  13.8 0.0 copy-start.3
  13.8 1.8 %pad.4 = bf16[64,32,512]{2,1,0:T(8,128)(2,1)S(1)} pad(bf16[64,30,512]{2,1,0:T(8,128)(2,1)} %reshape.18, bf16[]{:T(256)} %constant.20.clone.1), padding=0_0x0_2x0_0 | pad | bytes 4063234 | tf_op jit(solution)/shard_map/jit(_pad)/pad | solution.py:349
  15.6 0.1 stack.27.refs_0_.at_ref
  15.7 0.0 copy-done
  15.7 0.0 copy-done.3
  15.7 3.1 %plan.1 = (bf16[8,8,512]{2,1,0:T(8,128)(2,1)S(1)}, bf16[16,64]{1,0:T(8,128)(2,1)S(1)}, bf16[64,128]{1,0:T(8,128)(2,1)S(1)}, f32[16,512]{1,0:T(8,128)S(1)}, s32[128,128]{1,0:T(8,128)S(1)}) custom-call(s32[6]{0:T(128)S(1)} %stack.27.refs_0_.at_ref, s32[4,128]{1,0:T(4,128)S(1)} %copy-done.3, f32[4,4,512]{2,1,0:T(4,128)S(1)} %copy-done), custom_call_target="tpu_custom_call" | custom-call | tf_op jit(solution)/shard_map/plan/pallas_call | solution.py:358
  18.8 2.8 %all-to-all-done.ours_ref.refs_4_ = bf16[4,4,256,128]{3,2,1,0:T(8,128)(2,1)S(1)} async-done(((bf16[4,4,256,128]{3,2,1,0:T(8,128)(2,1)}), bf16[4,4,256,128]{3,2,1,0:T(8,128)(2,1)S(1)}, u32[]{:S(2)}, u32[]{:S(2)}) %all-to-all-start) | async-done | bytes 1048608 | tf_op jit(solution)/shard_map/all_to_all | solution.py:21
  21.6 0.0 copy-start.1
  21.6 0.0 copy-start.2
  21.6 2.0 %collective-permute-start = (bf16[4,4,256,128]{3,2,1,0:T(8,128)(2,1)S(1)}, bf16[4,4,256,128]{3,2,1,0:T(8,128)(2,1)S(1)}, u32[]{:S(2)}, u32[]{:S(2)}) collective-permute-start(bf16[4,4,256,128]{3,2,1,0:T(8,128)(2,1)S(1)} %all-to-all-done.ours_ref.refs_4_), channel_id=1, source_target_pairs={{0,1},{1,0},{2,3},{3,2},{4,5},{5,4},{6,7},{7,6},{8,9},{9,8},{10,11... | collective-permute-start | bytes 3145736 | tf_op jit(solution)/shard_map/ppermute | solution.py:376
  23.7 1.3 half.1.half_ref
  25.0 0.0 copy-done.1
  25.0 0.0 copy-done.2
  25.0 1.2 cover.1
  26.2 0.1 collective-permute-done.other_ref.refs_5_
  26.3 2.3 %forward.1 = (bf16[8,72,512]{2,1,0:T(8,128)(2,1)S(1)}, f32[512,512]{1,0:T(8,128)S(1)}) custom-call(s32[6]{0:T(128)S(1)} %stack.27.refs_0_.at_ref, f32[512,512]{1,0:T(8,128)S(1)} %half.1.half_ref, bf16[4,4,256,128]{3,2,1,0:T(8,128)(2,1)S(1)} %collective-permute-done.other_ref.refs_5_, bf16[8,256,512]{2,1,0:T(8,128)(2,1)S(1)} %bitcast.13, ...), custom_call_target="tpu_custom_call" | custom-call | tf_op jit(solution)/shard_map/forward/pallas_call | solution.py:398
  28.6 20.6 %all_to_all.30.refs_0_ = bf16[8,72,512]{2,1,0:T(8,128)(2,1)S(1)} all-to-all(bf16[8,72,512]{2,1,0:T(8,128)(2,1)S(1)} %get-tuple-element.36), channel_id=1, replica_groups={{0,64,128,192,256,320,384,448},{1,9,17,25,33,41,49,57},{8,72,136,200,26..., dimensions={0} | all-to-all | bytes 1179648 | tf_op jit(solution)/shard_map/all_to_all | solution.py:21
  49.1 0.4 second.1
  49.6 24.8 %all_to_all.31.refs_0_ = bf16[8,80,512]{2,1,0:T(8,128)(2,1)S(1)} all-to-all(bf16[8,80,512]{2,1,0:T(8,128)(2,1)S(1)} %second.1), channel_id=1, replica_groups={{0,8,16,24,32,40,48,56},{1,65,129,193,257,321,385,449},{64,72,80,88,96,..., dimensions={0} | all-to-all | bytes 1310720 | tf_op jit(solution)/shard_map/all_to_all | solution.py:21
  74.4 0.6 third.1
  75.1 17.1 %all_to_all.32.refs_1_ = bf16[8,80,512]{2,1,0:T(8,128)(2,1)S(1)} all-to-all(bf16[8,80,512]{2,1,0:T(8,128)(2,1)S(1)} %third.1), channel_id=1, replica_groups={{0,64,128,192,256,320,384,448},{1,9,17,25,33,41,49,57},{8,72,136,200,26..., dimensions={0} | all-to-all | bytes 1310720 | tf_op jit(solution)/shard_map/all_to_all | solution.py:21
  92.1 3.1 %backward.1 = (bf16[64,32,512]{2,1,0:T(8,128)(2,1)S(1)}, f32[4,512]{1,0:T(4,128)}, f32[4,4,512]{2,1,0:T(4,128)}) custom-call(s32[6]{0:T(128)S(1)} %stack.27.refs_0_.at_ref, bf16[8,80,512]{2,1,0:T(8,128)(2,1)S(1)} %all_to_all.32.refs_1_, bf16[512,512]{1,0:T(8,128)(2,1)S(1)} %get-tuple-element.39.refs_2_, f32[512,512]{1,0:T(8,128)S(1)} %get-tuple-element.40.refs_3_, ...), custom_call_target="tpu_custom_call" | custom-call | tf_op jit(solution)/shard_map/backward/pallas_call | solution.py:429
  95.2 32.6 %all_to_all.33 = bf16[8,256,512]{2,1,0:T(8,128)(2,1)S(1)} all-to-all(bf16[8,256,512]{2,1,0:T(8,128)(2,1)S(1)} %bitcast.15), channel_id=1, replica_groups={{0,64,128,192,256,320,384,448},{1,9,17,25,33,41,49,57},{8,72,136,200,26..., dimensions={0} | all-to-all | bytes 4194304 | tf_op jit(solution)/shard_map/all_to_all | solution.py:21
  127.8 0.3 fold.1
  128.1 12.9 %all_to_all.34.got_ref = bf16[8,32,512]{2,1,0:T(8,128)(2,1)S(1)} all-to-all(bf16[8,32,512]{2,1,0:T(8,128)(2,1)S(1)} %fold.1), channel_id=1, replica_groups={{0,8,16,24,32,40,48,56},{1,65,129,193,257,321,385,449},{64,72,80,88,96,..., dimensions={0} | all-to-all | bytes 524288 | tf_op jit(solution)/shard_map/all_to_all | solution.py:21
  141.0 0.8 finish.1
Async XLA Ops:
  0.6 11.6 %copy-start.4 = (bf16[1920,512]{1,0:T(8,128)(2,1)S(1)}, bf16[1920,512]{1,0:T(8,128)(2,1)}, u32[]{:S(2)}) copy-start(bf16[1920,512]{1,0:T(8,128)(2,1)} %param.7) | copy-start | bytes 5898244
  2.8 18.8 %all-to-all-start = ((bf16[4,4,256,128]{3,2,1,0:T(8,128)(2,1)}), bf16[4,4,256,128]{3,2,1,0:T(8,128)(2,1)S(1)}, u32[]{:S(2)}, u32[]{:S(2)}) async-start(bf16[4,4,256,128]{3,2,1,0:T(8,128)(2,1)} %pack.1), calls=%async_computation | async-start | bytes 2097152 | tf_op jit(solution)/shard_map/all_to_all | solution.py:21
  13.8 1.9 %copy-start = (f32[4,4,512]{2,1,0:T(4,128)S(1)}, f32[4,4,512]{2,1,0:T(4,128)}, u32[]{:S(2)}) copy-start(f32[4,4,512]{2,1,0:T(4,128)} %refs_7_.1) | copy-start | bytes 98308
  13.8 1.9 %copy-start.3 = (s32[4,128]{1,0:T(4,128)S(1)}, s32[4,128]{1,0:T(4,128)}, u32[]{:S(2)}) copy-start(s32[4,128]{1,0:T(4,128)} %refs_1_.1) | copy-start | bytes 6148
  21.6 3.3 %copy-start.1 = (s32[4,128,8]{1,2,0:T(8,128)S(1)}, s32[4,128,8]{1,2,0:T(8,128)}, u32[]{:S(2)}) copy-start(s32[4,128,8]{1,2,0:T(8,128)} %param.8) | copy-start | bytes 49156
  21.6 3.4 %copy-start.2 = (s32[4,128,8]{1,2,0:T(8,128)S(1)}, s32[4,128,8]{1,2,0:T(8,128)}, u32[]{:S(2)}) copy-start(s32[4,128,8]{1,2,0:T(8,128)} %param.9) | copy-start | bytes 49156
  21.6 4.7 %collective-permute-start = (bf16[4,4,256,128]{3,2,1,0:T(8,128)(2,1)S(1)}, bf16[4,4,256,128]{3,2,1,0:T(8,128)(2,1)S(1)}, u32[]{:S(2)}, u32[]{:S(2)}) collective-permute-start(bf16[4,4,256,128]{3,2,1,0:T(8,128)(2,1)S(1)} %all-to-all-done.ours_ref.refs_4_), channel_id=1, source_target_pairs={{0,1},{1,0},{2,3},{3,2},{4,5},{5,4},{6,7},{7,6},{8,9},{9,8},{10,11... | collective-permute-start | bytes 3145736 | tf_op jit(solution)/shard_map/ppermute | solution.py:376
